TPU v7x, 32 devices: a whole 2x2x4 slice. The times are simulated.
32 devices in a mesh: grp: 2 (over y), edge: 4 (over z), tx: 2 (over x), rcv: 2 (over core).
Axes of the slice: x: 2, y: 2, z: 4, core: 2. Of those that a mesh axis runs over, the one named last changes fastest.
Arguments:
- fields: bfloat16 [8, 128, 65536], P(('grp', 'tx', 'rcv'), 'edge'), parts along dimension 0, may hold values from -6 to 6
- kblocks: bfloat16 [1024, 12288], P('edge'), may hold values from -0.4375 to 0.4375
- blk_index: int32 [1024, 3], P('edge'), may hold values from 0 to 1023, as said below
- sigma: float32 [131072], P(('grp', 'edge')), parts along dimension 0, may hold values from 0.1 to 3
- rec_edge: int32 [8192, 8], P(('grp', 'edge')), parts along dimension 0, may hold values from 0 to 16383
- rec_weight: float32 [8192, 8], P(('grp', 'edge')), parts along dimension 0, may hold values from -1 to 1
- rec_owner: int32 [8192, 1], P(('grp', 'edge')), parts along dimension 0, may hold values from 0 to 3; in each aligned block of 1024 rows (0 to 1023, 1024 to 2047, ...) at most 256 rows name the same one
- rec_slot: int32 [8192], P(('grp', 'edge')), parts along dimension 0, may hold values from 0 to 1023
Outputs:
- residual: bfloat16 [8, 128, 65536], P(('grp', 'tx', 'rcv'), None, 'edge'), parts along dimension 0
- site_data: float32 [8, 128, 4096], P(('grp', 'tx', 'rcv'), None, 'edge'), parts along dimension 0
There are 2 independent parts, one for each index of `grp`. A program takes and returns all parts, laid end to end along the dimension named above; an argument that names none is the same for every part. Nothing has to cross between parts.
Inputs may be any that keep to these rules, and one draw needn't show every extreme that they name: `blk_index`: entry 0 of row b is b itself; entry 1 is b minus a distance of 1 to 2 and entry 2 is b plus a distance of 1 to 2, each reflected at the ends (a negative index -j becomes j, an index 1023 + j becomes 1024 - 1 - j); the first block row of every edge range takes distance 2 in entry 1 and its last block row takes distance 2 in entry 2. `rec_edge`: receiver r interpolates edges of edge range r // 1024. `rec_owner`: among the 1024 receivers of one edge range at most 256 name the same owner, a bound that some block reaches.
All inputs are finite; a program needn't handle non-finite values.
Results may differ from a plain program's by a relative error of at most 0.001.
Values may be sent and summed in bfloat16 or wider, within the bound.
No kernel may reach another device: no remote copies, remote signals or barrier semaphores. Data moves between devices by JAX's collectives and lax.ppermute only.
A program may use at most 320 MiB of HBM per device.

v0:
```python
import functools

import jax
import jax.numpy as jnp
from jax import lax
from jax.experimental import pallas as pl
from jax.experimental.pallas import tpu as pltpu
from jax.sharding import PartitionSpec as P


BS = 64
NNZB = 3
HB = 2
IW = 8
SDEV = 1024

LANE = 128
PAIRS = 8
RIM = BS * HB


def padded_2(shard, sides, width):
    for axis, dim in sides:
        peers, length = (lax.axis_size(axis), shard.shape[dim])
        up = [(i, (i + 1) % peers) for i in range(peers - 1)]
        down = [(j, i) for i, j in up]
        last = lax.slice_in_dim(shard, length - width, length, axis=dim)
        initial = lax.slice_in_dim(shard, 0, width, axis=dim)
        before = lax.ppermute(last, axis, up)
        after = lax.ppermute(initial, axis, down)
        shard = jnp.concatenate([before, shard, after], axis=dim)
    return shard


def plain_device(fields, kblocks, blk_index, sigma, rec_edge, rec_weight, rec_owner, rec_slot):
    peers = lax.axis_size("edge")
    edge_count = sigma.shape[0]
    block_count = edge_count // BS
    rec_count = rec_edge.shape[0]
    rim_width = BS * HB
    tx_local = fields.shape[1] // 2
    first_block = lax.axis_index("edge") * block_count
    local_index = blk_index - first_block + HB
    flat_edges = rec_edge.reshape(-1)
    block_vals = kblocks.reshape(block_count, NNZB, BS, BS)
    source = fields.reshape(1, tx_local, 2, fields.shape[2])
    moved = lax.all_to_all(source, "edge", split_axis=3, concat_axis=0, tiled=True)
    item_count = moved.shape[1]
    columns = peers * item_count * 2
    flat_rows = moved.reshape(columns, edge_count)
    padded = padded_2(flat_rows, (("edge", 1),), rim_width)
    blocks = padded.reshape(columns, block_count + 2 * HB, BS)
    picked = jnp.take(blocks, local_index, axis=1)
    stiffness = jnp.einsum("cbkj,bkij->cbi", picked, block_vals, preferred_element_type=jnp.float32)
    stiffness = stiffness.reshape(columns, edge_count)
    paired = flat_rows.reshape(columns // 2, 2, edge_count).astype(jnp.float32)
    diagonal = jnp.stack([-sigma * paired[:, 1], sigma * paired[:, 0]], axis=1).reshape(
        columns, edge_count
    )
    residual = (stiffness + diagonal).astype(jnp.bfloat16).reshape(1, columns, edge_count)
    interp_vals = (
        jnp.take(flat_rows, flat_edges, axis=1).reshape(columns, rec_count, IW).astype(jnp.float32)
    )
    predicted = jnp.sum(interp_vals * rec_weight[None], axis=2)
    site_ids = rec_owner[:, 0] * SDEV + rec_slot
    local_sums = jax.ops.segment_sum(predicted.T, site_ids, num_segments=peers * SDEV)
    site_table = lax.psum_scatter(local_sums.T, "edge", scatter_dimension=1, tiled=True)
    return (residual, site_table.reshape(1, columns, SDEV))


def shifted(x, shift, peers):
    return lax.ppermute(x, "edge", [(i, (i + shift) % peers) for i in range(peers)])


HBM = pl.BlockSpec(memory_space=pltpu.HBM)
VMEM = pl.BlockSpec(memory_space=pltpu.VMEM)
SMEM = pl.BlockSpec(memory_space=pltpu.SMEM)


def list_kernel(edge_ref, weight_ref, owner_ref, slot_ref, list_ref):
    list_ref[:IW, :] = edge_ref[...].astype(jnp.float32)
    list_ref[IW : 2 * IW, :] = weight_ref[...]
    sites = owner_ref[...] * SDEV + slot_ref[...]
    list_ref[2 * IW :, :] = sites.astype(jnp.float32)


def listed(rec_edge, rec_weight, rec_owner, rec_slot):
    recs = rec_slot.shape[0]
    return pl.pallas_call(
        list_kernel,
        in_specs=[VMEM] * 4,
        out_specs=VMEM,
        out_shape=jax.ShapeDtypeStruct((2 * IW + 1, recs), jnp.float32),
        compiler_params=pltpu.CompilerParams(vmem_limit_bytes=1 << 20),
        name="listed",
    )(rec_edge.T, rec_weight.T, rec_owner.T, rec_slot.reshape(1, recs))


def cut_kernel(peers, me_ref, rows_ref, *refs):
    pieces, held, in_sems, out_sems = refs[: peers - 1], *refs[peers - 1 :]
    me = me_ref[0]
    length = held.shape[2]
    all_edges = rows_ref.shape[1]
    taken, put = [], []
    for s in range(1, peers):
        start = start_of(lax.rem(me + s, peers), peers, all_edges)
        taken.append(
            pltpu.make_async_copy(
                rows_ref.at[:, pl.ds(pl.multiple_of(start, RIM), length)],
                held.at[s - 1],
                in_sems.at[s - 1],
            )
        )
        put.append(pltpu.make_async_copy(held.at[s - 1], pieces[s - 1], out_sems.at[s - 1]))
    for copy in taken:
        copy.start()
    for copy, onward in zip(taken, put):
        copy.wait()
        onward.start()
    for copy in put:
        copy.wait()


def start_of(target, peers, all_edges):
    edge_count = all_edges // peers
    return jnp.clip(target * edge_count - RIM, 0, all_edges - edge_count - 2 * RIM)


def cut(me, rows, peers):
    cols, all_edges = rows.shape
    length = all_edges // peers + 2 * RIM
    piece = jax.ShapeDtypeStruct((cols, length), rows.dtype)
    return pl.pallas_call(
        functools.partial(cut_kernel, peers),
        in_specs=[SMEM, HBM],
        out_specs=[HBM] * (peers - 1),
        out_shape=[piece] * (peers - 1),
        scratch_shapes=[
            pltpu.VMEM((peers - 1, cols, length), rows.dtype),
            pltpu.SemaphoreType.DMA((peers - 1,)),
            pltpu.SemaphoreType.DMA((peers - 1,)),
        ],
        compiler_params=pltpu.CompilerParams(vmem_limit_bytes=8 << 20),
        cost_estimate=pl.CostEstimate(flops=0, bytes_accessed=8 << 20, transcendentals=0),
        name="cut",
    )(me, rows)


def site_kernel(peers, me_ref, rows_ref, *refs):
    list_refs = refs[:peers]
    out_ref, rows, turned, picked, pred, ints, row_sems, int_sems = refs[peers : peers + 8]
    edge_refs = refs[peers + 8 : 2 * peers + 8]
    tables = refs[2 * peers + 8 :]
    cols = rows_ref.shape[0]
    edge_count = turned.shape[0]
    recs = list_refs[0].shape[1]
    per = picked.shape[1]
    parts = row_sems.shape[0]
    width = edge_count // parts

    def fetch(part, s):
        start = lax.rem(me_ref[0] + peers - s, peers) * edge_count + part * width
        return pltpu.make_async_copy(
            rows_ref.at[:, pl.ds(pl.multiple_of(start, LANE), width)],
            rows.at[pl.ds(s * cols, cols), pl.ds(part * width, width)],
            row_sems.at[part, s],
        )

    for part in range(parts):
        for s in range(peers):
            fetch(part, s).start()
    lists = []
    for s in range(peers):
        ints[s, :IW, :] = list_refs[s][:IW, :].astype(jnp.int32)
        ints[s, IW : IW + 1, :] = list_refs[s][2 * IW :, :].astype(jnp.int32)
        lists.append(pltpu.make_async_copy(ints.at[s], edge_refs[s], int_sems.at[s]))
        lists[s].start()
    for table in tables:
        table[...] = jnp.zeros_like(table)

    for part in range(parts):
        for s in range(peers):
            fetch(part, s).wait()

        def turn(t, _, part=part):
            at = pl.multiple_of(part * width + t * LANE, LANE)
            turned[pl.ds(at, LANE), :] = rows[:, pl.ds(at, LANE)].astype(jnp.float32).T
            return 0

        lax.fori_loop(0, width // LANE, turn, 0, unroll=2)
    lane = lax.broadcasted_iota(jnp.int32, (1, LANE), 1) // cols
    lanes = lax.broadcasted_iota(jnp.int32, (per, LANE), 1) // cols
    for copy in lists:
        copy.wait()

    def receivers(g, _):
        first = pl.multiple_of(g * per, per)

        def gather(r, _):
            for k in range(IW):
                row = turned[pl.ds(edge_refs[0][k, first + r], 1), :]
                for q in range(1, peers):
                    other = turned[pl.ds(edge_refs[q][k, first + r], 1), :]
                    row = jnp.where(lane == q, other, row)
                picked[k, pl.ds(r, 1), :] = row
            return 0

        lax.fori_loop(0, per, gather, 0, unroll=2)
        weights = [ref[IW : 2 * IW, pl.ds(first, per)] for ref in list_refs]
        weights.append(jnp.zeros((LANE - peers * IW, per), jnp.float32))
        weights = jnp.concatenate(weights, axis=0).T
        total = jnp.zeros((per, LANE), jnp.float32)
        for k in range(IW):
            total += picked[k] * jnp.take_along_axis(weights, lanes * IW + k, axis=1)
        pred[...] = total

        def scatter(r, _):
            row = pred[pl.ds(r, 1), :]
            for q in range(peers):
                at = pl.ds(edge_refs[q][IW, first + r], 1)
                tables[q][at, :] = tables[q][at, :] + row
            return 0

        lax.fori_loop(0, per, scatter, 0, unroll=2)
        return 0

    lax.fori_loop(0, recs // per, receivers, 0)
    owned = out_ref.shape[2]
    per_owner = owned // LANE

    def back(t, _):
        at = pl.ds(pl.multiple_of(t * LANE, LANE), LANE)
        tile = tables[0][at, :]
        for q in range(1, peers):
            tile = jnp.where(lane == q, tables[q][at, :], tile)
        tile = tile.T
        total = tile[:cols]
        for q in range(1, peers):
            total += tile[q * cols : (q + 1) * cols]
        out_ref[t // per_owner, :, pl.ds(pl.multiple_of((t % per_owner) * LANE, LANE), LANE)] = total
        return 0

    lax.fori_loop(0, peers * per_owner, back, 0)


def site_sums(me, rows, lists, peers):
    cols, all_edges = rows.shape
    edge_count = all_edges // peers
    per = LANE
    parts = 4
    recs = lists[0].shape[1]
    return pl.pallas_call(
        functools.partial(site_kernel, peers),
        in_specs=[SMEM, HBM] + [VMEM] * peers,
        out_specs=VMEM,
        out_shape=jax.ShapeDtypeStruct((peers, cols, SDEV), jnp.float32),
        scratch_shapes=[
            pltpu.VMEM((peers * cols, edge_count), rows.dtype),
            pltpu.VMEM((edge_count, LANE), jnp.float32),
            pltpu.VMEM((IW, per, LANE), jnp.float32),
            pltpu.VMEM((per, LANE), jnp.float32),
            pltpu.VMEM((peers, IW + 1, recs), jnp.int32),
            pltpu.SemaphoreType.DMA((parts, peers)),
            pltpu.SemaphoreType.DMA((peers,)),
        ]
        + [pltpu.SMEM((IW + 1, recs), jnp.int32)] * peers
        + [pltpu.VMEM((peers * SDEV, LANE), jnp.float32)] * peers,
        compiler_params=pltpu.CompilerParams(vmem_limit_bytes=24 << 20),
        cost_estimate=pl.CostEstimate(
            flops=2 * recs * peers * IW * 8 * LANE, bytes_accessed=64 << 20, transcendentals=0
        ),
        name="site_sums",
    )(me, rows, *lists)


def place_kernel(peers, me_ref, _, *refs):
    out_ref = refs[peers]
    cols = refs[0].shape[0]
    for s in range(peers):
        at = lax.rem(me_ref[0] + peers - s, peers) * cols
        out_ref[pl.ds(pl.multiple_of(at, 8), cols), :] = refs[s][...]


def placed_rows(me, after, got, peers):
    cols, width = got[0].shape
    return pl.pallas_call(
        functools.partial(place_kernel, peers),
        in_specs=[SMEM] + [VMEM] * (peers + 1),
        out_specs=VMEM,
        out_shape=jax.ShapeDtypeStruct((peers * cols, width), got[0].dtype),
        compiler_params=pltpu.CompilerParams(vmem_limit_bytes=4 << 20),
        name="placed_rows",
    )(me, after, *got)


def band_kernel(first_ref, index_ref, blocks_ref, band_ref, lines):
    count = NNZB * BS // 2
    half = lax.broadcasted_iota(jnp.int32, (1, 2 * BS), 1) // BS

    def pair(p, _):
        base = 2 * p - HB + first_ref[0]
        for side in range(2):
            both = blocks_ref[2 * p + side].astype(jnp.float32)
            crossed = pltpu.roll(both, BS, 1)
            lines[side, pl.ds(0, count, stride=2), :] = jnp.where(half == 0, both, crossed)
            lines[side, pl.ds(1, count, stride=2), :] = jnp.where(half == 0, crossed, both)
        for side in range(2):
            offs = [index_ref[k, 2 * p + side] - base for k in range(NNZB)]
            for tile in range(band_ref.shape[2] // (2 * BS)):
                here = half + 2 * tile
                total = jnp.where(here == offs[0], lines[side, :BS], 0.0)
                for k in range(1, NNZB):
                    total += jnp.where(here == offs[k], lines[side, k * BS : (k + 1) * BS], 0.0)
                band_ref[p, side * BS : (side + 1) * BS, tile * 2 * BS : (tile + 1) * 2 * BS] = (
                    total.astype(band_ref.dtype)
                )
        return 0

    lax.fori_loop(0, band_ref.shape[0], pair, 0)


def banded(kblocks, blk_index, first_block):
    count = kblocks.shape[0]
    pairs = count // 2
    lines = NNZB * BS // 2
    window = 2 + 2 * HB
    return pl.pallas_call(
        band_kernel,
        in_specs=[SMEM, SMEM, VMEM],
        out_specs=VMEM,
        scratch_shapes=[pltpu.VMEM((2, 2 * lines, 2 * BS), jnp.float32)],
        out_shape=jax.ShapeDtypeStruct((pairs, 2 * BS, window * BS), jnp.bfloat16),
        compiler_params=pltpu.CompilerParams(vmem_limit_bytes=24 << 20),
        cost_estimate=pl.CostEstimate(flops=0, bytes_accessed=40 << 20, transcendentals=0),
        name="banded",
    )(first_block, blk_index.T, kblocks.reshape(count, lines, 2 * BS))


def residual_kernel(peers, me_ref, *refs):
    pieces = refs[: peers - 1]
    rows_ref, band_ref, sigma_ref, out_ref, panel, swap, own, own_sem = refs[peers - 1 :]
    pieces = (own,) + pieces
    cols, length = own.shape
    columns = panel.shape[0]
    step = pl.program_id(0)
    width = PAIRS * 2 * BS
    reach = width + 2 * RIM
    me = me_ref[0]

    @pl.when(step == 0)
    def _():
        at = pl.multiple_of(start_of(me, peers, rows_ref.shape[1]), RIM)
        copy = pltpu.make_async_copy(rows_ref.at[:, pl.ds(at, length)], own, own_sem)
        copy.start()
        panel[...] = jnp.zeros_like(panel)
        row = lax.broadcasted_iota(jnp.int32, (columns, columns), 0)
        col = lax.broadcasted_iota(jnp.int32, (columns, columns), 1)
        sign = jnp.where(row % 2 == 0, -1.0, 1.0)
        swap[...] = jnp.where(row + 1 - 2 * (row % 2) == col, sign, 0.0).astype(swap.dtype)
        copy.wait()

    first = jnp.where(me == 0, 0, jnp.where(me == peers - 1, -2 * RIM, -RIM))
    want = step * width - RIM - first
    start = jnp.clip(want, 0, length - reach)
    src = pl.ds(pl.multiple_of(start, RIM), reach)
    dst = pl.ds(pl.multiple_of(RIM + start - want, RIM), reach)
    for s in range(peers):
        at = pl.ds(pl.multiple_of(lax.rem(me + peers - s, peers) * cols, cols), cols)
        panel[at, dst] = pieces[s][:, src]
    swapped = jnp.dot(
        swap[...], panel[:, 2 * RIM : 2 * RIM + width], preferred_element_type=jnp.float32
    )
    turned = swapped * sigma_ref[:, pl.ds(pl.multiple_of(step * width, width), width)]
    for t in range(PAIRS):
        at = t * 2 * BS
        stiff = lax.dot_general(
            panel[:, RIM + at : RIM + at + 2 * (BS + RIM)],
            band_ref[step * PAIRS + t],
            (((1,), (1,)), ((), ())),
            preferred_element_type=jnp.float32,
        )
        out_ref[:, at : at + 2 * BS] = (stiff + turned[:, at : at + 2 * BS]).astype(out_ref.dtype)


def residual_of(rows, pieces, band, sigma, me, peers):
    cols = pieces[0].shape[0]
    edge_count = sigma.shape[0]
    columns = peers * cols
    width = PAIRS * 2 * BS
    return pl.pallas_call(
        functools.partial(residual_kernel, peers),
        grid_spec=pltpu.PrefetchScalarGridSpec(
            num_scalar_prefetch=1,
            grid=(edge_count // width,),
            in_specs=[VMEM] * (peers - 1) + [HBM, VMEM, VMEM],
            out_specs=pl.BlockSpec((columns, width), lambda i, me: (0, i)),
            scratch_shapes=[
                pltpu.VMEM((columns, width + 4 * RIM), jnp.bfloat16),
                pltpu.VMEM((columns, columns), jnp.bfloat16),
                pltpu.VMEM(pieces[0].shape, rows.dtype),
                pltpu.SemaphoreType.DMA,
            ],
        ),
        out_shape=jax.ShapeDtypeStruct((columns, edge_count), jnp.bfloat16),
        compiler_params=pltpu.CompilerParams(vmem_limit_bytes=24 << 20),
        cost_estimate=pl.CostEstimate(
            flops=2 * columns * edge_count * 384, bytes_accessed=21 << 20, transcendentals=0
        ),
        name="residual",
    )(me, *pieces, rows, band, sigma.reshape(1, edge_count))


def on_device(fields, kblocks, blk_index, sigma, rec_edge, rec_weight, rec_owner, rec_slot):
    return ordered(
        fields, kblocks, blk_index, sigma, rec_edge, rec_weight, rec_owner, rec_slot
    )


def ordered(fields, kblocks, blk_index, sigma, rec_edge, rec_weight, rec_owner, rec_slot):
    peers = lax.axis_size("edge")
    position = lax.axis_index("edge")
    me = position.reshape(1)
    rows = fields[0]
    edge_count = sigma.shape[0]
    shifts = range(1, peers)

    mine = listed(rec_edge, rec_weight, rec_owner, rec_slot)
    lists = [mine] + [shifted(mine, s, peers) for s in shifts]
    rows = pltpu.with_memory_space_constraint(rows, pltpu.HBM)
    parts = cut(me, rows, peers)
    pieces = [shifted(parts[s - 1], s, peers) for s in shifts]
    band = banded(kblocks, blk_index, me * (edge_count // BS))
    own = site_sums(me, rows, lists, peers)

    def owned(target):
        return lax.dynamic_index_in_dim(own, target, axis=0, keepdims=False)

    got = [owned(position)] + [shifted(owned((position + s) % peers), s, peers) for s in shifts]
    residual = residual_of(rows, pieces, band, sigma, me, peers)
    site_out = placed_rows(me, residual[:16, :LANE], got, peers)
    return residual[None], site_out[None]


def fits(mesh, fields, sigma, rec_edge):
    peers = mesh.shape["edge"]
    cols = fields.shape[1] // peers
    edge_count = sigma.shape[0] // (mesh.shape["grp"] * peers)
    recs = rec_edge.shape[0] // (mesh.shape["grp"] * peers)
    return (
        cols % 16 == 0
        and cols * peers == LANE
        and peers * IW <= LANE
        and edge_count % (PAIRS * 2 * BS) == 0
        and recs % LANE == 0
        and peers > 1
    )


def solution(mesh):
    placed = (
        P(("grp", "tx", "rcv"), "edge", None),
        P("edge", None),
        P("edge", None),
        P(("grp", "edge")),
        P(("grp", "edge"), None),
        P(("grp", "edge"), None),
        P(("grp", "edge"), None),
        P(("grp", "edge")),
    )

    def run(fields, kblocks, blk_index, sigma, rec_edge, rec_weight, rec_owner, rec_slot):
        body = on_device if fits(mesh, fields, sigma, rec_edge) else plain_device
        return jax.shard_map(
            body,
            mesh=mesh,
            in_specs=placed,
            out_specs=(P(("grp", "tx", "rcv"), None, "edge"), P(("grp", "tx", "rcv"), None, "edge")),
            check_vma=False,
        )(fields, kblocks, blk_index, sigma, rec_edge, rec_weight, rec_owner, rec_slot)

    return run
```

profile of v0, /device:TPU:0, one launch (start us, length us, event | category | flops | bytes accessed | tf_op | source)
XLA Modules:
  0.0 200.0 jit_solution(11131217339991004354)
XLA Ops:
  0.6 0.0 copy-start.2
  0.6 0.0 copy-start.3
  0.7 0.0 copy-start.5
  0.7 0.0 copy-start.6
  0.7 3.1 %cut.1 = (bf16[32,16640]{1,0:T(8,128)(2,1)}, bf16[32,16640]{1,0:T(8,128)(2,1)}, bf16[32,16640]{1,0:T(8,128)(2,1)}) custom-call(s32[1]{0:T(128)} %bitcast.me_ref, bf16[32,65536]{1,0:T(8,128)(2,1)} %bitcast.27), custom_call_target="tpu_custom_call" | custom-call | bytes 8388608 | tf_op jit(solution)/shard_map/cut/pallas_call | solution.py:133
  3.7 3.1 %collective-permute-start = (bf16[32,16640]{1,0:T(8,128)(2,1)}, bf16[32,16640]{1,0:T(8,128)(2,1)S(1)}, u32[]{:S(2)}, u32[]{:S(2)}) collective-permute-start(bf16[32,16640]{1,0:T(8,128)(2,1)} %get-tuple-element.5), channel_id=1, source_target_pairs={{0,4},{4,8},{8,12},{12,0},{1,5},{5,9},{9,13},{13,1},{2,6},{6,10},{... | collective-permute-start | bytes 3194888 | tf_op jit(solution)/shard_map/ppermute | solution.py:72
  6.8 2.6 %collective-permute-start.1 = (bf16[32,16640]{1,0:T(8,128)(2,1)}, bf16[32,16640]{1,0:T(8,128)(2,1)S(1)}, u32[]{:S(2)}, u32[]{:S(2)}) collective-permute-start(bf16[32,16640]{1,0:T(8,128)(2,1)} %get-tuple-element.6), channel_id=1, source_target_pairs={{0,8},{4,12},{8,0},{12,4},{1,9},{5,13},{9,1},{13,5},{2,10},{6,14},... | collective-permute-start | bytes 3194888 | tf_op jit(solution)/shard_map/ppermute | solution.py:72
  9.4 1.3 collective-permute-start.2
  10.8 0.7 collective-permute-start.3
  11.5 0.3 collective-permute-start.4
  11.9 69.5 %collective-permute-done.3.refs_1_ = f32[17,1024]{1,0:T(8,128)S(1)} collective-permute-done((f32[17,1024]{1,0:T(8,128)S(1)}, f32[17,1024]{1,0:T(8,128)S(1)}, u32[]{:S(2)}, u32[]{:S(2)}) %collective-permute-start.3) | collective-permute-done | bytes 69664 | tf_op jit(solution)/shard_map/ppermute | solution.py:72
  81.4 0.0 collective-permute-start.5
  81.4 6.9 %copy.10 = bf16[32,8,96,128]{3,2,1,0:T(8,128)(2,1)} copy(bf16[32,8,96,128]{3,1,2,0:T(8,128)(2,1)} %bitcast.30) | data formatting | bytes 12582912
  88.3 2.8 %copy-done = bf16[32,8,96,128]{3,2,1,0:T(8,128)(2,1)S(1)} copy-done((bf16[32,8,96,128]{3,2,1,0:T(8,128)(2,1)S(1)}, bf16[32,8,96,128]{3,2,1,0:T(8,128)(2,1)}, u32[]{:S(2)}) %copy-start) | copy-done | bytes 6291480
  91.1 17.4 %banded.1.refs_4_ = bf16[128,128,384]{2,1,0:T(8,128)(2,1)S(1)} custom-call(s32[1]{0:T(128)S(6)} %mul.3.first_ref, s32[3,256]{1,0:T(4,128)S(1)} %bitcast.24, bf16[256,96,128]{2,1,0:T(8,128)(2,1)S(1)} %bitcast.20), custom_call_target="tpu_custom_call" | custom-call | bytes 41943040 | tf_op jit(solution)/shard_map/banded/pallas_call | solution.py:327
  108.5 0.0 collective-permute-done.4.refs_2_
  108.6 1.4 collective-permute-done.5.refs_3_
  109.9 47.2 %site_sums.1 = f32[4,32,1024]{2,1,0:T(8,128)S(1)} custom-call(s32[1]{0:T(128)} %bitcast.me_ref, bf16[32,65536]{1,0:T(8,128)(2,1)} %bitcast.28, f32[17,1024]{1,0:T(8,128)S(1)} %listed.1.refs_0_, f32[17,1024]{1,0:T(8,128)S(1)} %collective-permute-done.3.refs_1_, f32[17,1024]{1,0:T(8,128)S(1)} %collective-permute-done.4.refs_2_, ...), custom_call_target="tpu_custom_call" | custom-call | flops 67108864 | bytes 67108864 | tf_op jit(solution)/shard_map/site_sums/pallas_call | solution.py:252
  157.1 0.0 copy-start.1
  157.1 0.1 dynamic-slice_bitcast_fusion
  157.2 24.5 %collective-permute-start.6 = (f32[32,1024]{1,0:T(8,128)S(1)}, f32[32,1024]{1,0:T(8,128)S(1)}, u32[]{:S(2)}, u32[]{:S(2)}) collective-permute-start(f32[32,1024]{1,0:T(8,128)S(1)} %get-tuple-element.10), channel_id=1, source_target_pairs={{0,4},{4,8},{8,12},{12,0},{1,5},{5,9},{9,13},{13,1},{2,6},{6,10},{... | collective-permute-start | bytes 393224 | tf_op jit(solution)/shard_map/ppermute | solution.py:72
  181.7 3.9 %collective-permute-start.7 = (f32[32,1024]{1,0:T(8,128)S(1)}, f32[32,1024]{1,0:T(8,128)S(1)}, u32[]{:S(2)}, u32[]{:S(2)}) collective-permute-start(f32[32,1024]{1,0:T(8,128)S(1)} %get-tuple-element.9), channel_id=1, source_target_pairs={{0,8},{4,12},{8,0},{12,4},{1,9},{5,13},{9,1},{13,5},{2,10},{6,14},... | collective-permute-start | bytes 393224 | tf_op jit(solution)/shard_map/ppermute | solution.py:72
  185.7 0.0 collective-permute-done.refs_0_
  185.7 0.9 collective-permute-start.8
  186.6 0.0 collective-permute-done.1.refs_1_
  186.6 0.0 collective-permute-done.2.refs_2_
  186.6 11.9 %residual.1 = bf16[128,16384]{1,0:T(8,128)(2,1)} custom-call(s32[1]{0:T(128)} %bitcast.me_ref, bf16[32,16640]{1,0:T(8,128)(2,1)S(1)} %collective-permute-done.refs_0_, bf16[32,16640]{1,0:T(8,128)(2,1)S(1)} %collective-permute-done.1.refs_1_, bf16[32,16640]{1,0:T(8,128)(2,1)S(1)} %collective-permute-done.2.refs_2_, bf16[32,65536]{1,0:T(8,128)(2,1)} %bitcast.29, ...), custom_call_target="tpu_custom_call" | custom-call | flops 1610612736 | bytes 22020096 | tf_op jit(solution)/shard_map/residual/pallas_call | solution.py:390
  198.5 0.7 slice.4._
  199.2 0.0 collective-permute-done.6.refs_1_
  199.2 0.0 collective-permute-done.7.refs_2_
  199.2 0.0 collective-permute-done.8.refs_3_
  199.2 0.8 placed_rows.1
  (9 shorter events, 0.0 us)
Async XLA Ops:
  0.6 10.1 %copy-start.2 = (s32[1024,8]{0,1:T(8,128)S(1)}, s32[1024,8]{0,1:T(8,128)}, u32[]{:S(2)}) copy-start(s32[1024,8]{0,1:T(8,128)} %param.12) | copy-start | bytes 98308
  0.6 10.1 %copy-start.3 = (f32[1024,8]{0,1:T(8,128)S(1)}, f32[1024,8]{0,1:T(8,128)}, u32[]{:S(2)}) copy-start(f32[1024,8]{0,1:T(8,128)} %param.13) | copy-start | bytes 98308
  0.7 10.1 %copy-start.5 = (s32[1024,1]{0,1:T(1,128)S(1)}, s32[1024,1]{0,1:T(1,128)}, u32[]{:S(2)}) copy-start(s32[1024,1]{0,1:T(1,128)} %param.14) | copy-start | bytes 12292
  0.7 10.1 %copy-start.6 = (s32[1024]{0:T(1024)S(1)}, s32[1024]{0:T(1024)}, u32[]{:S(2)}) copy-start(s32[1024]{0:T(1024)} %param.15) | copy-start | bytes 12292
  3.7 181.9 %collective-permute-start = (bf16[32,16640]{1,0:T(8,128)(2,1)}, bf16[32,16640]{1,0:T(8,128)(2,1)S(1)}, u32[]{:S(2)}, u32[]{:S(2)}) collective-permute-start(bf16[32,16640]{1,0:T(8,128)(2,1)} %get-tuple-element.5), channel_id=1, source_target_pairs={{0,4},{4,8},{8,12},{12,0},{1,5},{5,9},{9,13},{13,1},{2,6},{6,10},{... | collective-permute-start | bytes 3194888 | tf_op jit(solution)/shard_map/ppermute | solution.py:72
  6.8 179.7 %collective-permute-start.1 = (bf16[32,16640]{1,0:T(8,128)(2,1)}, bf16[32,16640]{1,0:T(8,128)(2,1)S(1)}, u32[]{:S(2)}, u32[]{:S(2)}) collective-permute-start(bf16[32,16640]{1,0:T(8,128)(2,1)} %get-tuple-element.6), channel_id=1, source_target_pairs={{0,8},{4,12},{8,0},{12,4},{1,9},{5,13},{9,1},{13,5},{2,10},{6,14},... | collective-permute-start | bytes 3194888 | tf_op jit(solution)/shard_map/ppermute | solution.py:72
  9.4 177.1 %collective-permute-start.2 = (bf16[32,16640]{1,0:T(8,128)(2,1)}, bf16[32,16640]{1,0:T(8,128)(2,1)S(1)}, u32[]{:S(2)}, u32[]{:S(2)}) collective-permute-start(bf16[32,16640]{1,0:T(8,128)(2,1)} %get-tuple-element.7), channel_id=1, source_target_pairs={{0,12},{4,0},{8,4},{12,8},{1,13},{5,1},{9,5},{13,9},{2,14},{6,2},{... | collective-permute-start | bytes 3194888 | tf_op jit(solution)/shard_map/ppermute | solution.py:72
  10.8 70.6 %collective-permute-start.3 = (f32[17,1024]{1,0:T(8,128)S(1)}, f32[17,1024]{1,0:T(8,128)S(1)}, u32[]{:S(2)}, u32[]{:S(2)}) collective-permute-start(f32[17,1024]{1,0:T(8,128)S(1)} %listed.1.refs_0_), channel_id=1, source_target_pairs={{0,4},{4,8},{8,12},{12,0},{1,5},{5,9},{9,13},{13,1},{2,6},{6,10},{... | collective-permute-start | bytes 208904 | tf_op jit(solution)/shard_map/ppermute | solution.py:72
  11.5 97.0 %collective-permute-start.4 = (f32[17,1024]{1,0:T(8,128)S(1)}, f32[17,1024]{1,0:T(8,128)S(1)}, u32[]{:S(2)}, u32[]{:S(2)}) collective-permute-start(f32[17,1024]{1,0:T(8,128)S(1)} %listed.1.refs_0_), channel_id=1, source_target_pairs={{0,8},{4,12},{8,0},{12,4},{1,9},{5,13},{9,1},{13,5},{2,10},{6,14},... | collective-permute-start | bytes 208904 | tf_op jit(solution)/shard_map/ppermute | solution.py:72
  81.4 28.6 %collective-permute-start.5 = (f32[17,1024]{1,0:T(8,128)S(1)}, f32[17,1024]{1,0:T(8,128)}, u32[]{:S(2)}, u32[]{:S(2)}) collective-permute-start(f32[17,1024]{1,0:T(8,128)S(1)} %listed.1.refs_0_), channel_id=1, source_target_pairs={{0,12},{4,0},{8,4},{12,8},{1,13},{5,1},{9,5},{13,9},{2,14},{6,2},{... | collective-permute-start | bytes 208904 | tf_op jit(solution)/shard_map/ppermute | solution.py:72
  81.4 6.9 %copy-start.4 = (s32[256,3]{0,1:T(4,128)S(1)}, s32[256,3]{0,1:T(4,128)}, u32[]{:S(2)}) copy-start(s32[256,3]{0,1:T(4,128)} %param.10) | copy-start | bytes 9220
  88.3 2.8 %copy-start = (bf16[32,8,96,128]{3,2,1,0:T(8,128)(2,1)S(1)}, bf16[32,8,96,128]{3,2,1,0:T(8,128)(2,1)}, u32[]{:S(2)}) copy-start(bf16[32,8,96,128]{3,2,1,0:T(8,128)(2,1)} %copy.10) | copy-start | bytes 18874372
  157.1 29.5 %copy-start.1 = (f32[16384]{0:T(1024)S(1)}, f32[16384]{0:T(1024)}, u32[]{:S(2)}) copy-start(f32[16384]{0:T(1024)} %param.11) | copy-start | bytes 196612
  157.2 42.0 %collective-permute-start.6 = (f32[32,1024]{1,0:T(8,128)S(1)}, f32[32,1024]{1,0:T(8,128)S(1)}, u32[]{:S(2)}, u32[]{:S(2)}) collective-permute-start(f32[32,1024]{1,0:T(8,128)S(1)} %get-tuple-element.10), channel_id=1, source_target_pairs={{0,4},{4,8},{8,12},{12,0},{1,5},{5,9},{9,13},{13,1},{2,6},{6,10},{... | collective-permute-start | bytes 393224 | tf_op jit(solution)/shard_map/ppermute | solution.py:72
  181.7 17.5 %collective-permute-start.7 = (f32[32,1024]{1,0:T(8,128)S(1)}, f32[32,1024]{1,0:T(8,128)S(1)}, u32[]{:S(2)}, u32[]{:S(2)}) collective-permute-start(f32[32,1024]{1,0:T(8,128)S(1)} %get-tuple-element.9), channel_id=1, source_target_pairs={{0,8},{4,12},{8,0},{12,4},{1,9},{5,13},{9,1},{13,5},{2,10},{6,14},... | collective-permute-start | bytes 393224 | tf_op jit(solution)/shard_map/ppermute | solution.py:72
  185.7 13.5 %collective-permute-start.8 = (f32[32,1024]{1,0:T(8,128)S(1)}, f32[32,1024]{1,0:T(8,128)S(1)}, u32[]{:S(2)}, u32[]{:S(2)}) collective-permute-start(f32[32,1024]{1,0:T(8,128)S(1)} %get-tuple-element.8), channel_id=1, source_target_pairs={{0,12},{4,0},{8,4},{12,8},{1,13},{5,1},{9,5},{13,9},{2,14},{6,2},{... | collective-permute-start | bytes 393224 | tf_op jit(solution)/shard_map/ppermute | solution.py:72
where the time goes:
time: 200 us
  Pallas kernels  80.4 us (40%)
  waiting for transfers between devices  70.9 us (35%)
  starting transfers between devices  37.5 us (19%)
  local copies, waits for them, and re-layouts  10.5 us (5%)
    ppermute x9, waiting for transfers between devices, shifted(): lax.ppermute(x, 'edge', [(i, (i + shift) % peers) for i in range(peers)])  70.9 us
    pallas_call x1, Pallas kernels, site_sums(): pl.pallas_call(functools.partial(site_kernel, peers), in_specs=[SMEM, HBM...  47.2 us
    ppermute x9, starting transfers between devices, shifted(): lax.ppermute(x, 'edge', [(i, (i + shift) % peers) for i in range(peers)])  37.5 us
    pallas_call x1, Pallas kernels, banded(): pl.pallas_call(band_kernel, in_specs=[SMEM, SMEM, VMEM], out_specs=VMEM,...  17.4 us
    pallas_call x1, Pallas kernels, residual_of(): pl.pallas_call(functools.partial(residual_kernel, peers), grid_spec=pltpu...  11.9 us
    unnamed x15, local copies, waits for them, and re-layouts  9.74 us
  transfers between devices with their start and end apart: 9, of which 2 were waited for; matrix products, arithmetic and copies ran while one was open for 4% of the time, Pallas kernels for 38%

commit v1 on v0

--- a/solution.py
+++ b/solution.py
@@ -16,7 +16,9 @@
 
 LANE = 128
 PAIRS = 8
+TRIP = 2
 RIM = BS * HB
+KEEP = 4 * RIM
 
 
 def padded_2(shard, sides, width):
@@ -96,17 +98,16 @@
     )(rec_edge.T, rec_weight.T, rec_owner.T, rec_slot.reshape(1, recs))
 
 
-def cut_kernel(peers, me_ref, rows_ref, *refs):
+def cut_kernel(peers, low, me_ref, rows_ref, *refs):
     pieces, held, in_sems, out_sems = refs[: peers - 1], *refs[peers - 1 :]
     me = me_ref[0]
-    length = held.shape[2]
-    all_edges = rows_ref.shape[1]
+    width = held.shape[2]
     taken, put = [], []
     for s in range(1, peers):
-        start = start_of(lax.rem(me + s, peers), peers, all_edges)
+        start = start_of(lax.rem(me + s, peers), peers, rows_ref.shape[1]) + low
         taken.append(
             pltpu.make_async_copy(
-                rows_ref.at[:, pl.ds(pl.multiple_of(start, RIM), length)],
+                rows_ref.at[:, pl.ds(pl.multiple_of(start, RIM), width)],
                 held.at[s - 1],
                 in_sems.at[s - 1],
             )
@@ -126,17 +127,15 @@
     return jnp.clip(target * edge_count - RIM, 0, all_edges - edge_count - 2 * RIM)
 
 
-def cut(me, rows, peers):
-    cols, all_edges = rows.shape
-    length = all_edges // peers + 2 * RIM
-    piece = jax.ShapeDtypeStruct((cols, length), rows.dtype)
+def cut(me, rows, peers, low, high):
+    piece = jax.ShapeDtypeStruct((rows.shape[0], high - low), rows.dtype)
     return pl.pallas_call(
-        functools.partial(cut_kernel, peers),
+        functools.partial(cut_kernel, peers, low),
         in_specs=[SMEM, HBM],
         out_specs=[HBM] * (peers - 1),
         out_shape=[piece] * (peers - 1),
         scratch_shapes=[
-            pltpu.VMEM((peers - 1, cols, length), rows.dtype),
+            pltpu.VMEM((peers - 1,) + piece.shape, rows.dtype),
             pltpu.SemaphoreType.DMA((peers - 1,)),
             pltpu.SemaphoreType.DMA((peers - 1,)),
         ],
@@ -149,8 +148,11 @@
 def site_kernel(peers, me_ref, rows_ref, *refs):
     list_refs = refs[:peers]
     out_ref, rows, turned, picked, pred, ints, row_sems, int_sems = refs[peers : peers + 8]
-    edge_refs = refs[peers + 8 : 2 * peers + 8]
-    tables = refs[2 * peers + 8 :]
+    count = peers * (IW + 1)
+    edge_refs = [
+        refs[peers + 8 + s * (IW + 1) : peers + 8 + (s + 1) * (IW + 1)] for s in range(peers)
+    ]
+    tables = refs[peers + 8 + count :]
     cols = rows_ref.shape[0]
     edge_count = turned.shape[0]
     recs = list_refs[0].shape[1]
@@ -173,8 +175,12 @@
     for s in range(peers):
         ints[s, :IW, :] = list_refs[s][:IW, :].astype(jnp.int32)
         ints[s, IW : IW + 1, :] = list_refs[s][2 * IW :, :].astype(jnp.int32)
-        lists.append(pltpu.make_async_copy(ints.at[s], edge_refs[s], int_sems.at[s]))
-        lists[s].start()
+        for k in range(IW + 1):
+            copy = pltpu.make_async_copy(
+                ints.at[s, pl.ds(k, 1)], edge_refs[s][k], int_sems.at[s, k]
+            )
+            copy.start()
+            lists.append(copy)
     for table in tables:
         table[...] = jnp.zeros_like(table)
 
@@ -184,7 +190,7 @@
 
         def turn(t, _, part=part):
             at = pl.multiple_of(part * width + t * LANE, LANE)
-            turned[pl.ds(at, LANE), :] = rows[:, pl.ds(at, LANE)].astype(jnp.float32).T
+            turned[pl.ds(at, LANE), :] = rows[:, pl.ds(at, LANE)].T.astype(jnp.float32)
             return 0
 
         lax.fori_loop(0, width // LANE, turn, 0, unroll=2)
@@ -198,14 +204,14 @@
 
         def gather(r, _):
             for k in range(IW):
-                row = turned[pl.ds(edge_refs[0][k, first + r], 1), :]
+                row = turned[pl.ds(edge_refs[0][k][0, first + r], 1), :]
                 for q in range(1, peers):
-                    other = turned[pl.ds(edge_refs[q][k, first + r], 1), :]
+                    other = turned[pl.ds(edge_refs[q][k][0, first + r], 1), :]
                     row = jnp.where(lane == q, other, row)
                 picked[k, pl.ds(r, 1), :] = row
             return 0
 
-        lax.fori_loop(0, per, gather, 0, unroll=2)
+        lax.fori_loop(0, per, gather, 0, unroll=4)
         weights = [ref[IW : 2 * IW, pl.ds(first, per)] for ref in list_refs]
         weights.append(jnp.zeros((LANE - peers * IW, per), jnp.float32))
         weights = jnp.concatenate(weights, axis=0).T
@@ -217,11 +223,11 @@
         def scatter(r, _):
             row = pred[pl.ds(r, 1), :]
             for q in range(peers):
-                at = pl.ds(edge_refs[q][IW, first + r], 1)
+                at = pl.ds(edge_refs[q][IW][0, first + r], 1)
                 tables[q][at, :] = tables[q][at, :] + row
             return 0
 
-        lax.fori_loop(0, per, scatter, 0, unroll=2)
+        lax.fori_loop(0, per, scatter, 0, unroll=8)
         return 0
 
     lax.fori_loop(0, recs // per, receivers, 0)
@@ -261,9 +267,9 @@
             pltpu.VMEM((per, LANE), jnp.float32),
             pltpu.VMEM((peers, IW + 1, recs), jnp.int32),
             pltpu.SemaphoreType.DMA((parts, peers)),
-            pltpu.SemaphoreType.DMA((peers,)),
+            pltpu.SemaphoreType.DMA((peers, IW + 1)),
         ]
-        + [pltpu.SMEM((IW + 1, recs), jnp.int32)] * peers
+        + [pltpu.SMEM((1, recs), jnp.int32)] * (peers * (IW + 1))
         + [pltpu.VMEM((peers * SDEV, LANE), jnp.float32)] * peers,
         compiler_params=pltpu.CompilerParams(vmem_limit_bytes=24 << 20),
         cost_estimate=pl.CostEstimate(
@@ -294,29 +300,35 @@
 
 
 def band_kernel(first_ref, index_ref, blocks_ref, band_ref, lines):
+    step = pl.program_id(0)
     count = NNZB * BS // 2
     half = lax.broadcasted_iota(jnp.int32, (1, 2 * BS), 1) // BS
 
-    def pair(p, _):
-        base = 2 * p - HB + first_ref[0]
-        for side in range(2):
-            both = blocks_ref[2 * p + side].astype(jnp.float32)
+    def pairs(trip, _):
+        for row in range(2 * TRIP):
+            both = blocks_ref[trip * 2 * TRIP + row].astype(jnp.float32)
             crossed = pltpu.roll(both, BS, 1)
-            lines[side, pl.ds(0, count, stride=2), :] = jnp.where(half == 0, both, crossed)
-            lines[side, pl.ds(1, count, stride=2), :] = jnp.where(half == 0, crossed, both)
-        for side in range(2):
-            offs = [index_ref[k, 2 * p + side] - base for k in range(NNZB)]
+            lines[row, pl.ds(0, count, stride=2), :] = jnp.where(half == 0, both, crossed)
+            lines[row, pl.ds(1, count, stride=2), :] = jnp.where(half == 0, crossed, both)
+        for row in range(2 * TRIP):
+            p = step * PAIRS + trip * TRIP + row // 2
+            base = 2 * p - HB + first_ref[0]
+            offs = [index_ref[k, 2 * p + row % 2] - base for k in range(NNZB)]
+            blocks = [
+                lines[row, k * BS : (k + 1) * BS].astype(band_ref.dtype) for k in range(NNZB)
+            ]
+            side = pl.ds(row % 2 * BS, BS)
             for tile in range(band_ref.shape[2] // (2 * BS)):
-                here = half + 2 * tile
-                total = jnp.where(here == offs[0], lines[side, :BS], 0.0)
+                masks = [
+                    jnp.where(half + 2 * tile == off, 1.0, 0.0).astype(band_ref.dtype) for off in offs
+                ]
+                total = blocks[0] * masks[0]
                 for k in range(1, NNZB):
-                    total += jnp.where(here == offs[k], lines[side, k * BS : (k + 1) * BS], 0.0)
-                band_ref[p, side * BS : (side + 1) * BS, tile * 2 * BS : (tile + 1) * 2 * BS] = (
-                    total.astype(band_ref.dtype)
-                )
+                    total += blocks[k] * masks[k]
+                band_ref[p, side, tile * 2 * BS : (tile + 1) * 2 * BS] = total
         return 0
 
-    lax.fori_loop(0, band_ref.shape[0], pair, 0)
+    lax.fori_loop(0, PAIRS // TRIP, pairs, 0)
 
 
 def banded(kblocks, blk_index, first_block):
@@ -326,88 +338,116 @@
     window = 2 + 2 * HB
     return pl.pallas_call(
         band_kernel,
-        in_specs=[SMEM, SMEM, VMEM],
+        grid=(pairs // PAIRS,),
+        in_specs=[SMEM, SMEM, pl.BlockSpec((2 * PAIRS, lines, 2 * BS), lambda i: (i, 0, 0))],
         out_specs=VMEM,
-        scratch_shapes=[pltpu.VMEM((2, 2 * lines, 2 * BS), jnp.float32)],
+        scratch_shapes=[pltpu.VMEM((2 * TRIP, 2 * lines, 2 * BS), jnp.float32)],
         out_shape=jax.ShapeDtypeStruct((pairs, 2 * BS, window * BS), jnp.bfloat16),
         compiler_params=pltpu.CompilerParams(vmem_limit_bytes=24 << 20),
         cost_estimate=pl.CostEstimate(flops=0, bytes_accessed=40 << 20, transcendentals=0),
         name="banded",
-    )(first_block, blk_index.T, kblocks.reshape(count, lines, 2 * BS))
-
-
-def residual_kernel(peers, me_ref, *refs):
+    )(
+        first_block,
+        blk_index.T,
+        pltpu.with_memory_space_constraint(kblocks.reshape(count, lines, 2 * BS), pltpu.HBM),
+    )
+
+
+def residual_kernel(peers, first, low, keep, me_ref, *refs):
     pieces = refs[: peers - 1]
-    rows_ref, band_ref, sigma_ref, out_ref, panel, swap, own, own_sem = refs[peers - 1 :]
-    pieces = (own,) + pieces
-    cols, length = own.shape
+    refs = refs[peers - 1 :]
+    if keep:
+        ends, refs = refs[: peers - 1], refs[peers - 1 :]
+    rows_ref, band_ref, sigma_ref = refs[:3]
+    out_ref, panel, swap, own, own_sem = refs[3 if keep == 0 else 4 :]
+    cols, span = own.shape
     columns = panel.shape[0]
     step = pl.program_id(0)
     width = PAIRS * 2 * BS
-    reach = width + 2 * RIM
     me = me_ref[0]
 
     @pl.when(step == 0)
     def _():
-        at = pl.multiple_of(start_of(me, peers, rows_ref.shape[1]), RIM)
-        copy = pltpu.make_async_copy(rows_ref.at[:, pl.ds(at, length)], own, own_sem)
+        at = start_of(me, peers, rows_ref.shape[1]) + (low - keep)
+        copy = pltpu.make_async_copy(
+            rows_ref.at[:, pl.ds(pl.multiple_of(at, RIM), span)], own, own_sem
+        )
         copy.start()
-        panel[...] = jnp.zeros_like(panel)
+        panel[:, :RIM] = jnp.zeros((columns, RIM), panel.dtype)
+        panel[:, RIM + span :] = jnp.zeros((columns, RIM), panel.dtype)
         row = lax.broadcasted_iota(jnp.int32, (columns, columns), 0)
         col = lax.broadcasted_iota(jnp.int32, (columns, columns), 1)
         sign = jnp.where(row % 2 == 0, -1.0, 1.0)
         swap[...] = jnp.where(row + 1 - 2 * (row % 2) == col, sign, 0.0).astype(swap.dtype)
+        for s in range(1, peers):
+            at = pl.ds(pl.multiple_of(lax.rem(me + peers - s, peers) * cols, cols), cols)
+            if keep:
+                panel[at, RIM : RIM + keep] = ends[s - 1][:, ends[s - 1].shape[1] - keep :]
+            panel[at, RIM + keep : RIM + span] = pieces[s - 1][...]
         copy.wait()
-
-    first = jnp.where(me == 0, 0, jnp.where(me == peers - 1, -2 * RIM, -RIM))
-    want = step * width - RIM - first
-    start = jnp.clip(want, 0, length - reach)
-    src = pl.ds(pl.multiple_of(start, RIM), reach)
-    dst = pl.ds(pl.multiple_of(RIM + start - want, RIM), reach)
-    for s in range(peers):
-        at = pl.ds(pl.multiple_of(lax.rem(me + peers - s, peers) * cols, cols), cols)
-        panel[at, dst] = pieces[s][:, src]
-    swapped = jnp.dot(
-        swap[...], panel[:, 2 * RIM : 2 * RIM + width], preferred_element_type=jnp.float32
-    )
-    turned = swapped * sigma_ref[:, pl.ds(pl.multiple_of(step * width, width), width)]
+        panel[pl.ds(pl.multiple_of(me * cols, cols), cols), RIM : RIM + span] = own[...]
+
+    moved = jnp.where(me == 0, -RIM, jnp.where(me == peers - 1, RIM, 0))
+    start = (step + first) * width + RIM + moved - (low - keep)
+
+    def window(at, size):
+        return panel[:, pl.ds(pl.multiple_of(start + at, RIM), size)]
+
+    swapped = jnp.dot(swap[...], window(RIM, width), preferred_element_type=jnp.float32)
+    at = pl.multiple_of((step + first) * width, width)
+    turned = swapped * sigma_ref[:, pl.ds(at, width)]
     for t in range(PAIRS):
         at = t * 2 * BS
         stiff = lax.dot_general(
-            panel[:, RIM + at : RIM + at + 2 * (BS + RIM)],
-            band_ref[step * PAIRS + t],
+            window(at, 2 * (BS + RIM)),
+            band_ref[(step + first) * PAIRS + t],
             (((1,), (1,)), ((), ())),
             preferred_element_type=jnp.float32,
         )
         out_ref[:, at : at + 2 * BS] = (stiff + turned[:, at : at + 2 * BS]).astype(out_ref.dtype)
 
 
-def residual_of(rows, pieces, band, sigma, me, peers):
-    cols = pieces[0].shape[0]
+def residual_of(rows, parts, band, sigma, me, peers):
+    cols = rows.shape[0]
     edge_count = sigma.shape[0]
     columns = peers * cols
     width = PAIRS * 2 * BS
-    return pl.pallas_call(
-        functools.partial(residual_kernel, peers),
-        grid_spec=pltpu.PrefetchScalarGridSpec(
-            num_scalar_prefetch=1,
-            grid=(edge_count // width,),
-            in_specs=[VMEM] * (peers - 1) + [HBM, VMEM, VMEM],
-            out_specs=pl.BlockSpec((columns, width), lambda i, me: (0, i)),
-            scratch_shapes=[
-                pltpu.VMEM((columns, width + 4 * RIM), jnp.bfloat16),
-                pltpu.VMEM((columns, columns), jnp.bfloat16),
-                pltpu.VMEM(pieces[0].shape, rows.dtype),
-                pltpu.SemaphoreType.DMA,
-            ],
-        ),
-        out_shape=jax.ShapeDtypeStruct((columns, edge_count), jnp.bfloat16),
-        compiler_params=pltpu.CompilerParams(vmem_limit_bytes=24 << 20),
-        cost_estimate=pl.CostEstimate(
-            flops=2 * columns * edge_count * 384, bytes_accessed=21 << 20, transcendentals=0
-        ),
-        name="residual",
-    )(me, *pieces, rows, band, sigma.reshape(1, edge_count))
+    sigma = sigma.reshape(1, edge_count)
+    out, before = None, None
+    for first, steps, low, pieces in parts:
+        keep = KEEP if low else 0
+        span = keep + pieces[0].shape[1]
+        given = list(pieces) + (list(before) if keep else []) + [rows, band, sigma]
+        specs = [VMEM] * (len(given) - 3) + [HBM, VMEM, VMEM]
+        if out is not None:
+            given.append(out)
+            specs.append(pl.BlockSpec(memory_space=pl.ANY))
+        out = pl.pallas_call(
+            functools.partial(residual_kernel, peers, first, low, keep),
+            grid_spec=pltpu.PrefetchScalarGridSpec(
+                num_scalar_prefetch=1,
+                grid=(steps,),
+                in_specs=specs,
+                out_specs=pl.BlockSpec((columns, width), lambda i, me, first=first: (0, i + first)),
+                scratch_shapes=[
+                    pltpu.VMEM((columns, span + 2 * RIM), jnp.bfloat16),
+                    pltpu.VMEM((columns, columns), jnp.bfloat16),
+                    pltpu.VMEM((cols, span), rows.dtype),
+                    pltpu.SemaphoreType.DMA,
+                ],
+            ),
+            out_shape=jax.ShapeDtypeStruct((columns, edge_count), jnp.bfloat16),
+            input_output_aliases={len(given): 0} if out is not None else {},
+            compiler_params=pltpu.CompilerParams(vmem_limit_bytes=24 << 20),
+            cost_estimate=pl.CostEstimate(
+                flops=2 * columns * steps * width * 384,
+                bytes_accessed=(21 << 20) * steps * width // edge_count,
+                transcendentals=0,
+            ),
+            name="residual",
+        )(me, *given)
+        before = pieces
+    return out
 
 
 def on_device(fields, kblocks, blk_index, sigma, rec_edge, rec_weight, rec_owner, rec_slot):
@@ -424,11 +464,20 @@
     edge_count = sigma.shape[0]
     shifts = range(1, peers)
 
+    length = edge_count + 2 * RIM
+    width = PAIRS * 2 * BS
+    steps = edge_count // width
+    marks = [0, max(1, steps // 4), steps]
+    lanes = [0] + [m * width + KEEP - RIM for m in marks[1:-1]] + [length]
+
+    rows = pltpu.with_memory_space_constraint(rows, pltpu.HBM)
+    parts = []
+    for j, (low, high) in enumerate(zip(lanes, lanes[1:])):
+        blocks = cut(me, rows, peers, low, high)
+        pieces = [shifted(blocks[s - 1], s, peers) for s in shifts]
+        parts.append((marks[j], marks[j + 1] - marks[j], low, pieces))
     mine = listed(rec_edge, rec_weight, rec_owner, rec_slot)
     lists = [mine] + [shifted(mine, s, peers) for s in shifts]
-    rows = pltpu.with_memory_space_constraint(rows, pltpu.HBM)
-    parts = cut(me, rows, peers)
-    pieces = [shifted(parts[s - 1], s, peers) for s in shifts]
     band = banded(kblocks, blk_index, me * (edge_count // BS))
     own = site_sums(me, rows, lists, peers)
 
@@ -436,7 +485,7 @@
         return lax.dynamic_index_in_dim(own, target, axis=0, keepdims=False)
 
     got = [owned(position)] + [shifted(owned((position + s) % peers), s, peers) for s in shifts]
-    residual = residual_of(rows, pieces, band, sigma, me, peers)
+    residual = residual_of(rows, parts, band, sigma, me, peers)
     site_out = placed_rows(me, residual[:16, :LANE], got, peers)
     return residual[None], site_out[None]
 
@@ -451,6 +500,7 @@
         and cols * peers == LANE
         and peers * IW <= LANE
         and edge_count % (PAIRS * 2 * BS) == 0
+        and edge_count >= 4 * PAIRS * 2 * BS
         and recs % LANE == 0
         and peers > 1
     )

time: 200 us -> 177 us (0.89)
  Pallas kernels: 80.4 us -> 71.2 us
  waiting for transfers between devices: 70.9 us -> 62.5 us
  starting transfers between devices: 37.5 us -> 34.2 us
  local copies, waits for them, and re-layouts: 10.5 us -> 8.32 us
    pallas_call x1, Pallas kernels: 47.2 us -> 37.9 us  [site_sums(): pl.pallas_call(functools.partial(site_kernel, peers), in_specs=[SMEM, HBM...]
    ppermute x9 -> x12, waiting for transfers between devices: 70.9 us -> 62.5 us  [shifted(): lax.ppermute(x, 'edge', [(i, (i + shift) % peers) for i in range(peers)])]
    ppermute x9 -> x12, starting transfers between devices: 37.5 us -> 34.2 us  [shifted(): lax.ppermute(x, 'edge', [(i, (i + shift) % peers) for i in range(peers)])]
    unnamed x15 -> x17, local copies, waits for them, and re-layouts: 9.74 us -> 7.57 us
    pallas_call x3 -> x5, Pallas kernels: 32.4 us -> 32.4 us  [the longest x1 14.5 us: banded(): pl.pallas_call(band_kernel, grid=(pairs // PAIRS,), in_specs=[SMEM, SMEM,...]
  transfers between devices with their start and end apart: 9 -> 12, of which waited for: 2 -> 3; matrix products, arithmetic and copies ran while one was open for 4% -> 4% of each run, Pallas kernels for 38% -> 38%
where the time goes in v1:
time: 177 us
  Pallas kernels  71.2 us (40%)
  waiting for transfers between devices  62.5 us (35%)
  starting transfers between devices  34.2 us (19%)
  local copies, waits for them, and re-layouts  8.32 us (5%)
    ppermute x12, waiting for transfers between devices, shifted(): lax.ppermute(x, 'edge', [(i, (i + shift) % peers) for i in range(peers)])  62.5 us
    pallas_call x1, Pallas kernels, site_sums(): pl.pallas_call(functools.partial(site_kernel, peers), in_specs=[SMEM, HBM...  37.9 us
    ppermute x12, starting transfers between devices, shifted(): lax.ppermute(x, 'edge', [(i, (i + shift) % peers) for i in range(peers)])  34.2 us
    pallas_call x1, Pallas kernels, banded(): pl.pallas_call(band_kernel, grid=(pairs // PAIRS,), in_specs=[SMEM, SMEM,...  14.5 us
    pallas_call x2, Pallas kernels, residual_of(): pl.pallas_call(functools.partial(residual_kernel, peers, first, low, keep...  13.4 us
    unnamed x17, local copies, waits for them, and re-layouts  7.57 us
    pallas_call x2, Pallas kernels, cut(): pl.pallas_call(functools.partial(cut_kernel, peers, low), in_specs=[SMEM,...  4.54 us
  transfers between devices with their start and end apart: 12, of which 3 were waited for; matrix products, arithmetic and copies ran while one was open for 4% of the time, Pallas kernels for 38%

profile of v1, /device:TPU:0, one launch (start us, length us, event | category | flops | bytes accessed | tf_op | source)
XLA Modules:
  0.0 176.9 jit_solution(9000640292644077483)
XLA Ops:
  0.7 2.6 %cut.2 = (bf16[32,12160]{1,0:T(8,128)(2,1)}, bf16[32,12160]{1,0:T(8,128)(2,1)}, bf16[32,12160]{1,0:T(8,128)(2,1)}) custom-call(s32[1]{0:T(128)} %bitcast.me_ref, bf16[32,65536]{1,0:T(8,128)(2,1)} %bitcast.27), custom_call_target="tpu_custom_call" | custom-call | bytes 8388608 | tf_op jit(solution)/shard_map/cut/pallas_call | solution.py:132
  3.3 3.1 %collective-permute-start = (bf16[32,12160]{1,0:T(8,128)(2,1)}, bf16[32,12160]{1,0:T(8,128)(2,1)S(1)}, u32[]{:S(2)}, u32[]{:S(2)}) collective-permute-start(bf16[32,12160]{1,0:T(8,128)(2,1)} %get-tuple-element.8), channel_id=1, source_target_pairs={{0,4},{4,8},{8,12},{12,0},{1,5},{5,9},{9,13},{13,1},{2,6},{6,10},{... | collective-permute-start | bytes 2334728 | tf_op jit(solution)/shard_map/ppermute | solution.py:74
  6.4 2.6 %collective-permute-start.1 = (bf16[32,12160]{1,0:T(8,128)(2,1)}, bf16[32,12160]{1,0:T(8,128)(2,1)S(1)}, u32[]{:S(2)}, u32[]{:S(2)}) collective-permute-start(bf16[32,12160]{1,0:T(8,128)(2,1)} %get-tuple-element.9), channel_id=1, source_target_pairs={{0,8},{4,12},{8,0},{12,4},{1,9},{5,13},{9,1},{13,5},{2,10},{6,14},... | collective-permute-start | bytes 2334728 | tf_op jit(solution)/shard_map/ppermute | solution.py:74
  9.0 1.3 collective-permute-start.2
  10.3 1.9 %cut.3 = (bf16[32,4480]{1,0:T(8,128)(2,1)S(1)}, bf16[32,4480]{1,0:T(8,128)(2,1)}, bf16[32,4480]{1,0:T(8,128)(2,1)}) custom-call(s32[1]{0:T(128)} %bitcast.me_ref, bf16[32,65536]{1,0:T(8,128)(2,1)} %bitcast.28), custom_call_target="tpu_custom_call" | custom-call | bytes 8388608 | tf_op jit(solution)/shard_map/cut/pallas_call | solution.py:132
  12.3 0.7 collective-permute-start.3
  13.0 0.1 collective-permute-start.6
  13.2 54.6 %collective-permute-done.6.refs_1_ = f32[17,1024]{1,0:T(8,128)S(1)} collective-permute-done((f32[17,1024]{1,0:T(8,128)S(1)}, f32[17,1024]{1,0:T(8,128)S(1)}, u32[]{:S(2)}, u32[]{:S(2)}) %collective-permute-start.6) | collective-permute-done | bytes 69664 | tf_op jit(solution)/shard_map/ppermute | solution.py:74
  67.8 17.8 %collective-permute-start.7 = (f32[17,1024]{1,0:T(8,128)S(1)}, f32[17,1024]{1,0:T(8,128)S(1)}, u32[]{:S(2)}, u32[]{:S(2)}) collective-permute-start(f32[17,1024]{1,0:T(8,128)S(1)} %listed.1.refs_0_), channel_id=1, source_target_pairs={{0,8},{4,12},{8,0},{12,4},{1,9},{5,13},{9,1},{13,5},{2,10},{6,14},... | collective-permute-start | bytes 208904 | tf_op jit(solution)/shard_map/ppermute | solution.py:74
  85.6 3.6 %collective-permute-done.7.refs_2_ = f32[17,1024]{1,0:T(8,128)S(1)} collective-permute-done((f32[17,1024]{1,0:T(8,128)S(1)}, f32[17,1024]{1,0:T(8,128)S(1)}, u32[]{:S(2)}, u32[]{:S(2)}) %collective-permute-start.7) | collective-permute-done | bytes 69664 | tf_op jit(solution)/shard_map/ppermute | solution.py:74
  89.3 0.4 collective-permute-start.8
  89.7 4.2 %collective-permute-done.8.refs_3_ = f32[17,1024]{1,0:T(8,128)S(1)} collective-permute-done((f32[17,1024]{1,0:T(8,128)S(1)}, f32[17,1024]{1,0:T(8,128)S(1)}, u32[]{:S(2)}, u32[]{:S(2)}) %collective-permute-start.8) | collective-permute-done | bytes 69664 | tf_op jit(solution)/shard_map/ppermute | solution.py:74
  93.9 0.6 copy-done.1
  94.5 3.5 %collective-permute-start.4 = (bf16[32,4480]{1,0:T(8,128)(2,1)}, bf16[32,4480]{1,0:T(8,128)(2,1)S(1)}, u32[]{:S(2)}, u32[]{:S(2)}) collective-permute-start(bf16[32,4480]{1,0:T(8,128)(2,1)} %get-tuple-element.12), channel_id=1, source_target_pairs={{0,8},{4,12},{8,0},{12,4},{1,9},{5,13},{9,1},{13,5},{2,10},{6,14},... | collective-permute-start | bytes 860168 | tf_op jit(solution)/shard_map/ppermute | solution.py:74
  98.0 0.0 collective-permute-done.3.refs_0_.refs_3_
  98.0 0.0 collective-permute-start.5
  98.0 6.9 %copy.11 = bf16[32,8,96,128]{3,2,1,0:T(8,128)(2,1)} copy(bf16[32,8,96,128]{3,1,2,0:T(8,128)(2,1)} %bitcast.34) | data formatting | bytes 12582912
  105.0 14.5 %banded.1.refs_4_.refs_7_ = bf16[128,128,384]{2,1,0:T(8,128)(2,1)S(1)} custom-call(s32[1]{0:T(128)S(6)} %mul.3.first_ref, s32[3,256]{1,0:T(4,128)S(1)} %bitcast.24, bf16[256,96,128]{2,1,0:T(8,128)(2,1)} %bitcast.32), custom_call_target="tpu_custom_call" | custom-call | bytes 41943040 | tf_op jit(solution)/shard_map/banded/pallas_call | solution.py:339
  119.5 37.9 %site_sums.1 = f32[4,32,1024]{2,1,0:T(8,128)S(1)} custom-call(s32[1]{0:T(128)} %bitcast.me_ref, bf16[32,65536]{1,0:T(8,128)(2,1)} %bitcast.29, f32[17,1024]{1,0:T(8,128)S(1)} %listed.1.refs_0_, f32[17,1024]{1,0:T(8,128)S(1)} %collective-permute-done.6.refs_1_, f32[17,1024]{1,0:T(8,128)S(1)} %collective-permute-done.7.refs_2_, f32[17,1024]{1,0:T(8,128)S(1)} %copy-done.2), custom_call_target="tpu_custom_call" | custom-call | flops 67108864 | bytes 67108864 | tf_op jit(solution)/shard_map/site_sums/pallas_call | solution.py:258
  157.4 0.1 dynamic-slice_bitcast_fusion
  157.4 0.0 collective-permute-done.4.refs_1_.refs_4_
  157.4 1.1 collective-permute-start.10
  158.5 0.0 collective-permute-done.5.refs_2_.refs_5_
  158.5 3.4 %collective-permute-start.11 = (f32[32,1024]{1,0:T(8,128)S(1)}, f32[32,1024]{1,0:T(8,128)S(1)}, u32[]{:S(2)}, u32[]{:S(2)}) collective-permute-start(f32[32,1024]{1,0:T(8,128)S(1)} %get-tuple-element.14), channel_id=1, source_target_pairs={{0,12},{4,0},{8,4},{12,8},{1,13},{5,1},{9,5},{13,9},{2,14},{6,2},{... | collective-permute-start | bytes 393224 | tf_op jit(solution)/shard_map/ppermute | solution.py:74
  161.9 0.0 collective-permute-done.refs_0_
  161.9 0.0 collective-permute-start.9
  161.9 4.1 %residual.2.refs_9_ = bf16[128,16384]{1,0:T(8,128)(2,1)} custom-call(s32[1]{0:T(128)} %bitcast.me_ref, bf16[32,4480]{1,0:T(8,128)(2,1)S(1)} %collective-permute-done.3.refs_0_.refs_3_, bf16[32,4480]{1,0:T(8,128)(2,1)S(1)} %collective-permute-done.4.refs_1_.refs_4_, bf16[32,4480]{1,0:T(8,128)(2,1)S(1)} %collective-permute-done.5.refs_2_.refs_5_, ...), custom_call_target="tpu_custom_call" | custom-call | flops 402653184 | bytes 5505024 | tf_op jit(solution)/shard_map/residual/pallas_call | solution.py:425
  166.0 0.0 collective-permute-done.1.refs_1_
  166.0 0.0 collective-permute-done.2.refs_2_
  166.0 9.3 %residual.3 = bf16[128,16384]{1,0:T(8,128)(2,1)} custom-call(s32[1]{0:T(128)} %bitcast.me_ref, bf16[32,12160]{1,0:T(8,128)(2,1)S(1)} %collective-permute-done.refs_0_, bf16[32,12160]{1,0:T(8,128)(2,1)S(1)} %collective-permute-done.1.refs_1_, bf16[32,12160]{1,0:T(8,128)(2,1)S(1)} %collective-permute-done.2.refs_2_, ...), custom_call_target="tpu_custom_call", output_to_operand_aliasing={{}: (10, {})} | custom-call | flops 1207959552 | bytes 16515072 | tf_op jit(solution)/shard_map/residual/pallas_call | solution.py:425
  175.3 0.7 slice.4._
  176.0 0.8 placed_rows.1
  (19 shorter events, 0.0 us)
Async XLA Ops:
  0.6 12.4 %copy-start.3 = (s32[1024,8]{0,1:T(8,128)S(1)}, s32[1024,8]{0,1:T(8,128)}, u32[]{:S(2)}) copy-start(s32[1024,8]{0,1:T(8,128)} %param.12) | copy-start | bytes 98308
  0.6 12.4 %copy-start.4 = (f32[1024,8]{0,1:T(8,128)S(1)}, f32[1024,8]{0,1:T(8,128)}, u32[]{:S(2)}) copy-start(f32[1024,8]{0,1:T(8,128)} %param.13) | copy-start | bytes 98308
  0.7 12.4 %copy-start.6 = (s32[1024,1]{0,1:T(1,128)S(1)}, s32[1024,1]{0,1:T(1,128)}, u32[]{:S(2)}) copy-start(s32[1024,1]{0,1:T(1,128)} %param.14) | copy-start | bytes 12292
  0.7 12.3 %copy-start.7 = (s32[1024]{0:T(1024)S(1)}, s32[1024]{0:T(1024)}, u32[]{:S(2)}) copy-start(s32[1024]{0:T(1024)} %param.15) | copy-start | bytes 12292
  3.3 158.6 %collective-permute-start = (bf16[32,12160]{1,0:T(8,128)(2,1)}, bf16[32,12160]{1,0:T(8,128)(2,1)S(1)}, u32[]{:S(2)}, u32[]{:S(2)}) collective-permute-start(bf16[32,12160]{1,0:T(8,128)(2,1)} %get-tuple-element.8), channel_id=1, source_target_pairs={{0,4},{4,8},{8,12},{12,0},{1,5},{5,9},{9,13},{13,1},{2,6},{6,10},{... | collective-permute-start | bytes 2334728 | tf_op jit(solution)/shard_map/ppermute | solution.py:74
  6.4 159.6 %collective-permute-start.1 = (bf16[32,12160]{1,0:T(8,128)(2,1)}, bf16[32,12160]{1,0:T(8,128)(2,1)S(1)}, u32[]{:S(2)}, u32[]{:S(2)}) collective-permute-start(bf16[32,12160]{1,0:T(8,128)(2,1)} %get-tuple-element.9), channel_id=1, source_target_pairs={{0,8},{4,12},{8,0},{12,4},{1,9},{5,13},{9,1},{13,5},{2,10},{6,14},... | collective-permute-start | bytes 2334728 | tf_op jit(solution)/shard_map/ppermute | solution.py:74
  9.0 157.0 %collective-permute-start.2 = (bf16[32,12160]{1,0:T(8,128)(2,1)}, bf16[32,12160]{1,0:T(8,128)(2,1)S(1)}, u32[]{:S(2)}, u32[]{:S(2)}) collective-permute-start(bf16[32,12160]{1,0:T(8,128)(2,1)} %get-tuple-element.10), channel_id=1, source_target_pairs={{0,12},{4,0},{8,4},{12,8},{1,13},{5,1},{9,5},{13,9},{2,14},{6,2},{... | collective-permute-start | bytes 2334728 | tf_op jit(solution)/shard_map/ppermute | solution.py:74
  12.3 85.8 %collective-permute-start.3 = (bf16[32,4480]{1,0:T(8,128)(2,1)S(1)}, bf16[32,4480]{1,0:T(8,128)(2,1)S(1)}, u32[]{:S(2)}, u32[]{:S(2)}) collective-permute-start(bf16[32,4480]{1,0:T(8,128)(2,1)S(1)} %get-tuple-element.11), channel_id=1, source_target_pairs={{0,4},{4,8},{8,12},{12,0},{1,5},{5,9},{9,13},{13,1},{2,6},{6,10},{... | collective-permute-start | bytes 860168 | tf_op jit(solution)/shard_map/ppermute | solution.py:74
  13.0 54.7 %collective-permute-start.6 = (f32[17,1024]{1,0:T(8,128)S(1)}, f32[17,1024]{1,0:T(8,128)S(1)}, u32[]{:S(2)}, u32[]{:S(2)}) collective-permute-start(f32[17,1024]{1,0:T(8,128)S(1)} %listed.1.refs_0_), channel_id=1, source_target_pairs={{0,4},{4,8},{8,12},{12,0},{1,5},{5,9},{9,13},{13,1},{2,6},{6,10},{... | collective-permute-start | bytes 208904 | tf_op jit(solution)/shard_map/ppermute | solution.py:74
  67.8 21.5 %collective-permute-start.7 = (f32[17,1024]{1,0:T(8,128)S(1)}, f32[17,1024]{1,0:T(8,128)S(1)}, u32[]{:S(2)}, u32[]{:S(2)}) collective-permute-start(f32[17,1024]{1,0:T(8,128)S(1)} %listed.1.refs_0_), channel_id=1, source_target_pairs={{0,8},{4,12},{8,0},{12,4},{1,9},{5,13},{9,1},{13,5},{2,10},{6,14},... | collective-permute-start | bytes 208904 | tf_op jit(solution)/shard_map/ppermute | solution.py:74
  89.3 4.6 %collective-permute-start.8 = (f32[17,1024]{1,0:T(8,128)S(1)}, f32[17,1024]{1,0:T(8,128)S(1)}, u32[]{:S(2)}, u32[]{:S(2)}) collective-permute-start(f32[17,1024]{1,0:T(8,128)S(1)} %listed.1.refs_0_), channel_id=1, source_target_pairs={{0,12},{4,0},{8,4},{12,8},{1,13},{5,1},{9,5},{13,9},{2,14},{6,2},{... | collective-permute-start | bytes 208904 | tf_op jit(solution)/shard_map/ppermute | solution.py:74
  93.9 0.6 copy-start.1
  94.5 62.9 %collective-permute-start.4 = (bf16[32,4480]{1,0:T(8,128)(2,1)}, bf16[32,4480]{1,0:T(8,128)(2,1)S(1)}, u32[]{:S(2)}, u32[]{:S(2)}) collective-permute-start(bf16[32,4480]{1,0:T(8,128)(2,1)} %get-tuple-element.12), channel_id=1, source_target_pairs={{0,8},{4,12},{8,0},{12,4},{1,9},{5,13},{9,1},{13,5},{2,10},{6,14},... | collective-permute-start | bytes 860168 | tf_op jit(solution)/shard_map/ppermute | solution.py:74
  98.0 60.5 %collective-permute-start.5 = (bf16[32,4480]{1,0:T(8,128)(2,1)}, bf16[32,4480]{1,0:T(8,128)(2,1)S(1)}, u32[]{:S(2)}, u32[]{:S(2)}) collective-permute-start(bf16[32,4480]{1,0:T(8,128)(2,1)} %get-tuple-element.13), channel_id=1, source_target_pairs={{0,12},{4,0},{8,4},{12,8},{1,13},{5,1},{9,5},{13,9},{2,14},{6,2},{... | collective-permute-start | bytes 860168 | tf_op jit(solution)/shard_map/ppermute | solution.py:74
  98.0 6.9 %copy-start.5 = (s32[256,3]{0,1:T(4,128)S(1)}, s32[256,3]{0,1:T(4,128)}, u32[]{:S(2)}) copy-start(s32[256,3]{0,1:T(4,128)} %param.10) | copy-start | bytes 9220
  105.0 14.5 %copy-start.2 = (f32[17,1024]{1,0:T(8,128)S(1)}, f32[17,1024]{1,0:T(8,128)}, u32[]{:S(2)}) copy-start(f32[17,1024]{1,0:T(8,128)} %copy-done.1) | copy-start | bytes 208900
  105.0 56.9 %copy-start = (f32[16384]{0:T(1024)S(1)}, f32[16384]{0:T(1024)}, u32[]{:S(2)}) copy-start(f32[16384]{0:T(1024)} %param.11) | copy-start | bytes 196612
  157.4 18.6 %collective-permute-start.10 = (f32[32,1024]{1,0:T(8,128)S(1)}, f32[32,1024]{1,0:T(8,128)S(1)}, u32[]{:S(2)}, u32[]{:S(2)}) collective-permute-start(f32[32,1024]{1,0:T(8,128)S(1)} %get-tuple-element.15), channel_id=1, source_target_pairs={{0,8},{4,12},{8,0},{12,4},{1,9},{5,13},{9,1},{13,5},{2,10},{6,14},... | collective-permute-start | bytes 393224 | tf_op jit(solution)/shard_map/ppermute | solution.py:74
  158.5 17.5 %collective-permute-start.11 = (f32[32,1024]{1,0:T(8,128)S(1)}, f32[32,1024]{1,0:T(8,128)S(1)}, u32[]{:S(2)}, u32[]{:S(2)}) collective-permute-start(f32[32,1024]{1,0:T(8,128)S(1)} %get-tuple-element.14), channel_id=1, source_target_pairs={{0,12},{4,0},{8,4},{12,8},{1,13},{5,1},{9,5},{13,9},{2,14},{6,2},{... | collective-permute-start | bytes 393224 | tf_op jit(solution)/shard_map/ppermute | solution.py:74
  161.9 14.1 %collective-permute-start.9 = (f32[32,1024]{1,0:T(8,128)S(1)}, f32[32,1024]{1,0:T(8,128)S(1)}, u32[]{:S(2)}, u32[]{:S(2)}) collective-permute-start(f32[32,1024]{1,0:T(8,128)S(1)} %get-tuple-element.16), channel_id=1, source_target_pairs={{0,4},{4,8},{8,12},{12,0},{1,5},{5,9},{9,13},{13,1},{2,6},{6,10},{... | collective-permute-start | bytes 393224 | tf_op jit(solution)/shard_map/ppermute | solution.py:74

commit v2 on v1

--- a/solution.py
+++ b/solution.py
@@ -1,4 +1,5 @@
 import functools
+import math
 
 import jax
 import jax.numpy as jnp
@@ -19,6 +20,8 @@
 TRIP = 2
 RIM = BS * HB
 KEEP = 4 * RIM
+LINES = 2 * IW + 8
+TOP = 32000.0
 
 
 def padded_2(shard, sides, width):
@@ -79,42 +82,44 @@
 SMEM = pl.BlockSpec(memory_space=pltpu.SMEM)
 
 
-def list_kernel(edge_ref, weight_ref, owner_ref, slot_ref, list_ref):
-    list_ref[:IW, :] = edge_ref[...].astype(jnp.float32)
-    list_ref[IW : 2 * IW, :] = weight_ref[...]
-    sites = owner_ref[...] * SDEV + slot_ref[...]
-    list_ref[2 * IW :, :] = sites.astype(jnp.float32)
-
-
-def listed(rec_edge, rec_weight, rec_owner, rec_slot):
-    recs = rec_slot.shape[0]
-    return pl.pallas_call(
-        list_kernel,
-        in_specs=[VMEM] * 4,
-        out_specs=VMEM,
-        out_shape=jax.ShapeDtypeStruct((2 * IW + 1, recs), jnp.float32),
-        compiler_params=pltpu.CompilerParams(vmem_limit_bytes=1 << 20),
-        name="listed",
-    )(rec_edge.T, rec_weight.T, rec_owner.T, rec_slot.reshape(1, recs))
-
-
-def cut_kernel(peers, low, me_ref, rows_ref, *refs):
-    pieces, held, in_sems, out_sems = refs[: peers - 1], *refs[peers - 1 :]
-    me = me_ref[0]
-    width = held.shape[2]
+def pack_kernel(peers, lanes, me_ref, edge_ref, weight_ref, owner_ref, slot_ref, rows_ref, *refs):
+    parts = len(lanes) - 1
+    count = parts * (peers - 1)
+    list_ref, pieces, refs = refs[0], refs[1 : 1 + count], refs[1 + count :]
+    edges, weights, owners, slots, list_sems, in_sems, out_sems = refs[:7]
+    held = refs[7:]
+    recs = list_ref.shape[1]
+    share = pl.ds(pl.multiple_of(me_ref[1] * recs, recs), recs)
+    small = [
+        pltpu.make_async_copy(source.at[:, share], target, list_sems.at[i])
+        for i, (source, target) in enumerate(
+            [(edge_ref, edges), (weight_ref, weights), (owner_ref, owners), (slot_ref, slots)]
+        )
+    ]
+    for copy in small:
+        copy.start()
     taken, put = [], []
-    for s in range(1, peers):
-        start = start_of(lax.rem(me + s, peers), peers, rows_ref.shape[1]) + low
-        taken.append(
-            pltpu.make_async_copy(
-                rows_ref.at[:, pl.ds(pl.multiple_of(start, RIM), width)],
-                held.at[s - 1],
-                in_sems.at[s - 1],
+    for j in range(parts):
+        for s in range(1, peers):
+            target = lax.rem(me_ref[0] + s, peers)
+            start = start_of(target, peers, rows_ref.shape[1]) + lanes[j]
+            n = len(taken)
+            taken.append(
+                pltpu.make_async_copy(
+                    rows_ref.at[:, pl.ds(pl.multiple_of(start, RIM), lanes[j + 1] - lanes[j])],
+                    held[n],
+                    in_sems.at[n],
+                )
             )
-        )
-        put.append(pltpu.make_async_copy(held.at[s - 1], pieces[s - 1], out_sems.at[s - 1]))
+            put.append(pltpu.make_async_copy(held[n], pieces[n], out_sems.at[n]))
     for copy in taken:
         copy.start()
+    for copy in small:
+        copy.wait()
+    list_ref[:IW, :] = edges[...].astype(jnp.float32)
+    list_ref[IW : 2 * IW, :] = weights[...]
+    sites = (owners[...] * SDEV + slots[...]).astype(jnp.float32)
+    list_ref[2 * IW :, :] = jnp.broadcast_to(sites, (LINES - 2 * IW, recs))
     for copy, onward in zip(taken, put):
         copy.wait()
         onward.start()
@@ -127,35 +132,45 @@
     return jnp.clip(target * edge_count - RIM, 0, all_edges - edge_count - 2 * RIM)
 
 
-def cut(me, rows, peers, low, high):
-    piece = jax.ShapeDtypeStruct((rows.shape[0], high - low), rows.dtype)
-    return pl.pallas_call(
-        functools.partial(cut_kernel, peers, low),
-        in_specs=[SMEM, HBM],
-        out_specs=[HBM] * (peers - 1),
-        out_shape=[piece] * (peers - 1),
-        scratch_shapes=[
-            pltpu.VMEM((peers - 1,) + piece.shape, rows.dtype),
-            pltpu.SemaphoreType.DMA((peers - 1,)),
-            pltpu.SemaphoreType.DMA((peers - 1,)),
-        ],
+def packed(me, rec_edge, rec_weight, rec_owner, rec_slot, rows, peers, lanes, shares):
+    recs = rec_slot.shape[0]
+    share = recs // shares
+    cols = rows.shape[0]
+    shapes = [
+        (cols, high - low) for low, high in zip(lanes, lanes[1:]) for _ in range(1, peers)
+    ]
+    small = [rec_edge.T, rec_weight.T, rec_owner.T, rec_slot.reshape(1, recs)]
+    out = pl.pallas_call(
+        functools.partial(pack_kernel, peers, lanes),
+        in_specs=[SMEM] + [HBM] * 5,
+        out_specs=[VMEM] + [HBM] * len(shapes),
+        out_shape=[jax.ShapeDtypeStruct((LINES, share), jnp.float32)]
+        + [jax.ShapeDtypeStruct(shape, rows.dtype) for shape in shapes],
+        scratch_shapes=[pltpu.VMEM((x.shape[0], share), x.dtype) for x in small]
+        + [
+            pltpu.SemaphoreType.DMA((len(small),)),
+            pltpu.SemaphoreType.DMA((len(shapes),)),
+            pltpu.SemaphoreType.DMA((len(shapes),)),
+        ]
+        + [pltpu.VMEM(shape, rows.dtype) for shape in shapes],
         compiler_params=pltpu.CompilerParams(vmem_limit_bytes=8 << 20),
         cost_estimate=pl.CostEstimate(flops=0, bytes_accessed=8 << 20, transcendentals=0),
-        name="cut",
-    )(me, rows)
-
-
-def site_kernel(peers, me_ref, rows_ref, *refs):
-    list_refs = refs[:peers]
-    out_ref, rows, turned, picked, pred, ints, row_sems, int_sems = refs[peers : peers + 8]
-    count = peers * (IW + 1)
-    edge_refs = [
-        refs[peers + 8 + s * (IW + 1) : peers + 8 + (s + 1) * (IW + 1)] for s in range(peers)
-    ]
-    tables = refs[peers + 8 + count :]
+        name="packed",
+    )(me, *[pltpu.with_memory_space_constraint(x, pltpu.HBM) for x in small], rows)
+    return out[0], out[1:]
+
+
+def site_kernel(peers, shares, me_ref, rows_ref, *refs):
+    list_refs, refs = refs[:shares], refs[shares:]
+    own_ref, sent_refs, refs = refs[0], refs[1:peers], refs[peers:]
+    out_ref, rows, turned, picked, pred, ints, scale, row_sems, int_sems = refs[:9]
+    refs = refs[9:]
+    edge_refs = [refs[s * (IW + 1) : (s + 1) * (IW + 1)] for s in range(peers)]
+    tables = refs[peers * (IW + 1) :]
     cols = rows_ref.shape[0]
     edge_count = turned.shape[0]
-    recs = list_refs[0].shape[1]
+    share = list_refs[0].shape[1]
+    recs = shares * share
     per = picked.shape[1]
     parts = row_sems.shape[0]
     width = edge_count // parts
@@ -173,14 +188,20 @@
             fetch(part, s).start()
     lists = []
     for s in range(peers):
-        ints[s, :IW, :] = list_refs[s][:IW, :].astype(jnp.int32)
-        ints[s, IW : IW + 1, :] = list_refs[s][2 * IW :, :].astype(jnp.int32)
+        for j, ref in enumerate(list_refs):
+            at = slice(j * share, (j + 1) * share)
+            edges = ref[s * LINES : s * LINES + IW, :]
+            ints[s, :IW, at] = edges.astype(jnp.int32)
+            scale[s * IW : (s + 1) * IW, at] = ref[s * LINES + IW : s * LINES + 2 * IW, :]
+            sites = ref[s * LINES + 2 * IW : (s + 1) * LINES, :]
+            ints[s, IW:, at] = sites.astype(jnp.int32)
         for k in range(IW + 1):
             copy = pltpu.make_async_copy(
                 ints.at[s, pl.ds(k, 1)], edge_refs[s][k], int_sems.at[s, k]
             )
             copy.start()
             lists.append(copy)
+    scale[peers * IW :, :] = jnp.zeros((LANE - peers * IW, recs), jnp.float32)
     for table in tables:
         table[...] = jnp.zeros_like(table)
 
@@ -212,9 +233,7 @@
             return 0
 
         lax.fori_loop(0, per, gather, 0, unroll=4)
-        weights = [ref[IW : 2 * IW, pl.ds(first, per)] for ref in list_refs]
-        weights.append(jnp.zeros((LANE - peers * IW, per), jnp.float32))
-        weights = jnp.concatenate(weights, axis=0).T
+        weights = scale[:, pl.ds(first, per)].T
         total = jnp.zeros((per, LANE), jnp.float32)
         for k in range(IW):
             total += picked[k] * jnp.take_along_axis(weights, lanes * IW + k, axis=1)
@@ -247,6 +266,15 @@
         return 0
 
     lax.fori_loop(0, peers * per_owner, back, 0)
+    own_ref[...] = out_ref[me_ref[0]]
+    for s in range(1, peers):
+        block = out_ref[lax.rem(me_ref[0] + s, peers)]
+        most = jnp.max(jnp.abs(block), axis=1, keepdims=True)
+        power = jnp.floor(jnp.log(jnp.maximum(most, 1e-36)) * (1 / math.log(2.0))) + 1.0
+        coded = jnp.round(block * (TOP * jnp.exp2(-power)))
+        sent_refs[s - 1][:, :owned] = coded.astype(jnp.int32).astype(jnp.int16)
+        power = jnp.broadcast_to(power, (cols, LANE))
+        sent_refs[s - 1][:, owned:] = power.astype(jnp.int32).astype(jnp.int16)
 
 
 def site_sums(me, rows, lists, peers):
@@ -254,18 +282,22 @@
     edge_count = all_edges // peers
     per = LANE
     parts = 4
-    recs = lists[0].shape[1]
-    return pl.pallas_call(
-        functools.partial(site_kernel, peers),
-        in_specs=[SMEM, HBM] + [VMEM] * peers,
-        out_specs=VMEM,
-        out_shape=jax.ShapeDtypeStruct((peers, cols, SDEV), jnp.float32),
+    shares = len(lists)
+    recs = lists[0].shape[1] * shares
+    sent = jax.ShapeDtypeStruct((cols, SDEV + LANE), jnp.int16)
+    out = pl.pallas_call(
+        functools.partial(site_kernel, peers, shares),
+        in_specs=[SMEM, HBM] + [VMEM] * shares,
+        out_specs=[VMEM] * peers,
+        out_shape=[jax.ShapeDtypeStruct((cols, SDEV), jnp.float32)] + [sent] * (peers - 1),
         scratch_shapes=[
+            pltpu.VMEM((peers, cols, SDEV), jnp.float32),
             pltpu.VMEM((peers * cols, edge_count), rows.dtype),
             pltpu.VMEM((edge_count, LANE), jnp.float32),
             pltpu.VMEM((IW, per, LANE), jnp.float32),
             pltpu.VMEM((per, LANE), jnp.float32),
-            pltpu.VMEM((peers, IW + 1, recs), jnp.int32),
+            pltpu.VMEM((peers, IW + 8, recs), jnp.int32),
+            pltpu.VMEM((LANE, recs), jnp.float32),
             pltpu.SemaphoreType.DMA((parts, peers)),
             pltpu.SemaphoreType.DMA((peers, IW + 1)),
         ]
@@ -277,14 +309,19 @@
         ),
         name="site_sums",
     )(me, rows, *lists)
+    return out[0], out[1:]
 
 
 def place_kernel(peers, me_ref, _, *refs):
     out_ref = refs[peers]
-    cols = refs[0].shape[0]
+    cols, width = refs[0].shape
     for s in range(peers):
         at = lax.rem(me_ref[0] + peers - s, peers) * cols
-        out_ref[pl.ds(pl.multiple_of(at, 8), cols), :] = refs[s][...]
+        block = refs[s][:, :width].astype(jnp.int32) if s else refs[s][...]
+        if s:
+            power = refs[s][:, width:].astype(jnp.int32).astype(jnp.float32)
+            block = block.astype(jnp.float32) * (jnp.exp2(power[:, :1]) * (1 / TOP))
+        out_ref[pl.ds(pl.multiple_of(at, 8), cols), :] = block
 
 
 def placed_rows(me, after, got, peers):
@@ -458,8 +495,8 @@
 
 def ordered(fields, kblocks, blk_index, sigma, rec_edge, rec_weight, rec_owner, rec_slot):
     peers = lax.axis_size("edge")
-    position = lax.axis_index("edge")
-    me = position.reshape(1)
+    shares = lax.axis_size("tx") * lax.axis_size("rcv")
+    me = jnp.stack([lax.axis_index("edge"), lax.axis_index(("tx", "rcv"))])
     rows = fields[0]
     edge_count = sigma.shape[0]
     shifts = range(1, peers)
@@ -467,24 +504,24 @@
     length = edge_count + 2 * RIM
     width = PAIRS * 2 * BS
     steps = edge_count // width
-    marks = [0, max(1, steps // 4), steps]
+    marks = [0, 1, 1 + steps // 2, steps]
     lanes = [0] + [m * width + KEEP - RIM for m in marks[1:-1]] + [length]
 
     rows = pltpu.with_memory_space_constraint(rows, pltpu.HBM)
+    mine, blocks = packed(me, rec_edge, rec_weight, rec_owner, rec_slot, rows, peers, lanes, shares)
     parts = []
-    for j, (low, high) in enumerate(zip(lanes, lanes[1:])):
-        blocks = cut(me, rows, peers, low, high)
-        pieces = [shifted(blocks[s - 1], s, peers) for s in shifts]
-        parts.append((marks[j], marks[j + 1] - marks[j], low, pieces))
-    mine = listed(rec_edge, rec_weight, rec_owner, rec_slot)
+    for j in range(len(lanes) - 1):
+        pieces = [shifted(blocks[j * (peers - 1) + s - 1], s, peers) for s in shifts]
+        parts.append((marks[j], marks[j + 1] - marks[j], lanes[j], pieces))
     lists = [mine] + [shifted(mine, s, peers) for s in shifts]
-    band = banded(kblocks, blk_index, me * (edge_count // BS))
-    own = site_sums(me, rows, lists, peers)
-
-    def owned(target):
-        return lax.dynamic_index_in_dim(own, target, axis=0, keepdims=False)
-
-    got = [owned(position)] + [shifted(owned((position + s) % peers), s, peers) for s in shifts]
+    lists = jnp.concatenate(lists, axis=0)
+    lists = [lists] + [
+        lax.ppermute(lists, ("tx", "rcv"), [(i, (i + k) % shares) for i in range(shares)])
+        for k in range(1, shares)
+    ]
+    band = banded(kblocks, blk_index, me[:1] * (edge_count // BS))
+    own, sent = site_sums(me, rows, lists, peers)
+    got = [own] + [shifted(sent[s - 1], s, peers) for s in shifts]
     residual = residual_of(rows, parts, band, sigma, me, peers)
     site_out = placed_rows(me, residual[:16, :LANE], got, peers)
     return residual[None], site_out[None]
@@ -501,7 +538,7 @@
         and peers * IW <= LANE
         and edge_count % (PAIRS * 2 * BS) == 0
         and edge_count >= 4 * PAIRS * 2 * BS
-        and recs % LANE == 0
+        and recs % (LANE * mesh.shape["tx"] * mesh.shape["rcv"]) == 0
         and peers > 1
     )
 

time: 177 us -> 124 us (0.70)
  waiting for transfers between devices: 62.5 us -> 15.3 us
  starting transfers between devices: 34.2 us -> 24.2 us
  Pallas kernels: 71.2 us -> 74.9 us
    ppermute x12 -> x15, waiting for transfers between devices: 62.5 us -> 13.1 us  [shifted(): lax.ppermute(x, 'edge', [(i, (i + shift) % peers) for i in range(peers)])]
    ppermute x12 -> x15, starting transfers between devices: 34.2 us -> 22.2 us  [shifted(): lax.ppermute(x, 'edge', [(i, (i + shift) % peers) for i in range(peers)])]
    pallas_call x2 -> x3, Pallas kernels: 13.4 us -> 16.6 us  [residual_of(): pl.pallas_call(functools.partial(residual_kernel, peers, first, low, keep...]
    ppermute x0 -> x3, waiting for transfers between devices: none -> 2.22 us  [ordered(): lax.ppermute(lists, ('tx', 'rcv'), [(i, (i + k) % shares) for i in range(...]
    ppermute x0 -> x3, starting transfers between devices: none -> 2 us  [ordered(): lax.ppermute(lists, ('tx', 'rcv'), [(i, (i + k) % shares) for i in range(...]
    unnamed x17 -> x8, local copies, waits for them, and re-layouts: 7.57 us -> 6.94 us
    pallas_call x4 -> x2, Pallas kernels: 42.4 us -> 42.3 us  [the longest x1 38.6 us: site_sums(): pl.pallas_call(functools.partial(site_kernel, peers, shares), in_specs=[S...]
  transfers between devices with their start and end apart: 12 -> 18, of which waited for: 3 -> 5; matrix products, arithmetic and copies ran while one was open for 4% -> 6% of each run, Pallas kernels for 38% -> 57%
where the time goes in v2:
time: 124 us; the launch traced here: 123 us
  Pallas kernels  74.9 us (60%)
  starting transfers between devices  24.2 us (20%)
  waiting for transfers between devices  15.3 us (12%)
  local copies, waits for them, and re-layouts  7.64 us (6%)
    pallas_call x1, Pallas kernels, site_sums(): pl.pallas_call(functools.partial(site_kernel, peers, shares), in_specs=[S...  38.6 us
    ppermute x15, starting transfers between devices, shifted(): lax.ppermute(x, 'edge', [(i, (i + shift) % peers) for i in range(peers)])  22.2 us
    pallas_call x3, Pallas kernels, residual_of(): pl.pallas_call(functools.partial(residual_kernel, peers, first, low, keep...  16.6 us
    pallas_call x1, Pallas kernels, banded(): pl.pallas_call(band_kernel, grid=(pairs // PAIRS,), in_specs=[SMEM, SMEM,...  14.5 us
    ppermute x15, waiting for transfers between devices, shifted(): lax.ppermute(x, 'edge', [(i, (i + shift) % peers) for i in range(peers)])  13.1 us
    unnamed x8, local copies, waits for them, and re-layouts  6.94 us
    pallas_call x1, Pallas kernels, packed(): pl.pallas_call(functools.partial(pack_kernel, peers, lanes), in_specs=[SM...  3.74 us
  transfers between devices with their start and end apart: 18, of which 5 were waited for; matrix products, arithmetic and copies ran while one was open for 6% of the time, Pallas kernels for 57%

profile of v2, /device:TPU:0, one launch (start us, length us, event | category | flops | bytes accessed | tf_op | source)
XLA Modules:
  0.0 122.8 jit_solution(6676068164016260992)
XLA Ops:
  0.6 0.1 pad_add_fusion.me_ref
  0.7 3.7 %packed.1 = (f32[24,256]{1,0:T(8,128)S(1)}, bf16[32,1408]{1,0:T(8,128)(2,1)S(1)}, bf16[32,1408]{1,0:T(8,128)(2,1)S(1)}, bf16[32,1408]{1,0:T(8,128)(2,1)S(1)}, bf...) custom-call(s32[2]{0:T(128)S(1)} %pad_add_fusion.me_ref, ...), custom_call_target="tpu_custom_call" | custom-call | bytes 8388608 | tf_op jit(solution)/shard_map/packed/pallas_call | solution.py:143
  4.5 3.1 %collective-permute-start.9 = (f32[24,256]{1,0:T(8,128)S(1)}, f32[24,256]{1,0:T(8,128)S(1)}, u32[]{:S(2)}, u32[]{:S(2)}) collective-permute-start(f32[24,256]{1,0:T(8,128)S(1)} %get-tuple-element.25), channel_id=1, source_target_pairs={{0,4},{4,8},{8,12},{12,0},{1,5},{5,9},{9,13},{13,1},{2,6},{6,10},{... | collective-permute-start | bytes 73736 | tf_op jit(solution)/shard_map/ppermute | solution.py:77
  7.6 2.6 %collective-permute-start.10 = (f32[24,256]{1,0:T(8,128)S(1)}, f32[24,256]{1,0:T(8,128)S(1)}, u32[]{:S(2)}, u32[]{:S(2)}) collective-permute-start(f32[24,256]{1,0:T(8,128)S(1)} %get-tuple-element.25), channel_id=1, source_target_pairs={{0,8},{4,12},{8,0},{12,4},{1,9},{5,13},{9,1},{13,5},{2,10},{6,14},... | collective-permute-start | bytes 73736 | tf_op jit(solution)/shard_map/ppermute | solution.py:77
  10.2 1.3 %collective-permute-start.11 = (f32[24,256]{1,0:T(8,128)S(1)}, f32[24,256]{1,0:T(8,128)S(1)}, u32[]{:S(2)}, u32[]{:S(2)}) collective-permute-start(f32[24,256]{1,0:T(8,128)S(1)} %get-tuple-element.25), channel_id=1, source_target_pairs={{0,12},{4,0},{8,4},{12,8},{1,13},{5,1},{9,5},{13,9},{2,14},{6,2},{... | collective-permute-start | bytes 73736 | tf_op jit(solution)/shard_map/ppermute | solution.py:77
  11.5 0.7 collective-permute-start
  12.2 0.1 collective-permute-start.6
  12.3 0.2 collective-permute-done.10
  12.5 1.5 %collective-permute-done.11 = f32[24,256]{1,0:T(8,128)S(1)} collective-permute-done((f32[24,256]{1,0:T(8,128)S(1)}, f32[24,256]{1,0:T(8,128)S(1)}, u32[]{:S(2)}, u32[]{:S(2)}) %collective-permute-start.11) | collective-permute-done | bytes 24608 | tf_op jit(solution)/shard_map/ppermute | solution.py:77
  14.0 2.1 %collective-permute-start.7 = (bf16[32,1408]{1,0:T(8,128)(2,1)S(1)}, bf16[32,1408]{1,0:T(8,128)(2,1)S(1)}, u32[]{:S(2)}, u32[]{:S(2)}) collective-permute-start(bf16[32,1408]{1,0:T(8,128)(2,1)S(1)} %get-tuple-element.23), channel_id=1, source_target_pairs={{0,8},{4,12},{8,0},{12,4},{1,9},{5,13},{9,1},{13,5},{2,10},{6,14},... | collective-permute-start | bytes 270344 | tf_op jit(solution)/shard_map/ppermute | solution.py:77
  16.1 1.4 %collective-permute-start.8 = (bf16[32,1408]{1,0:T(8,128)(2,1)S(1)}, bf16[32,1408]{1,0:T(8,128)(2,1)S(1)}, u32[]{:S(2)}, u32[]{:S(2)}) collective-permute-start(bf16[32,1408]{1,0:T(8,128)(2,1)S(1)} %get-tuple-element.24), channel_id=1, source_target_pairs={{0,12},{4,0},{8,4},{12,8},{1,13},{5,1},{9,5},{13,9},{2,14},{6,2},{... | collective-permute-start | bytes 270344 | tf_op jit(solution)/shard_map/ppermute | solution.py:77
  17.5 11.0 %collective-permute-done.6.refs_0_.refs_3_ = bf16[32,1408]{1,0:T(8,128)(2,1)S(1)} collective-permute-done((bf16[32,1408]{1,0:T(8,128)(2,1)S(1)}, bf16[32,1408]{1,0:T(8,128)(2,1)S(1)}, u32[]{:S(2)}, u32[]{:S(2)}) %collective-permute-start.6) | collective-permute-done | bytes 90144 | tf_op jit(solution)/shard_map/ppermute | solution.py:77
  28.5 1.5 %collective-permute-start.13 = (f32[96,256]{1,0:T(8,128)S(1)}, f32[96,256]{1,0:T(8,128)S(1)}, u32[]{:S(2)}, u32[]{:S(2)}) collective-permute-start(f32[96,256]{1,0:T(8,128)S(1)} %constant_dynamic-update-slice_fusion.refs_0_), channel_id=1, source_target_pairs={{0,2},{1,3},{2,0},{3,1},{4,6},{5,7},{6,4},{7,5},{8,10},{9,11},{10,... | collective-permute-start | bytes 294920 | tf_op jit(solution)/shard_map/ppermute | solution.py:519
  30.0 0.3 collective-permute-done.7.refs_1_.refs_4_
  30.3 0.2 collective-permute-start.3
  30.6 2.8 %collective-permute-start.4 = (bf16[32,8192]{1,0:T(8,128)(2,1)S(1)}, bf16[32,8192]{1,0:T(8,128)(2,1)S(1)}, u32[]{:S(2)}, u32[]{:S(2)}) collective-permute-start(bf16[32,8192]{1,0:T(8,128)(2,1)S(1)} %get-tuple-element.20), channel_id=1, source_target_pairs={{0,8},{4,12},{8,0},{12,4},{1,9},{5,13},{9,1},{13,5},{2,10},{6,14},... | collective-permute-start | bytes 1572872 | tf_op jit(solution)/shard_map/ppermute | solution.py:77
  33.4 2.0 %collective-permute-start.5 = (bf16[32,8192]{1,0:T(8,128)(2,1)S(1)}, bf16[32,8192]{1,0:T(8,128)(2,1)S(1)}, u32[]{:S(2)}, u32[]{:S(2)}) collective-permute-start(bf16[32,8192]{1,0:T(8,128)(2,1)S(1)} %get-tuple-element.21), channel_id=1, source_target_pairs={{0,12},{4,0},{8,4},{12,8},{1,13},{5,1},{9,5},{13,9},{2,14},{6,2},{... | collective-permute-start | bytes 1572872 | tf_op jit(solution)/shard_map/ppermute | solution.py:77
  35.4 0.5 collective-permute-start.14
  35.9 2.2 %collective-permute-done.14.refs_3_ = f32[96,256]{1,0:T(8,128)S(1)} collective-permute-done((f32[96,256]{1,0:T(8,128)S(1)}, f32[96,256]{1,0:T(8,128)S(1)}, u32[]{:S(2)}, u32[]{:S(2)}) %collective-permute-start.14) | collective-permute-done | bytes 98336 | tf_op jit(solution)/shard_map/ppermute | solution.py:519
  38.1 0.7 collective-permute-start.1
  38.8 1.2 %collective-permute-start.2 = (bf16[32,7040]{1,0:T(8,128)(2,1)S(1)}, bf16[32,7040]{1,0:T(8,128)(2,1)S(1)}, u32[]{:S(2)}, u32[]{:S(2)}) collective-permute-start(bf16[32,7040]{1,0:T(8,128)(2,1)S(1)} %get-tuple-element.18), channel_id=1, source_target_pairs={{0,12},{4,0},{8,4},{12,8},{1,13},{5,1},{9,5},{13,9},{2,14},{6,2},{... | collective-permute-start | bytes 1351688 | tf_op jit(solution)/shard_map/ppermute | solution.py:77
  40.0 6.9 %copy.12 = bf16[32,8,96,128]{3,2,1,0:T(8,128)(2,1)} copy(bf16[32,8,96,128]{3,1,2,0:T(8,128)(2,1)} %bitcast.24) | data formatting | bytes 12582912
  47.0 14.5 %banded.1.refs_4_.refs_7_ = bf16[128,128,384]{2,1,0:T(8,128)(2,1)S(1)} custom-call(s32[1]{0:T(128)S(6)} %mul.7.first_ref, s32[3,256]{1,0:T(4,128)S(1)} %bitcast.16, bf16[256,96,128]{2,1,0:T(8,128)(2,1)} %bitcast.23), custom_call_target="tpu_custom_call" | custom-call | bytes 41943040 | tf_op jit(solution)/shard_map/banded/pallas_call | solution.py:376
  61.5 2.7 %residual.3.refs_9_ = bf16[128,16384]{1,0:T(8,128)(2,1)} custom-call(s32[2]{0:T(128)S(1)} %pad_add_fusion.me_ref, bf16[32,1408]{1,0:T(8,128)(2,1)S(1)} %collective-permute-done.6.refs_0_.refs_3_, bf16[32,1408]{1,0:T(8,128)(2,1)S(1)} %collective-permute-done.7.refs_1_.refs_4_, bf16[32,1408]{1,0:T(8,128)(2,1)S(1)} %collective-permute-done.8.refs_2_.refs_5_, ...), custom_call_target="tpu_custom_call" | custom-call | flops 100663296 | bytes 1376256 | tf_op jit(solution)/shard_map/residual/pallas_call | solution.py:462
  64.2 38.6 %site_sums.1 = (f32[32,1024]{1,0:T(8,128)S(1)}, s16[32,1152]{1,0:T(8,128)(2,1)S(1)}, s16[32,1152]{1,0:T(8,128)(2,1)S(1)}, s16[32,1152]{1,0:T(8,128)(2,1)S(1)}) custom-call(s32[2]{0:T(128)S(1)} %pad_add_fusion.me_ref, bf16[32,65536]{1,0:T(8,128)(2,1)} %bitcast.19, f32[96,256]{1,0:T(8,128)S(1)} %constant_dynamic-update-slice_fusion.refs_0_, ...), custom_call_target="tpu_custom_call" | custom-call | flops 67108864 | bytes 67108864 | tf_op jit(solution)/shard_map/site_sums/pallas_call | solution.py:288
  102.8 0.8 collective-permute-start.15
  103.6 2.2 %collective-permute-start.16 = (s16[32,1152]{1,0:T(8,128)(2,1)S(1)}, s16[32,1152]{1,0:T(8,128)(2,1)S(1)}, u32[]{:S(2)}, u32[]{:S(2)}) collective-permute-start(s16[32,1152]{1,0:T(8,128)(2,1)S(1)} %get-tuple-element.28), channel_id=1, source_target_pairs={{0,8},{4,12},{8,0},{12,4},{1,9},{5,13},{9,1},{13,5},{2,10},{6,14},... | collective-permute-start | bytes 221192 | tf_op jit(solution)/shard_map/ppermute | solution.py:77
  105.8 0.9 collective-permute-start.17
  106.7 7.3 %residual.4.refs_9_ = bf16[128,16384]{1,0:T(8,128)(2,1)} custom-call(s32[2]{0:T(128)S(1)} %pad_add_fusion.me_ref, bf16[32,8192]{1,0:T(8,128)(2,1)S(1)} %collective-permute-done.3.refs_0_.refs_3_, bf16[32,8192]{1,0:T(8,128)(2,1)S(1)} %collective-permute-done.4.refs_1_.refs_4_, ...), custom_call_target="tpu_custom_call", output_to_operand_aliasing={{}: (10, {})} | custom-call | flops 805306368 | bytes 11010048 | tf_op jit(solution)/shard_map/residual/pallas_call | solution.py:462
  114.0 6.7 %residual.5 = bf16[128,16384]{1,0:T(8,128)(2,1)} custom-call(s32[2]{0:T(128)S(1)} %pad_add_fusion.me_ref, bf16[32,7040]{1,0:T(8,128)(2,1)S(1)} %collective-permute-done.refs_0_, bf16[32,7040]{1,0:T(8,128)(2,1)S(1)} %collective-permute-done.1.refs_1_, bf16[32,7040]{1,0:T(8,128)(2,1)S(1)} %collective-permute-done.2.refs_2_, ...), custom_call_target="tpu_custom_call", output_to_operand_aliasing={{}: (10, {})} | custom-call | flops 704643072 | bytes 9633792 | tf_op jit(solution)/shard_map/residual/pallas_call | solution.py:462
  120.7 0.7 slice.4._
  121.4 1.4 %placed_rows.1 = f32[128,1024]{1,0:T(8,128)} custom-call(s32[2]{0:T(128)S(1)} %pad_add_fusion.me_ref, bf16[16,128]{1,0:T(8,128)(2,1)S(1)} %slice.4._, f32[32,1024]{1,0:T(8,128)S(1)} %get-tuple-element.26.refs_0_, s16[32,1152]{1,0:T(8,128)(2,1)S(1)} %collective-permute-done.15.refs_1_, s16[32,1152]{1,0:T(8,128)(2,1)S(1)} %collective-permute-done.16.refs_2_, ...), custom_call_target="tpu_custom_call" | custom-call | tf_op jit(solution)/shard_map/placed_rows/pallas_call | solution.py:329
  (22 shorter events, 0.1 us)
Async XLA Ops:
  4.5 7.8 %collective-permute-start.9 = (f32[24,256]{1,0:T(8,128)S(1)}, f32[24,256]{1,0:T(8,128)S(1)}, u32[]{:S(2)}, u32[]{:S(2)}) collective-permute-start(f32[24,256]{1,0:T(8,128)S(1)} %get-tuple-element.25), channel_id=1, source_target_pairs={{0,4},{4,8},{8,12},{12,0},{1,5},{5,9},{9,13},{13,1},{2,6},{6,10},{... | collective-permute-start | bytes 73736 | tf_op jit(solution)/shard_map/ppermute | solution.py:77
  7.6 5.0 %collective-permute-start.10 = (f32[24,256]{1,0:T(8,128)S(1)}, f32[24,256]{1,0:T(8,128)S(1)}, u32[]{:S(2)}, u32[]{:S(2)}) collective-permute-start(f32[24,256]{1,0:T(8,128)S(1)} %get-tuple-element.25), channel_id=1, source_target_pairs={{0,8},{4,12},{8,0},{12,4},{1,9},{5,13},{9,1},{13,5},{2,10},{6,14},... | collective-permute-start | bytes 73736 | tf_op jit(solution)/shard_map/ppermute | solution.py:77
  10.2 3.8 %collective-permute-start.11 = (f32[24,256]{1,0:T(8,128)S(1)}, f32[24,256]{1,0:T(8,128)S(1)}, u32[]{:S(2)}, u32[]{:S(2)}) collective-permute-start(f32[24,256]{1,0:T(8,128)S(1)} %get-tuple-element.25), channel_id=1, source_target_pairs={{0,12},{4,0},{8,4},{12,8},{1,13},{5,1},{9,5},{13,9},{2,14},{6,2},{... | collective-permute-start | bytes 73736 | tf_op jit(solution)/shard_map/ppermute | solution.py:77
  11.5 27.3 %collective-permute-start = (bf16[32,7040]{1,0:T(8,128)(2,1)S(1)}, bf16[32,7040]{1,0:T(8,128)(2,1)S(1)}, u32[]{:S(2)}, u32[]{:S(2)}) collective-permute-start(bf16[32,7040]{1,0:T(8,128)(2,1)S(1)} %get-tuple-element.16), channel_id=1, source_target_pairs={{0,4},{4,8},{8,12},{12,0},{1,5},{5,9},{9,13},{13,1},{2,6},{6,10},{... | collective-permute-start | bytes 1351688 | tf_op jit(solution)/shard_map/ppermute | solution.py:77
  12.2 16.3 %collective-permute-start.6 = (bf16[32,1408]{1,0:T(8,128)(2,1)S(1)}, bf16[32,1408]{1,0:T(8,128)(2,1)S(1)}, u32[]{:S(2)}, u32[]{:S(2)}) collective-permute-start(bf16[32,1408]{1,0:T(8,128)(2,1)S(1)} %get-tuple-element.22), channel_id=1, source_target_pairs={{0,4},{4,8},{8,12},{12,0},{1,5},{5,9},{9,13},{13,1},{2,6},{6,10},{... | collective-permute-start | bytes 270344 | tf_op jit(solution)/shard_map/ppermute | solution.py:77
  14.0 19.4 %collective-permute-start.12 = (f32[96,256]{1,0:T(8,128)S(1)}, f32[96,256]{1,0:T(8,128)S(1)}, u32[]{:S(2)}, u32[]{:S(2)}) collective-permute-start(f32[96,256]{1,0:T(8,128)S(1)} %constant_dynamic-update-slice_fusion.refs_0_), channel_id=1, source_target_pairs={{0,1},{1,2},{2,3},{3,0},{4,5},{5,6},{6,7},{7,4},{8,9},{9,10},{10,1... | collective-permute-start | bytes 294920 | tf_op jit(solution)/shard_map/ppermute | solution.py:519
  14.0 16.3 %collective-permute-start.7 = (bf16[32,1408]{1,0:T(8,128)(2,1)S(1)}, bf16[32,1408]{1,0:T(8,128)(2,1)S(1)}, u32[]{:S(2)}, u32[]{:S(2)}) collective-permute-start(bf16[32,1408]{1,0:T(8,128)(2,1)S(1)} %get-tuple-element.23), channel_id=1, source_target_pairs={{0,8},{4,12},{8,0},{12,4},{1,9},{5,13},{9,1},{13,5},{2,10},{6,14},... | collective-permute-start | bytes 270344 | tf_op jit(solution)/shard_map/ppermute | solution.py:77
  16.1 14.5 %collective-permute-start.8 = (bf16[32,1408]{1,0:T(8,128)(2,1)S(1)}, bf16[32,1408]{1,0:T(8,128)(2,1)S(1)}, u32[]{:S(2)}, u32[]{:S(2)}) collective-permute-start(bf16[32,1408]{1,0:T(8,128)(2,1)S(1)} %get-tuple-element.24), channel_id=1, source_target_pairs={{0,12},{4,0},{8,4},{12,8},{1,13},{5,1},{9,5},{13,9},{2,14},{6,2},{... | collective-permute-start | bytes 270344 | tf_op jit(solution)/shard_map/ppermute | solution.py:77
  28.5 6.9 %collective-permute-start.13 = (f32[96,256]{1,0:T(8,128)S(1)}, f32[96,256]{1,0:T(8,128)S(1)}, u32[]{:S(2)}, u32[]{:S(2)}) collective-permute-start(f32[96,256]{1,0:T(8,128)S(1)} %constant_dynamic-update-slice_fusion.refs_0_), channel_id=1, source_target_pairs={{0,2},{1,3},{2,0},{3,1},{4,6},{5,7},{6,4},{7,5},{8,10},{9,11},{10,... | collective-permute-start | bytes 294920 | tf_op jit(solution)/shard_map/ppermute | solution.py:519
  30.3 72.4 %collective-permute-start.3 = (bf16[32,8192]{1,0:T(8,128)(2,1)S(1)}, bf16[32,8192]{1,0:T(8,128)(2,1)S(1)}, u32[]{:S(2)}, u32[]{:S(2)}) collective-permute-start(bf16[32,8192]{1,0:T(8,128)(2,1)S(1)} %get-tuple-element.19), channel_id=1, source_target_pairs={{0,4},{4,8},{8,12},{12,0},{1,5},{5,9},{9,13},{13,1},{2,6},{6,10},{... | collective-permute-start | bytes 1572872 | tf_op jit(solution)/shard_map/ppermute | solution.py:77
  30.6 73.1 %collective-permute-start.4 = (bf16[32,8192]{1,0:T(8,128)(2,1)S(1)}, bf16[32,8192]{1,0:T(8,128)(2,1)S(1)}, u32[]{:S(2)}, u32[]{:S(2)}) collective-permute-start(bf16[32,8192]{1,0:T(8,128)(2,1)S(1)} %get-tuple-element.20), channel_id=1, source_target_pairs={{0,8},{4,12},{8,0},{12,4},{1,9},{5,13},{9,1},{13,5},{2,10},{6,14},... | collective-permute-start | bytes 1572872 | tf_op jit(solution)/shard_map/ppermute | solution.py:77
  33.4 72.5 %collective-permute-start.5 = (bf16[32,8192]{1,0:T(8,128)(2,1)S(1)}, bf16[32,8192]{1,0:T(8,128)(2,1)S(1)}, u32[]{:S(2)}, u32[]{:S(2)}) collective-permute-start(bf16[32,8192]{1,0:T(8,128)(2,1)S(1)} %get-tuple-element.21), channel_id=1, source_target_pairs={{0,12},{4,0},{8,4},{12,8},{1,13},{5,1},{9,5},{13,9},{2,14},{6,2},{... | collective-permute-start | bytes 1572872 | tf_op jit(solution)/shard_map/ppermute | solution.py:77
  35.4 2.7 %collective-permute-start.14 = (f32[96,256]{1,0:T(8,128)S(1)}, f32[96,256]{1,0:T(8,128)S(1)}, u32[]{:S(2)}, u32[]{:S(2)}) collective-permute-start(f32[96,256]{1,0:T(8,128)S(1)} %constant_dynamic-update-slice_fusion.refs_0_), channel_id=1, source_target_pairs={{0,3},{1,0},{2,1},{3,2},{4,7},{5,4},{6,5},{7,6},{8,11},{9,8},{10,9... | collective-permute-start | bytes 294920 | tf_op jit(solution)/shard_map/ppermute | solution.py:519
  38.1 75.9 %collective-permute-start.1 = (bf16[32,7040]{1,0:T(8,128)(2,1)S(1)}, bf16[32,7040]{1,0:T(8,128)(2,1)S(1)}, u32[]{:S(2)}, u32[]{:S(2)}) collective-permute-start(bf16[32,7040]{1,0:T(8,128)(2,1)S(1)} %get-tuple-element.17), channel_id=1, source_target_pairs={{0,8},{4,12},{8,0},{12,4},{1,9},{5,13},{9,1},{13,5},{2,10},{6,14},... | collective-permute-start | bytes 1351688 | tf_op jit(solution)/shard_map/ppermute | solution.py:77
  38.8 75.2 %collective-permute-start.2 = (bf16[32,7040]{1,0:T(8,128)(2,1)S(1)}, bf16[32,7040]{1,0:T(8,128)(2,1)S(1)}, u32[]{:S(2)}, u32[]{:S(2)}) collective-permute-start(bf16[32,7040]{1,0:T(8,128)(2,1)S(1)} %get-tuple-element.18), channel_id=1, source_target_pairs={{0,12},{4,0},{8,4},{12,8},{1,13},{5,1},{9,5},{13,9},{2,14},{6,2},{... | collective-permute-start | bytes 1351688 | tf_op jit(solution)/shard_map/ppermute | solution.py:77
  40.0 6.9 %copy-start.1 = (s32[256,3]{0,1:T(4,128)S(1)}, s32[256,3]{0,1:T(4,128)}, u32[]{:S(2)}) copy-start(s32[256,3]{0,1:T(4,128)} %param.10) | copy-start | bytes 9220
  47.0 14.5 %copy-start = (f32[16384]{0:T(1024)S(1)}, f32[16384]{0:T(1024)}, u32[]{:S(2)}) copy-start(f32[16384]{0:T(1024)} %param.11) | copy-start | bytes 196612
  102.8 18.6 %collective-permute-start.15 = (s16[32,1152]{1,0:T(8,128)(2,1)S(1)}, s16[32,1152]{1,0:T(8,128)(2,1)S(1)}, u32[]{:S(2)}, u32[]{:S(2)}) collective-permute-start(s16[32,1152]{1,0:T(8,128)(2,1)S(1)} %get-tuple-element.27), channel_id=1, source_target_pairs={{0,4},{4,8},{8,12},{12,0},{1,5},{5,9},{9,13},{13,1},{2,6},{6,10},{... | collective-permute-start | bytes 221192 | tf_op jit(solution)/shard_map/ppermute | solution.py:77
  103.6 17.8 %collective-permute-start.16 = (s16[32,1152]{1,0:T(8,128)(2,1)S(1)}, s16[32,1152]{1,0:T(8,128)(2,1)S(1)}, u32[]{:S(2)}, u32[]{:S(2)}) collective-permute-start(s16[32,1152]{1,0:T(8,128)(2,1)S(1)} %get-tuple-element.28), channel_id=1, source_target_pairs={{0,8},{4,12},{8,0},{12,4},{1,9},{5,13},{9,1},{13,5},{2,10},{6,14},... | collective-permute-start | bytes 221192 | tf_op jit(solution)/shard_map/ppermute | solution.py:77
  105.8 15.6 %collective-permute-start.17 = (s16[32,1152]{1,0:T(8,128)(2,1)S(1)}, s16[32,1152]{1,0:T(8,128)(2,1)S(1)}, u32[]{:S(2)}, u32[]{:S(2)}) collective-permute-start(s16[32,1152]{1,0:T(8,128)(2,1)S(1)} %get-tuple-element.29), channel_id=1, source_target_pairs={{0,12},{4,0},{8,4},{12,8},{1,13},{5,1},{9,5},{13,9},{2,14},{6,2},{... | collective-permute-start | bytes 221192 | tf_op jit(solution)/shard_map/ppermute | solution.py:77

commit v3 on v2

--- a/solution.py
+++ b/solution.py
@@ -396,7 +396,7 @@
     if keep:
         ends, refs = refs[: peers - 1], refs[peers - 1 :]
     rows_ref, band_ref, sigma_ref = refs[:3]
-    out_ref, panel, swap, own, own_sem = refs[3 if keep == 0 else 4 :]
+    out_ref, token_ref, panel, swap, own, own_sem = refs[3 if keep == 0 else 4 :]
     cols, span = own.shape
     columns = panel.shape[0]
     step = pl.program_id(0)
@@ -405,6 +405,7 @@
 
     @pl.when(step == 0)
     def _():
+        token_ref[...] = jnp.zeros_like(token_ref)
         at = start_of(me, peers, rows_ref.shape[1]) + (low - keep)
         copy = pltpu.make_async_copy(
             rows_ref.at[:, pl.ds(pl.multiple_of(at, RIM), span)], own, own_sem
@@ -459,13 +460,16 @@
         if out is not None:
             given.append(out)
             specs.append(pl.BlockSpec(memory_space=pl.ANY))
-        out = pl.pallas_call(
+        out, token = pl.pallas_call(
             functools.partial(residual_kernel, peers, first, low, keep),
             grid_spec=pltpu.PrefetchScalarGridSpec(
                 num_scalar_prefetch=1,
                 grid=(steps,),
                 in_specs=specs,
-                out_specs=pl.BlockSpec((columns, width), lambda i, me, first=first: (0, i + first)),
+                out_specs=[
+                    pl.BlockSpec((columns, width), lambda i, me, first=first: (0, i + first)),
+                    pl.BlockSpec((8, LANE), lambda i, me: (0, 0)),
+                ],
                 scratch_shapes=[
                     pltpu.VMEM((columns, span + 2 * RIM), jnp.bfloat16),
                     pltpu.VMEM((columns, columns), jnp.bfloat16),
@@ -473,7 +477,10 @@
                     pltpu.SemaphoreType.DMA,
                 ],
             ),
-            out_shape=jax.ShapeDtypeStruct((columns, edge_count), jnp.bfloat16),
+            out_shape=[
+                jax.ShapeDtypeStruct((columns, edge_count), jnp.bfloat16),
+                jax.ShapeDtypeStruct((8, LANE), jnp.float32),
+            ],
             input_output_aliases={len(given): 0} if out is not None else {},
             compiler_params=pltpu.CompilerParams(vmem_limit_bytes=24 << 20),
             cost_estimate=pl.CostEstimate(
@@ -481,10 +488,9 @@
                 bytes_accessed=(21 << 20) * steps * width // edge_count,
                 transcendentals=0,
             ),
-            name="residual",
         )(me, *given)
         before = pieces
-    return out
+    return out, token
 
 
 def on_device(fields, kblocks, blk_index, sigma, rec_edge, rec_weight, rec_owner, rec_slot):
@@ -504,7 +510,7 @@
     length = edge_count + 2 * RIM
     width = PAIRS * 2 * BS
     steps = edge_count // width
-    marks = [0, 1, 1 + steps // 2, steps]
+    marks = [0, 1, 1 + 5 * steps // 8, steps]
     lanes = [0] + [m * width + KEEP - RIM for m in marks[1:-1]] + [length]
 
     rows = pltpu.with_memory_space_constraint(rows, pltpu.HBM)
@@ -522,8 +528,8 @@
     band = banded(kblocks, blk_index, me[:1] * (edge_count // BS))
     own, sent = site_sums(me, rows, lists, peers)
     got = [own] + [shifted(sent[s - 1], s, peers) for s in shifts]
-    residual = residual_of(rows, parts, band, sigma, me, peers)
-    site_out = placed_rows(me, residual[:16, :LANE], got, peers)
+    residual, token = residual_of(rows, parts, band, sigma, me, peers)
+    site_out = placed_rows(me, token, got, peers)
     return residual[None], site_out[None]
 
 

time: 124 us -> 184 us (1.48)
  waiting for transfers between devices: 15.3 us -> 66.3 us
  starting transfers between devices: 24.2 us -> 34.8 us
    ppermute x15, waiting for transfers between devices: 13.1 us -> 56.9 us  [shifted(): lax.ppermute(x, 'edge', [(i, (i + shift) % peers) for i in range(peers)])]
    ppermute x15, starting transfers between devices: 22.2 us -> 33.3 us  [shifted(): lax.ppermute(x, 'edge', [(i, (i + shift) % peers) for i in range(peers)])]
    ppermute x3, waiting for transfers between devices: 2.22 us -> 9.38 us  [ordered(): lax.ppermute(lists, ('tx', 'rcv'), [(i, (i + k) % shares) for i in range(...]
  transfers between devices with their start and end apart: 18 -> 18, of which waited for: 5 -> 6; matrix products, arithmetic and copies ran while one was open for 6% -> 4% of each run, Pallas kernels for 57% -> 38%
where the time goes in v3:
time: 184 us
  Pallas kernels  74.9 us (41%)
  waiting for transfers between devices  66.3 us (36%)
  starting transfers between devices  34.8 us (19%)
  local copies, waits for them, and re-layouts  6.95 us (4%)
    ppermute x15, waiting for transfers between devices, shifted(): lax.ppermute(x, 'edge', [(i, (i + shift) % peers) for i in range(peers)])  56.9 us
    pallas_call x1, Pallas kernels, site_sums(): pl.pallas_call(functools.partial(site_kernel, peers, shares), in_specs=[S...  38.6 us
    ppermute x15, starting transfers between devices, shifted(): lax.ppermute(x, 'edge', [(i, (i + shift) % peers) for i in range(peers)])  33.3 us
    pallas_call x3, Pallas kernels, residual_of(): pl.pallas_call(functools.partial(residual_kernel, peers, first, low, keep...  16.6 us
    pallas_call x1, Pallas kernels, banded(): pl.pallas_call(band_kernel, grid=(pairs // PAIRS,), in_specs=[SMEM, SMEM,...  14.5 us
    ppermute x3, waiting for transfers between devices, ordered(): lax.ppermute(lists, ('tx', 'rcv'), [(i, (i + k) % shares) for i in range(...  9.38 us
    unnamed x8, local copies, waits for them, and re-layouts  6.94 us
    pallas_call x1, Pallas kernels, packed(): pl.pallas_call(functools.partial(pack_kernel, peers, lanes), in_specs=[SM...  3.78 us
  transfers between devices with their start and end apart: 18, of which 6 were waited for; matrix products, arithmetic and copies ran while one was open for 4% of the time, Pallas kernels for 38%

profile of v3, /device:TPU:0, one launch (start us, length us, event | category | flops | bytes accessed | tf_op | source)
XLA Modules:
  0.0 183.7 jit_solution(10092141332837253579)
XLA Ops:
  0.6 0.1 pad_add_fusion.me_ref
  0.7 3.8 %packed.1 = (f32[24,256]{1,0:T(8,128)S(1)}, bf16[32,1408]{1,0:T(8,128)(2,1)S(1)}, bf16[32,1408]{1,0:T(8,128)(2,1)S(1)}, bf16[32,1408]{1,0:T(8,128)(2,1)S(1)}, bf...) custom-call(s32[2]{0:T(128)S(1)} %pad_add_fusion.me_ref, ...), custom_call_target="tpu_custom_call" | custom-call | bytes 8388608 | tf_op jit(solution)/shard_map/packed/pallas_call | solution.py:143
  4.5 3.1 %collective-permute-start.9 = (f32[24,256]{1,0:T(8,128)S(1)}, f32[24,256]{1,0:T(8,128)S(1)}, u32[]{:S(2)}, u32[]{:S(2)}) collective-permute-start(f32[24,256]{1,0:T(8,128)S(1)} %get-tuple-element.33), channel_id=1, source_target_pairs={{0,4},{4,8},{8,12},{12,0},{1,5},{5,9},{9,13},{13,1},{2,6},{6,10},{... | collective-permute-start | bytes 73736 | tf_op jit(solution)/shard_map/ppermute | solution.py:77
  7.6 2.6 %collective-permute-start.10 = (f32[24,256]{1,0:T(8,128)S(1)}, f32[24,256]{1,0:T(8,128)S(1)}, u32[]{:S(2)}, u32[]{:S(2)}) collective-permute-start(f32[24,256]{1,0:T(8,128)S(1)} %get-tuple-element.33), channel_id=1, source_target_pairs={{0,8},{4,12},{8,0},{12,4},{1,9},{5,13},{9,1},{13,5},{2,10},{6,14},... | collective-permute-start | bytes 73736 | tf_op jit(solution)/shard_map/ppermute | solution.py:77
  10.2 1.3 collective-permute-start.11
  11.5 0.7 collective-permute-start.3
  12.2 0.3 collective-permute-start.4
  12.6 0.0 collective-permute-done.9
  12.6 2.9 %collective-permute-start.5 = (bf16[32,10240]{1,0:T(8,128)(2,1)S(1)}, bf16[32,10240]{1,0:T(8,128)(2,1)S(1)}, u32[]{:S(2)}, u32[]{:S(2)}) collective-permute-start(bf16[32,10240]{1,0:T(8,128)(2,1)S(1)} %get-tuple-element.25), channel_id=1, source_target_pairs={{0,12},{4,0},{8,4},{12,8},{1,13},{5,1},{9,5},{13,9},{2,14},{6,2},{... | collective-permute-start | bytes 1966088 | tf_op jit(solution)/shard_map/ppermute | solution.py:77
  15.4 0.6 collective-permute-start.6
  16.0 1.5 collective-permute-start.7
  17.5 42.7 %collective-permute-done.6.refs_0_.refs_3_ = bf16[32,1408]{1,0:T(8,128)(2,1)S(1)} collective-permute-done((bf16[32,1408]{1,0:T(8,128)(2,1)S(1)}, bf16[32,1408]{1,0:T(8,128)(2,1)S(1)}, u32[]{:S(2)}, u32[]{:S(2)}) %collective-permute-start.6) | collective-permute-done | bytes 90144 | tf_op jit(solution)/shard_map/ppermute | solution.py:77
  60.1 13.5 %collective-permute-start = (bf16[32,4992]{1,0:T(8,128)(2,1)S(1)}, bf16[32,4992]{1,0:T(8,128)(2,1)S(1)}, u32[]{:S(2)}, u32[]{:S(2)}) collective-permute-start(bf16[32,4992]{1,0:T(8,128)(2,1)S(1)} %get-tuple-element.20), channel_id=1, source_target_pairs={{0,4},{4,8},{8,12},{12,0},{1,5},{5,9},{9,13},{13,1},{2,6},{6,10},{... | collective-permute-start | bytes 958472 | tf_op jit(solution)/shard_map/ppermute | solution.py:77
  73.7 9.7 %collective-permute-done.7.refs_1_.refs_4_ = bf16[32,1408]{1,0:T(8,128)(2,1)S(1)} collective-permute-done((bf16[32,1408]{1,0:T(8,128)(2,1)S(1)}, bf16[32,1408]{1,0:T(8,128)(2,1)S(1)}, u32[]{:S(2)}, u32[]{:S(2)}) %collective-permute-start.7) | collective-permute-done | bytes 90144 | tf_op jit(solution)/shard_map/ppermute | solution.py:77
  83.4 4.5 %collective-permute-done.8.refs_2_.refs_5_ = bf16[32,1408]{1,0:T(8,128)(2,1)S(1)} collective-permute-done((bf16[32,1408]{1,0:T(8,128)(2,1)S(1)}, bf16[32,1408]{1,0:T(8,128)(2,1)S(1)}, u32[]{:S(2)}, u32[]{:S(2)}) %collective-permute-start.8) | collective-permute-done | bytes 90144 | tf_op jit(solution)/shard_map/ppermute | solution.py:77
  87.9 0.0 collective-permute-start.12
  87.9 4.0 %collective-permute-done.12.refs_1_ = f32[96,256]{1,0:T(8,128)S(1)} collective-permute-done((f32[96,256]{1,0:T(8,128)S(1)}, f32[96,256]{1,0:T(8,128)S(1)}, u32[]{:S(2)}, u32[]{:S(2)}) %collective-permute-start.12) | collective-permute-done | bytes 98336 | tf_op jit(solution)/shard_map/ppermute | solution.py:525
  91.9 1.5 collective-permute-start.13
  93.4 3.1 %collective-permute-done.13.refs_2_ = f32[96,256]{1,0:T(8,128)S(1)} collective-permute-done((f32[96,256]{1,0:T(8,128)S(1)}, f32[96,256]{1,0:T(8,128)S(1)}, u32[]{:S(2)}, u32[]{:S(2)}) %collective-permute-start.13) | collective-permute-done | bytes 98336 | tf_op jit(solution)/shard_map/ppermute | solution.py:525
  96.6 0.0 collective-permute-start.14
  96.6 2.2 %collective-permute-done.14.refs_3_ = f32[96,256]{1,0:T(8,128)S(1)} collective-permute-done((f32[96,256]{1,0:T(8,128)S(1)}, f32[96,256]{1,0:T(8,128)S(1)}, u32[]{:S(2)}, u32[]{:S(2)}) %collective-permute-start.14) | collective-permute-done | bytes 98336 | tf_op jit(solution)/shard_map/ppermute | solution.py:525
  98.8 2.0 %collective-permute-start.2 = (bf16[32,4992]{1,0:T(8,128)(2,1)S(1)}, bf16[32,4992]{1,0:T(8,128)(2,1)S(1)}, u32[]{:S(2)}, u32[]{:S(2)}) collective-permute-start(bf16[32,4992]{1,0:T(8,128)(2,1)S(1)} %get-tuple-element.22), channel_id=1, source_target_pairs={{0,12},{4,0},{8,4},{12,8},{1,13},{5,1},{9,5},{13,9},{2,14},{6,2},{... | collective-permute-start | bytes 958472 | tf_op jit(solution)/shard_map/ppermute | solution.py:77
  100.8 6.9 %copy.12 = bf16[32,8,96,128]{3,2,1,0:T(8,128)(2,1)} copy(bf16[32,8,96,128]{3,1,2,0:T(8,128)(2,1)} %bitcast.24) | data formatting | bytes 12582912
  107.7 14.5 %banded.1.refs_4_.refs_7_ = bf16[128,128,384]{2,1,0:T(8,128)(2,1)S(1)} custom-call(s32[1]{0:T(128)S(6)} %mul.7.first_ref, s32[3,256]{1,0:T(4,128)S(1)} %bitcast.16, bf16[256,96,128]{2,1,0:T(8,128)(2,1)} %bitcast.22), custom_call_target="tpu_custom_call" | custom-call | bytes 41943040 | tf_op jit(solution)/shard_map/banded/pallas_call | solution.py:376
  122.2 2.7 %shard_map.95 = (bf16[128,16384]{1,0:T(8,128)(2,1)}, f32[8,128]{1,0:T(8,128)}) custom-call(s32[2]{0:T(128)S(1)} %pad_add_fusion.me_ref, bf16[32,1408]{1,0:T(8,128)(2,1)S(1)} %collective-permute-done.6.refs_0_.refs_3_, bf16[32,1408]{1,0:T(8,128)(2,1)S(1)} %collective-permute-done.7.refs_1_.refs_4_, ...), custom_call_target="tpu_custom_call" | custom-call | flops 100663296 | bytes 1376256 | tf_op jit(solution)/shard_map/pallas_call | solution.py:463
  124.9 38.6 %site_sums.1 = (f32[32,1024]{1,0:T(8,128)S(1)}, s16[32,1152]{1,0:T(8,128)(2,1)S(1)}, s16[32,1152]{1,0:T(8,128)(2,1)S(1)}, s16[32,1152]{1,0:T(8,128)(2,1)S(1)}) custom-call(s32[2]{0:T(128)S(1)} %pad_add_fusion.me_ref, bf16[32,65536]{1,0:T(8,128)(2,1)} %bitcast.19, f32[96,256]{1,0:T(8,128)S(1)} %constant_dynamic-update-slice_fusion.refs_0_, ...), custom_call_target="tpu_custom_call" | custom-call | flops 67108864 | bytes 67108864 | tf_op jit(solution)/shard_map/site_sums/pallas_call | solution.py:288
  163.5 0.4 collective-permute-start.15
  163.9 2.6 %collective-permute-start.16 = (s16[32,1152]{1,0:T(8,128)(2,1)S(1)}, s16[32,1152]{1,0:T(8,128)(2,1)S(1)}, u32[]{:S(2)}, u32[]{:S(2)}) collective-permute-start(s16[32,1152]{1,0:T(8,128)(2,1)S(1)} %get-tuple-element.36), channel_id=1, source_target_pairs={{0,8},{4,12},{8,0},{12,4},{1,9},{5,13},{9,1},{13,5},{2,10},{6,14},... | collective-permute-start | bytes 221192 | tf_op jit(solution)/shard_map/ppermute | solution.py:77
  166.5 1.8 collective-permute-start.17
  168.3 8.6 %shard_map.96 = (bf16[128,16384]{1,0:T(8,128)(2,1)}, f32[8,128]{1,0:T(8,128)}) custom-call(s32[2]{0:T(128)S(1)} %pad_add_fusion.me_ref, bf16[32,10240]{1,0:T(8,128)(2,1)S(1)} %collective-permute-done.3.refs_0_.refs_3_, bf16[32,10240]{1,0:T(8,128)(2,1)S(1)} %collective-permute-done.4.refs_1_.refs_4_, ...), custom_call_target="tpu_custom_call", output_to_operand_aliasing={{0}: (10, {})} | custom-call | flops 1006632960 | bytes 13762560 | tf_op jit(solution)/shard_map/pallas_call | solution.py:463
  176.9 5.3 %shard_map.97 = (bf16[128,16384]{1,0:T(8,128)(2,1)}, f32[8,128]{1,0:T(8,128)S(1)}) custom-call(s32[2]{0:T(128)S(1)} %pad_add_fusion.me_ref, bf16[32,4992]{1,0:T(8,128)(2,1)S(1)} %collective-permute-done.refs_0_, bf16[32,4992]{1,0:T(8,128)(2,1)S(1)} %collective-permute-done.1.refs_1_, ...), custom_call_target="tpu_custom_call", output_to_operand_aliasing={{0}: (10, {})} | custom-call | flops 503316480 | bytes 6881280 | tf_op jit(solution)/shard_map/pallas_call | solution.py:463
  182.3 1.4 placed_rows.1
  (21 shorter events, 0.1 us)
Async XLA Ops:
  4.5 8.1 %collective-permute-start.9 = (f32[24,256]{1,0:T(8,128)S(1)}, f32[24,256]{1,0:T(8,128)S(1)}, u32[]{:S(2)}, u32[]{:S(2)}) collective-permute-start(f32[24,256]{1,0:T(8,128)S(1)} %get-tuple-element.33), channel_id=1, source_target_pairs={{0,4},{4,8},{8,12},{12,0},{1,5},{5,9},{9,13},{13,1},{2,6},{6,10},{... | collective-permute-start | bytes 73736 | tf_op jit(solution)/shard_map/ppermute | solution.py:77
  7.6 7.8 %collective-permute-start.10 = (f32[24,256]{1,0:T(8,128)S(1)}, f32[24,256]{1,0:T(8,128)S(1)}, u32[]{:S(2)}, u32[]{:S(2)}) collective-permute-start(f32[24,256]{1,0:T(8,128)S(1)} %get-tuple-element.33), channel_id=1, source_target_pairs={{0,8},{4,12},{8,0},{12,4},{1,9},{5,13},{9,1},{13,5},{2,10},{6,14},... | collective-permute-start | bytes 73736 | tf_op jit(solution)/shard_map/ppermute | solution.py:77
  10.2 5.8 %collective-permute-start.11 = (f32[24,256]{1,0:T(8,128)S(1)}, f32[24,256]{1,0:T(8,128)S(1)}, u32[]{:S(2)}, u32[]{:S(2)}) collective-permute-start(f32[24,256]{1,0:T(8,128)S(1)} %get-tuple-element.33), channel_id=1, source_target_pairs={{0,12},{4,0},{8,4},{12,8},{1,13},{5,1},{9,5},{13,9},{2,14},{6,2},{... | collective-permute-start | bytes 73736 | tf_op jit(solution)/shard_map/ppermute | solution.py:77
  11.5 152.0 %collective-permute-start.3 = (bf16[32,10240]{1,0:T(8,128)(2,1)S(1)}, bf16[32,10240]{1,0:T(8,128)(2,1)S(1)}, u32[]{:S(2)}, u32[]{:S(2)}) collective-permute-start(bf16[32,10240]{1,0:T(8,128)(2,1)S(1)} %get-tuple-element.23), channel_id=1, source_target_pairs={{0,4},{4,8},{8,12},{12,0},{1,5},{5,9},{9,13},{13,1},{2,6},{6,10},{... | collective-permute-start | bytes 1966088 | tf_op jit(solution)/shard_map/ppermute | solution.py:77
  12.2 151.7 %collective-permute-start.4 = (bf16[32,10240]{1,0:T(8,128)(2,1)S(1)}, bf16[32,10240]{1,0:T(8,128)(2,1)S(1)}, u32[]{:S(2)}, u32[]{:S(2)}) collective-permute-start(bf16[32,10240]{1,0:T(8,128)(2,1)S(1)} %get-tuple-element.24), channel_id=1, source_target_pairs={{0,8},{4,12},{8,0},{12,4},{1,9},{5,13},{9,1},{13,5},{2,10},{6,14},... | collective-permute-start | bytes 1966088 | tf_op jit(solution)/shard_map/ppermute | solution.py:77
  12.6 154.0 %collective-permute-start.5 = (bf16[32,10240]{1,0:T(8,128)(2,1)S(1)}, bf16[32,10240]{1,0:T(8,128)(2,1)S(1)}, u32[]{:S(2)}, u32[]{:S(2)}) collective-permute-start(bf16[32,10240]{1,0:T(8,128)(2,1)S(1)} %get-tuple-element.25), channel_id=1, source_target_pairs={{0,12},{4,0},{8,4},{12,8},{1,13},{5,1},{9,5},{13,9},{2,14},{6,2},{... | collective-permute-start | bytes 1966088 | tf_op jit(solution)/shard_map/ppermute | solution.py:77
  15.4 44.7 %collective-permute-start.6 = (bf16[32,1408]{1,0:T(8,128)(2,1)S(1)}, bf16[32,1408]{1,0:T(8,128)(2,1)S(1)}, u32[]{:S(2)}, u32[]{:S(2)}) collective-permute-start(bf16[32,1408]{1,0:T(8,128)(2,1)S(1)} %get-tuple-element.26), channel_id=1, source_target_pairs={{0,4},{4,8},{8,12},{12,0},{1,5},{5,9},{9,13},{13,1},{2,6},{6,10},{... | collective-permute-start | bytes 270344 | tf_op jit(solution)/shard_map/ppermute | solution.py:77
  16.0 67.3 %collective-permute-start.7 = (bf16[32,1408]{1,0:T(8,128)(2,1)S(1)}, bf16[32,1408]{1,0:T(8,128)(2,1)S(1)}, u32[]{:S(2)}, u32[]{:S(2)}) collective-permute-start(bf16[32,1408]{1,0:T(8,128)(2,1)S(1)} %get-tuple-element.27), channel_id=1, source_target_pairs={{0,8},{4,12},{8,0},{12,4},{1,9},{5,13},{9,1},{13,5},{2,10},{6,14},... | collective-permute-start | bytes 270344 | tf_op jit(solution)/shard_map/ppermute | solution.py:77
  60.1 38.6 %collective-permute-start = (bf16[32,4992]{1,0:T(8,128)(2,1)S(1)}, bf16[32,4992]{1,0:T(8,128)(2,1)S(1)}, u32[]{:S(2)}, u32[]{:S(2)}) collective-permute-start(bf16[32,4992]{1,0:T(8,128)(2,1)S(1)} %get-tuple-element.20), channel_id=1, source_target_pairs={{0,4},{4,8},{8,12},{12,0},{1,5},{5,9},{9,13},{13,1},{2,6},{6,10},{... | collective-permute-start | bytes 958472 | tf_op jit(solution)/shard_map/ppermute | solution.py:77
  83.4 4.5 %collective-permute-start.8 = (bf16[32,1408]{1,0:T(8,128)(2,1)S(1)}, bf16[32,1408]{1,0:T(8,128)(2,1)S(1)}, u32[]{:S(2)}, u32[]{:S(2)}) collective-permute-start(bf16[32,1408]{1,0:T(8,128)(2,1)S(1)} %get-tuple-element.28), channel_id=1, source_target_pairs={{0,12},{4,0},{8,4},{12,8},{1,13},{5,1},{9,5},{13,9},{2,14},{6,2},{... | collective-permute-start | bytes 270344 | tf_op jit(solution)/shard_map/ppermute | solution.py:77
  87.9 4.0 %collective-permute-start.12 = (f32[96,256]{1,0:T(8,128)S(1)}, f32[96,256]{1,0:T(8,128)S(1)}, u32[]{:S(2)}, u32[]{:S(2)}) collective-permute-start(f32[96,256]{1,0:T(8,128)S(1)} %constant_dynamic-update-slice_fusion.refs_0_), channel_id=1, source_target_pairs={{0,1},{1,2},{2,3},{3,0},{4,5},{5,6},{6,7},{7,4},{8,9},{9,10},{10,1... | collective-permute-start | bytes 294920 | tf_op jit(solution)/shard_map/ppermute | solution.py:525
  91.9 4.6 %collective-permute-start.13 = (f32[96,256]{1,0:T(8,128)S(1)}, f32[96,256]{1,0:T(8,128)S(1)}, u32[]{:S(2)}, u32[]{:S(2)}) collective-permute-start(f32[96,256]{1,0:T(8,128)S(1)} %constant_dynamic-update-slice_fusion.refs_0_), channel_id=1, source_target_pairs={{0,2},{1,3},{2,0},{3,1},{4,6},{5,7},{6,4},{7,5},{8,10},{9,11},{10,... | collective-permute-start | bytes 294920 | tf_op jit(solution)/shard_map/ppermute | solution.py:525
  96.6 2.2 %collective-permute-start.14 = (f32[96,256]{1,0:T(8,128)S(1)}, f32[96,256]{1,0:T(8,128)S(1)}, u32[]{:S(2)}, u32[]{:S(2)}) collective-permute-start(f32[96,256]{1,0:T(8,128)S(1)} %constant_dynamic-update-slice_fusion.refs_0_), channel_id=1, source_target_pairs={{0,3},{1,0},{2,1},{3,2},{4,7},{5,4},{6,5},{7,6},{8,11},{9,8},{10,9... | collective-permute-start | bytes 294920 | tf_op jit(solution)/shard_map/ppermute | solution.py:525
  98.8 78.1 %collective-permute-start.1 = (bf16[32,4992]{1,0:T(8,128)(2,1)S(1)}, bf16[32,4992]{1,0:T(8,128)(2,1)S(1)}, u32[]{:S(2)}, u32[]{:S(2)}) collective-permute-start(bf16[32,4992]{1,0:T(8,128)(2,1)S(1)} %get-tuple-element.21), channel_id=1, source_target_pairs={{0,8},{4,12},{8,0},{12,4},{1,9},{5,13},{9,1},{13,5},{2,10},{6,14},... | collective-permute-start | bytes 958472 | tf_op jit(solution)/shard_map/ppermute | solution.py:77
  98.8 78.1 %collective-permute-start.2 = (bf16[32,4992]{1,0:T(8,128)(2,1)S(1)}, bf16[32,4992]{1,0:T(8,128)(2,1)S(1)}, u32[]{:S(2)}, u32[]{:S(2)}) collective-permute-start(bf16[32,4992]{1,0:T(8,128)(2,1)S(1)} %get-tuple-element.22), channel_id=1, source_target_pairs={{0,12},{4,0},{8,4},{12,8},{1,13},{5,1},{9,5},{13,9},{2,14},{6,2},{... | collective-permute-start | bytes 958472 | tf_op jit(solution)/shard_map/ppermute | solution.py:77
  100.8 6.9 %copy-start.1 = (s32[256,3]{0,1:T(4,128)S(1)}, s32[256,3]{0,1:T(4,128)}, u32[]{:S(2)}) copy-start(s32[256,3]{0,1:T(4,128)} %param.10) | copy-start | bytes 9220
  107.7 14.5 %copy-start = (f32[16384]{0:T(1024)S(1)}, f32[16384]{0:T(1024)}, u32[]{:S(2)}) copy-start(f32[16384]{0:T(1024)} %param.11) | copy-start | bytes 196612
  163.5 18.8 %collective-permute-start.15 = (s16[32,1152]{1,0:T(8,128)(2,1)S(1)}, s16[32,1152]{1,0:T(8,128)(2,1)S(1)}, u32[]{:S(2)}, u32[]{:S(2)}) collective-permute-start(s16[32,1152]{1,0:T(8,128)(2,1)S(1)} %get-tuple-element.35), channel_id=1, source_target_pairs={{0,4},{4,8},{8,12},{12,0},{1,5},{5,9},{9,13},{13,1},{2,6},{6,10},{... | collective-permute-start | bytes 221192 | tf_op jit(solution)/shard_map/ppermute | solution.py:77
  163.9 18.3 %collective-permute-start.16 = (s16[32,1152]{1,0:T(8,128)(2,1)S(1)}, s16[32,1152]{1,0:T(8,128)(2,1)S(1)}, u32[]{:S(2)}, u32[]{:S(2)}) collective-permute-start(s16[32,1152]{1,0:T(8,128)(2,1)S(1)} %get-tuple-element.36), channel_id=1, source_target_pairs={{0,8},{4,12},{8,0},{12,4},{1,9},{5,13},{9,1},{13,5},{2,10},{6,14},... | collective-permute-start | bytes 221192 | tf_op jit(solution)/shard_map/ppermute | solution.py:77
  166.5 15.8 %collective-permute-start.17 = (s16[32,1152]{1,0:T(8,128)(2,1)S(1)}, s16[32,1152]{1,0:T(8,128)(2,1)S(1)}, u32[]{:S(2)}, u32[]{:S(2)}) collective-permute-start(s16[32,1152]{1,0:T(8,128)(2,1)S(1)} %get-tuple-element.37), channel_id=1, source_target_pairs={{0,12},{4,0},{8,4},{12,8},{1,13},{5,1},{9,5},{13,9},{2,14},{6,2},{... | collective-permute-start | bytes 221192 | tf_op jit(solution)/shard_map/ppermute | solution.py:77

commit v4 on v3

--- a/solution.py
+++ b/solution.py
@@ -16,8 +16,9 @@
 SDEV = 1024
 
 LANE = 128
-PAIRS = 8
-TRIP = 2
+GROUP = 4
+GROUPS = 4
+REACH = GROUP * BS + 2 * BS * HB
 RIM = BS * HB
 KEEP = 4 * RIM
 LINES = 2 * IW + 8
@@ -341,46 +342,50 @@
     count = NNZB * BS // 2
     half = lax.broadcasted_iota(jnp.int32, (1, 2 * BS), 1) // BS
 
-    def pairs(trip, _):
-        for row in range(2 * TRIP):
-            both = blocks_ref[trip * 2 * TRIP + row].astype(jnp.float32)
+    def group(trip, _):
+        p = step * GROUPS + trip
+        base = GROUP * p - HB + first_ref[0]
+        for row in range(GROUP):
+            both = blocks_ref[trip * GROUP + row].astype(jnp.float32)
             crossed = pltpu.roll(both, BS, 1)
             lines[row, pl.ds(0, count, stride=2), :] = jnp.where(half == 0, both, crossed)
             lines[row, pl.ds(1, count, stride=2), :] = jnp.where(half == 0, crossed, both)
-        for row in range(2 * TRIP):
-            p = step * PAIRS + trip * TRIP + row // 2
-            base = 2 * p - HB + first_ref[0]
-            offs = [index_ref[k, 2 * p + row % 2] - base for k in range(NNZB)]
+        for row in range(GROUP):
+            offs = [index_ref[k, GROUP * p + row] - base for k in range(NNZB)]
             blocks = [
                 lines[row, k * BS : (k + 1) * BS].astype(band_ref.dtype) for k in range(NNZB)
             ]
-            side = pl.ds(row % 2 * BS, BS)
-            for tile in range(band_ref.shape[2] // (2 * BS)):
-                masks = [
-                    jnp.where(half + 2 * tile == off, 1.0, 0.0).astype(band_ref.dtype) for off in offs
-                ]
-                total = blocks[0] * masks[0]
-                for k in range(1, NNZB):
-                    total += blocks[k] * masks[k]
-                band_ref[p, side, tile * 2 * BS : (tile + 1) * 2 * BS] = total
+            for tile in range(REACH // (2 * BS)):
+                at = slice(tile * 2 * BS, (tile + 1) * 2 * BS)
+                if row // 2 <= tile <= (row + 2 * HB) // 2:
+                    masks = [
+                        jnp.where(half + 2 * tile == off, 1.0, 0.0).astype(band_ref.dtype)
+                        for off in offs
+                    ]
+                    total = blocks[0] * masks[0]
+                    for k in range(1, NNZB):
+                        total += blocks[k] * masks[k]
+                else:
+                    total = jnp.zeros((BS, 2 * BS), band_ref.dtype)
+                band_ref[p, row * BS : (row + 1) * BS, at] = total
         return 0
 
-    lax.fori_loop(0, PAIRS // TRIP, pairs, 0)
+    lax.fori_loop(0, GROUPS, group, 0)
 
 
 def banded(kblocks, blk_index, first_block):
     count = kblocks.shape[0]
-    pairs = count // 2
+    groups = count // GROUP
     lines = NNZB * BS // 2
-    window = 2 + 2 * HB
+    blocks = pl.BlockSpec((GROUPS * GROUP, lines, 2 * BS), lambda i: (i, 0, 0))
     return pl.pallas_call(
         band_kernel,
-        grid=(pairs // PAIRS,),
-        in_specs=[SMEM, SMEM, pl.BlockSpec((2 * PAIRS, lines, 2 * BS), lambda i: (i, 0, 0))],
+        grid=(groups // GROUPS,),
+        in_specs=[SMEM, SMEM, blocks],
         out_specs=VMEM,
-        scratch_shapes=[pltpu.VMEM((2 * TRIP, 2 * lines, 2 * BS), jnp.float32)],
-        out_shape=jax.ShapeDtypeStruct((pairs, 2 * BS, window * BS), jnp.bfloat16),
-        compiler_params=pltpu.CompilerParams(vmem_limit_bytes=24 << 20),
+        scratch_shapes=[pltpu.VMEM((GROUP, 2 * lines, 2 * BS), jnp.float32)],
+        out_shape=jax.ShapeDtypeStruct((groups, GROUP * BS, REACH), jnp.bfloat16),
+        compiler_params=pltpu.CompilerParams(vmem_limit_bytes=28 << 20),
         cost_estimate=pl.CostEstimate(flops=0, bytes_accessed=40 << 20, transcendentals=0),
         name="banded",
     )(
@@ -400,7 +405,7 @@
     cols, span = own.shape
     columns = panel.shape[0]
     step = pl.program_id(0)
-    width = PAIRS * 2 * BS
+    width = GROUPS * GROUP * BS
     me = me_ref[0]
 
     @pl.when(step == 0)
@@ -434,22 +439,22 @@
     swapped = jnp.dot(swap[...], window(RIM, width), preferred_element_type=jnp.float32)
     at = pl.multiple_of((step + first) * width, width)
     turned = swapped * sigma_ref[:, pl.ds(at, width)]
-    for t in range(PAIRS):
-        at = t * 2 * BS
+    for t in range(GROUPS):
+        at = slice(t * GROUP * BS, (t + 1) * GROUP * BS)
         stiff = lax.dot_general(
-            window(at, 2 * (BS + RIM)),
-            band_ref[(step + first) * PAIRS + t],
+            window(t * GROUP * BS, REACH),
+            band_ref[(step + first) * GROUPS + t],
             (((1,), (1,)), ((), ())),
             preferred_element_type=jnp.float32,
         )
-        out_ref[:, at : at + 2 * BS] = (stiff + turned[:, at : at + 2 * BS]).astype(out_ref.dtype)
+        out_ref[:, at] = (stiff + turned[:, at]).astype(out_ref.dtype)
 
 
 def residual_of(rows, parts, band, sigma, me, peers):
     cols = rows.shape[0]
     edge_count = sigma.shape[0]
     columns = peers * cols
-    width = PAIRS * 2 * BS
+    width = GROUPS * GROUP * BS
     sigma = sigma.reshape(1, edge_count)
     out, before = None, None
     for first, steps, low, pieces in parts:
@@ -508,9 +513,9 @@
     shifts = range(1, peers)
 
     length = edge_count + 2 * RIM
-    width = PAIRS * 2 * BS
+    width = GROUPS * GROUP * BS
     steps = edge_count // width
-    marks = [0, 1, 1 + 5 * steps // 8, steps]
+    marks = [0, 1, steps - 2, steps]
     lanes = [0] + [m * width + KEEP - RIM for m in marks[1:-1]] + [length]
 
     rows = pltpu.with_memory_space_constraint(rows, pltpu.HBM)
@@ -542,8 +547,8 @@
         cols % 16 == 0
         and cols * peers == LANE
         and peers * IW <= LANE
-        and edge_count % (PAIRS * 2 * BS) == 0
-        and edge_count >= 4 * PAIRS * 2 * BS
+        and edge_count % (GROUPS * GROUP * BS) == 0
+        and edge_count >= 8 * GROUPS * GROUP * BS
         and recs % (LANE * mesh.shape["tx"] * mesh.shape["rcv"]) == 0
         and peers > 1
     )

time: 184 us -> 188 us (1.022)
  waiting for transfers between devices: 66.3 us -> 83.8 us
  starting transfers between devices: 34.8 us -> 20.3 us
    ppermute x15, waiting for transfers between devices: 56.9 us -> 80.6 us  [shifted(): lax.ppermute(x, 'edge', [(i, (i + shift) % peers) for i in range(peers)])]
    ppermute x15, starting transfers between devices: 33.3 us -> 18.8 us  [shifted(): lax.ppermute(x, 'edge', [(i, (i + shift) % peers) for i in range(peers)])]
    ppermute x3, waiting for transfers between devices: 9.38 us -> 3.2 us  [ordered(): lax.ppermute(lists, ('tx', 'rcv'), [(i, (i + k) % shares) for i in range(...]
  transfers between devices with their start and end apart: 18 -> 18, of which waited for: 6 -> 8; matrix products, arithmetic and copies ran while one was open for 4% -> 4% of each run, Pallas kernels for 38% -> 37%
where the time goes in v4:
time: 188 us; the launch traced here: 187 us
  waiting for transfers between devices  83.8 us (45%)
  Pallas kernels  75.2 us (40%)
  starting transfers between devices  20.3 us (11%)
  local copies, waits for them, and re-layouts  6.95 us (4%)
    ppermute x15, waiting for transfers between devices, shifted(): lax.ppermute(x, 'edge', [(i, (i + shift) % peers) for i in range(peers)])  80.6 us
    pallas_call x1, Pallas kernels, site_sums(): pl.pallas_call(functools.partial(site_kernel, peers, shares), in_specs=[S...  38.6 us
    ppermute x15, starting transfers between devices, shifted(): lax.ppermute(x, 'edge', [(i, (i + shift) % peers) for i in range(peers)])  18.8 us
    pallas_call x3, Pallas kernels, residual_of(): pl.pallas_call(functools.partial(residual_kernel, peers, first, low, keep...  16.8 us
    pallas_call x1, Pallas kernels, banded(): pl.pallas_call(band_kernel, grid=(groups // GROUPS,), in_specs=[SMEM, SME...  14.6 us
    unnamed x8, local copies, waits for them, and re-layouts  6.94 us
  transfers between devices with their start and end apart: 18, of which 8 were waited for; matrix products, arithmetic and copies ran while one was open for 4% of the time, Pallas kernels for 37%

profile of v4, /device:TPU:0, one launch (start us, length us, event | category | flops | bytes accessed | tf_op | source)
XLA Modules:
  0.0 187.1 jit_solution(1148523144855290762)
XLA Ops:
  0.6 0.1 pad_add_fusion.me_ref
  0.7 3.8 %packed.1 = (f32[24,256]{1,0:T(8,128)S(1)}, bf16[32,1408]{1,0:T(8,128)(2,1)S(1)}, bf16[32,1408]{1,0:T(8,128)(2,1)S(1)}, bf16[32,1408]{1,0:T(8,128)(2,1)S(1)}, bf...) custom-call(s32[2]{0:T(128)S(1)} %pad_add_fusion.me_ref, ...), custom_call_target="tpu_custom_call" | custom-call | bytes 8388608 | tf_op jit(solution)/shard_map/packed/pallas_call | solution.py:144
  4.5 3.1 %collective-permute-start.3 = (bf16[32,13312]{1,0:T(8,128)(2,1)}, bf16[32,13312]{1,0:T(8,128)(2,1)S(1)}, u32[]{:S(2)}, u32[]{:S(2)}) collective-permute-start(bf16[32,13312]{1,0:T(8,128)(2,1)} %get-tuple-element.23), channel_id=1, source_target_pairs={{0,4},{4,8},{8,12},{12,0},{1,5},{5,9},{9,13},{13,1},{2,6},{6,10},{... | collective-permute-start | bytes 2555912 | tf_op jit(solution)/shard_map/ppermute | solution.py:78
  7.6 2.6 %collective-permute-start.4 = (bf16[32,13312]{1,0:T(8,128)(2,1)S(1)}, bf16[32,13312]{1,0:T(8,128)(2,1)S(1)}, u32[]{:S(2)}, u32[]{:S(2)}) collective-permute-start(bf16[32,13312]{1,0:T(8,128)(2,1)S(1)} %get-tuple-element.24), channel_id=1, source_target_pairs={{0,8},{4,12},{8,0},{12,4},{1,9},{5,13},{9,1},{13,5},{2,10},{6,14},... | collective-permute-start | bytes 2555912 | tf_op jit(solution)/shard_map/ppermute | solution.py:78
  10.2 1.3 collective-permute-start.5
  11.5 0.7 collective-permute-start.9
  12.2 0.3 collective-permute-start.10
  12.5 53.7 %collective-permute-done.9 = f32[24,256]{1,0:T(8,128)S(1)} collective-permute-done((f32[24,256]{1,0:T(8,128)S(1)}, f32[24,256]{1,0:T(8,128)S(1)}, u32[]{:S(2)}, u32[]{:S(2)}) %collective-permute-start.9) | collective-permute-done | bytes 24608 | tf_op jit(solution)/shard_map/ppermute | solution.py:78
  66.3 18.9 %collective-permute-done.10 = f32[24,256]{1,0:T(8,128)S(1)} collective-permute-done((f32[24,256]{1,0:T(8,128)S(1)}, f32[24,256]{1,0:T(8,128)S(1)}, u32[]{:S(2)}, u32[]{:S(2)}) %collective-permute-start.10) | collective-permute-done | bytes 24608 | tf_op jit(solution)/shard_map/ppermute | solution.py:78
  85.2 0.0 collective-permute-start.6
  85.2 0.8 collective-permute-done.11
  86.0 3.9 %collective-permute-start.7 = (bf16[32,1408]{1,0:T(8,128)(2,1)S(1)}, bf16[32,1408]{1,0:T(8,128)(2,1)S(1)}, u32[]{:S(2)}, u32[]{:S(2)}) collective-permute-start(bf16[32,1408]{1,0:T(8,128)(2,1)S(1)} %get-tuple-element.27), channel_id=1, source_target_pairs={{0,8},{4,12},{8,0},{12,4},{1,9},{5,13},{9,1},{13,5},{2,10},{6,14},... | collective-permute-start | bytes 270344 | tf_op jit(solution)/shard_map/ppermute | solution.py:78
  89.9 2.6 %collective-permute-done.6.refs_0_.refs_3_ = bf16[32,1408]{1,0:T(8,128)(2,1)S(1)} collective-permute-done((bf16[32,1408]{1,0:T(8,128)(2,1)S(1)}, bf16[32,1408]{1,0:T(8,128)(2,1)S(1)}, u32[]{:S(2)}, u32[]{:S(2)}) %collective-permute-start.6) | collective-permute-done | bytes 90144 | tf_op jit(solution)/shard_map/ppermute | solution.py:78
  92.6 0.0 collective-permute-start.8
  92.6 2.9 %collective-permute-done.7.refs_1_.refs_4_ = bf16[32,1408]{1,0:T(8,128)(2,1)S(1)} collective-permute-done((bf16[32,1408]{1,0:T(8,128)(2,1)S(1)}, bf16[32,1408]{1,0:T(8,128)(2,1)S(1)}, u32[]{:S(2)}, u32[]{:S(2)}) %collective-permute-start.7) | collective-permute-done | bytes 90144 | tf_op jit(solution)/shard_map/ppermute | solution.py:78
  95.5 1.6 collective-permute-done.8.refs_2_.refs_5_
  97.1 1.5 collective-permute-start.13
  98.6 0.9 collective-permute-done.12.refs_1_
  99.5 0.0 collective-permute-start
  99.5 2.3 %collective-permute-done.13.refs_2_ = f32[96,256]{1,0:T(8,128)S(1)} collective-permute-done((f32[96,256]{1,0:T(8,128)S(1)}, f32[96,256]{1,0:T(8,128)S(1)}, u32[]{:S(2)}, u32[]{:S(2)}) %collective-permute-start.13) | collective-permute-done | bytes 98336 | tf_op jit(solution)/shard_map/ppermute | solution.py:530
  101.8 6.9 %copy.12 = bf16[32,8,96,128]{3,2,1,0:T(8,128)(2,1)} copy(bf16[32,8,96,128]{3,1,2,0:T(8,128)(2,1)} %bitcast.24) | data formatting | bytes 12582912
  108.7 14.6 %banded.1.refs_4_.refs_7_ = bf16[64,256,512]{2,1,0:T(8,128)(2,1)S(1)} custom-call(s32[1]{0:T(128)S(6)} %mul.7.first_ref, s32[3,256]{1,0:T(4,128)S(1)} %bitcast.16, bf16[256,96,128]{2,1,0:T(8,128)(2,1)} %bitcast.22), custom_call_target="tpu_custom_call" | custom-call | bytes 41943040 | tf_op jit(solution)/shard_map/banded/pallas_call | solution.py:381
  123.3 2.7 %shard_map.95 = (bf16[128,16384]{1,0:T(8,128)(2,1)}, f32[8,128]{1,0:T(8,128)}) custom-call(s32[2]{0:T(128)S(1)} %pad_add_fusion.me_ref, bf16[32,1408]{1,0:T(8,128)(2,1)S(1)} %collective-permute-done.6.refs_0_.refs_3_, bf16[32,1408]{1,0:T(8,128)(2,1)S(1)} %collective-permute-done.7.refs_1_.refs_4_, ...), custom_call_target="tpu_custom_call" | custom-call | flops 100663296 | bytes 1376256 | tf_op jit(solution)/shard_map/pallas_call | solution.py:468
  126.1 1.6 collective-permute-start.1
  127.7 38.6 %site_sums.1 = (f32[32,1024]{1,0:T(8,128)S(1)}, s16[32,1152]{1,0:T(8,128)(2,1)S(1)}, s16[32,1152]{1,0:T(8,128)(2,1)S(1)}, s16[32,1152]{1,0:T(8,128)(2,1)S(1)}) custom-call(s32[2]{0:T(128)S(1)} %pad_add_fusion.me_ref, bf16[32,65536]{1,0:T(8,128)(2,1)} %bitcast.19, f32[96,256]{1,0:T(8,128)S(1)} %constant_dynamic-update-slice_fusion.refs_0_, ...), custom_call_target="tpu_custom_call" | custom-call | flops 67108864 | bytes 67108864 | tf_op jit(solution)/shard_map/site_sums/pallas_call | solution.py:289
  166.3 0.8 collective-permute-start.2
  167.0 1.3 collective-permute-start.15
  168.3 1.4 collective-permute-start.16
  169.7 1.7 collective-permute-start.17
  171.5 10.7 %shard_map.96 = (bf16[128,16384]{1,0:T(8,128)(2,1)}, f32[8,128]{1,0:T(8,128)}) custom-call(s32[2]{0:T(128)S(1)} %pad_add_fusion.me_ref, bf16[32,13312]{1,0:T(8,128)(2,1)S(1)} %collective-permute-done.3.refs_0_.refs_3_, bf16[32,13312]{1,0:T(8,128)(2,1)S(1)} %collective-permute-done.4.refs_1_.refs_4_, ...), custom_call_target="tpu_custom_call", output_to_operand_aliasing={{0}: (10, {})} | custom-call | flops 1308622848 | bytes 17891328 | tf_op jit(solution)/shard_map/pallas_call | solution.py:468
  182.2 3.4 %shard_map.97 = (bf16[128,16384]{1,0:T(8,128)(2,1)}, f32[8,128]{1,0:T(8,128)S(1)}) custom-call(s32[2]{0:T(128)S(1)} %pad_add_fusion.me_ref, bf16[32,1920]{1,0:T(8,128)(2,1)S(1)} %collective-permute-done.refs_0_, bf16[32,1920]{1,0:T(8,128)(2,1)S(1)} %collective-permute-done.1.refs_1_, ...), custom_call_target="tpu_custom_call", output_to_operand_aliasing={{0}: (10, {})} | custom-call | flops 201326592 | bytes 2752512 | tf_op jit(solution)/shard_map/pallas_call | solution.py:468
  185.6 1.4 placed_rows.1
  (21 shorter events, 0.1 us)
Async XLA Ops:
  4.5 162.5 %collective-permute-start.3 = (bf16[32,13312]{1,0:T(8,128)(2,1)}, bf16[32,13312]{1,0:T(8,128)(2,1)S(1)}, u32[]{:S(2)}, u32[]{:S(2)}) collective-permute-start(bf16[32,13312]{1,0:T(8,128)(2,1)} %get-tuple-element.23), channel_id=1, source_target_pairs={{0,4},{4,8},{8,12},{12,0},{1,5},{5,9},{9,13},{13,1},{2,6},{6,10},{... | collective-permute-start | bytes 2555912 | tf_op jit(solution)/shard_map/ppermute | solution.py:78
  7.6 160.8 %collective-permute-start.4 = (bf16[32,13312]{1,0:T(8,128)(2,1)S(1)}, bf16[32,13312]{1,0:T(8,128)(2,1)S(1)}, u32[]{:S(2)}, u32[]{:S(2)}) collective-permute-start(bf16[32,13312]{1,0:T(8,128)(2,1)S(1)} %get-tuple-element.24), channel_id=1, source_target_pairs={{0,8},{4,12},{8,0},{12,4},{1,9},{5,13},{9,1},{13,5},{2,10},{6,14},... | collective-permute-start | bytes 2555912 | tf_op jit(solution)/shard_map/ppermute | solution.py:78
  10.2 159.6 %collective-permute-start.5 = (bf16[32,13312]{1,0:T(8,128)(2,1)S(1)}, bf16[32,13312]{1,0:T(8,128)(2,1)S(1)}, u32[]{:S(2)}, u32[]{:S(2)}) collective-permute-start(bf16[32,13312]{1,0:T(8,128)(2,1)S(1)} %get-tuple-element.25), channel_id=1, source_target_pairs={{0,12},{4,0},{8,4},{12,8},{1,13},{5,1},{9,5},{13,9},{2,14},{6,2},{... | collective-permute-start | bytes 2555912 | tf_op jit(solution)/shard_map/ppermute | solution.py:78
  11.5 54.7 %collective-permute-start.9 = (f32[24,256]{1,0:T(8,128)S(1)}, f32[24,256]{1,0:T(8,128)S(1)}, u32[]{:S(2)}, u32[]{:S(2)}) collective-permute-start(f32[24,256]{1,0:T(8,128)S(1)} %get-tuple-element.33), channel_id=1, source_target_pairs={{0,4},{4,8},{8,12},{12,0},{1,5},{5,9},{9,13},{13,1},{2,6},{6,10},{... | collective-permute-start | bytes 73736 | tf_op jit(solution)/shard_map/ppermute | solution.py:78
  12.2 73.0 %collective-permute-start.10 = (f32[24,256]{1,0:T(8,128)S(1)}, f32[24,256]{1,0:T(8,128)S(1)}, u32[]{:S(2)}, u32[]{:S(2)}) collective-permute-start(f32[24,256]{1,0:T(8,128)S(1)} %get-tuple-element.33), channel_id=1, source_target_pairs={{0,8},{4,12},{8,0},{12,4},{1,9},{5,13},{9,1},{13,5},{2,10},{6,14},... | collective-permute-start | bytes 73736 | tf_op jit(solution)/shard_map/ppermute | solution.py:78
  66.3 19.7 %collective-permute-start.11 = (f32[24,256]{1,0:T(8,128)S(1)}, f32[24,256]{1,0:T(8,128)S(1)}, u32[]{:S(2)}, u32[]{:S(2)}) collective-permute-start(f32[24,256]{1,0:T(8,128)S(1)} %get-tuple-element.33), channel_id=1, source_target_pairs={{0,12},{4,0},{8,4},{12,8},{1,13},{5,1},{9,5},{13,9},{2,14},{6,2},{... | collective-permute-start | bytes 73736 | tf_op jit(solution)/shard_map/ppermute | solution.py:78
  85.2 7.4 %collective-permute-start.6 = (bf16[32,1408]{1,0:T(8,128)(2,1)S(1)}, bf16[32,1408]{1,0:T(8,128)(2,1)S(1)}, u32[]{:S(2)}, u32[]{:S(2)}) collective-permute-start(bf16[32,1408]{1,0:T(8,128)(2,1)S(1)} %get-tuple-element.26), channel_id=1, source_target_pairs={{0,4},{4,8},{8,12},{12,0},{1,5},{5,9},{9,13},{13,1},{2,6},{6,10},{... | collective-permute-start | bytes 270344 | tf_op jit(solution)/shard_map/ppermute | solution.py:78
  86.0 9.5 %collective-permute-start.7 = (bf16[32,1408]{1,0:T(8,128)(2,1)S(1)}, bf16[32,1408]{1,0:T(8,128)(2,1)S(1)}, u32[]{:S(2)}, u32[]{:S(2)}) collective-permute-start(bf16[32,1408]{1,0:T(8,128)(2,1)S(1)} %get-tuple-element.27), channel_id=1, source_target_pairs={{0,8},{4,12},{8,0},{12,4},{1,9},{5,13},{9,1},{13,5},{2,10},{6,14},... | collective-permute-start | bytes 270344 | tf_op jit(solution)/shard_map/ppermute | solution.py:78
  92.6 4.5 %collective-permute-start.8 = (bf16[32,1408]{1,0:T(8,128)(2,1)S(1)}, bf16[32,1408]{1,0:T(8,128)(2,1)S(1)}, u32[]{:S(2)}, u32[]{:S(2)}) collective-permute-start(bf16[32,1408]{1,0:T(8,128)(2,1)S(1)} %get-tuple-element.28), channel_id=1, source_target_pairs={{0,12},{4,0},{8,4},{12,8},{1,13},{5,1},{9,5},{13,9},{2,14},{6,2},{... | collective-permute-start | bytes 270344 | tf_op jit(solution)/shard_map/ppermute | solution.py:78
  95.5 4.0 %collective-permute-start.12 = (f32[96,256]{1,0:T(8,128)S(1)}, f32[96,256]{1,0:T(8,128)S(1)}, u32[]{:S(2)}, u32[]{:S(2)}) collective-permute-start(f32[96,256]{1,0:T(8,128)S(1)} %constant_dynamic-update-slice_fusion.refs_0_), channel_id=1, source_target_pairs={{0,1},{1,2},{2,3},{3,0},{4,5},{5,6},{6,7},{7,4},{8,9},{9,10},{10,1... | collective-permute-start | bytes 294920 | tf_op jit(solution)/shard_map/ppermute | solution.py:530
  97.1 4.7 %collective-permute-start.13 = (f32[96,256]{1,0:T(8,128)S(1)}, f32[96,256]{1,0:T(8,128)S(1)}, u32[]{:S(2)}, u32[]{:S(2)}) collective-permute-start(f32[96,256]{1,0:T(8,128)S(1)} %constant_dynamic-update-slice_fusion.refs_0_), channel_id=1, source_target_pairs={{0,2},{1,3},{2,0},{3,1},{4,6},{5,7},{6,4},{7,5},{8,10},{9,11},{10,... | collective-permute-start | bytes 294920 | tf_op jit(solution)/shard_map/ppermute | solution.py:530
  99.5 66.7 %collective-permute-start = (bf16[32,1920]{1,0:T(8,128)(2,1)}, bf16[32,1920]{1,0:T(8,128)(2,1)S(1)}, u32[]{:S(2)}, u32[]{:S(2)}) collective-permute-start(bf16[32,1920]{1,0:T(8,128)(2,1)} %get-tuple-element.20), channel_id=1, source_target_pairs={{0,4},{4,8},{8,12},{12,0},{1,5},{5,9},{9,13},{13,1},{2,6},{6,10},{... | collective-permute-start | bytes 368648 | tf_op jit(solution)/shard_map/ppermute | solution.py:78
  101.8 24.3 %collective-permute-start.14 = (f32[96,256]{1,0:T(8,128)S(1)}, f32[96,256]{1,0:T(8,128)S(1)}, u32[]{:S(2)}, u32[]{:S(2)}) collective-permute-start(f32[96,256]{1,0:T(8,128)S(1)} %constant_dynamic-update-slice_fusion.refs_0_), channel_id=1, source_target_pairs={{0,3},{1,0},{2,1},{3,2},{4,7},{5,4},{6,5},{7,6},{8,11},{9,8},{10,9... | collective-permute-start | bytes 294920 | tf_op jit(solution)/shard_map/ppermute | solution.py:530
  101.8 6.9 %copy-start.1 = (s32[256,3]{0,1:T(4,128)S(1)}, s32[256,3]{0,1:T(4,128)}, u32[]{:S(2)}) copy-start(s32[256,3]{0,1:T(4,128)} %param.10) | copy-start | bytes 9220
  108.7 14.6 %copy-start = (f32[16384]{0:T(1024)S(1)}, f32[16384]{0:T(1024)}, u32[]{:S(2)}) copy-start(f32[16384]{0:T(1024)} %param.11) | copy-start | bytes 196612
  126.1 56.1 %collective-permute-start.1 = (bf16[32,1920]{1,0:T(8,128)(2,1)S(1)}, bf16[32,1920]{1,0:T(8,128)(2,1)S(1)}, u32[]{:S(2)}, u32[]{:S(2)}) collective-permute-start(bf16[32,1920]{1,0:T(8,128)(2,1)S(1)} %get-tuple-element.21), channel_id=1, source_target_pairs={{0,8},{4,12},{8,0},{12,4},{1,9},{5,13},{9,1},{13,5},{2,10},{6,14},... | collective-permute-start | bytes 368648 | tf_op jit(solution)/shard_map/ppermute | solution.py:78
  166.3 16.0 %collective-permute-start.2 = (bf16[32,1920]{1,0:T(8,128)(2,1)S(1)}, bf16[32,1920]{1,0:T(8,128)(2,1)S(1)}, u32[]{:S(2)}, u32[]{:S(2)}) collective-permute-start(bf16[32,1920]{1,0:T(8,128)(2,1)S(1)} %get-tuple-element.22), channel_id=1, source_target_pairs={{0,12},{4,0},{8,4},{12,8},{1,13},{5,1},{9,5},{13,9},{2,14},{6,2},{... | collective-permute-start | bytes 368648 | tf_op jit(solution)/shard_map/ppermute | solution.py:78
  167.0 18.6 %collective-permute-start.15 = (s16[32,1152]{1,0:T(8,128)(2,1)S(1)}, s16[32,1152]{1,0:T(8,128)(2,1)S(1)}, u32[]{:S(2)}, u32[]{:S(2)}) collective-permute-start(s16[32,1152]{1,0:T(8,128)(2,1)S(1)} %get-tuple-element.35), channel_id=1, source_target_pairs={{0,4},{4,8},{8,12},{12,0},{1,5},{5,9},{9,13},{13,1},{2,6},{6,10},{... | collective-permute-start | bytes 221192 | tf_op jit(solution)/shard_map/ppermute | solution.py:78
  168.3 17.3 %collective-permute-start.16 = (s16[32,1152]{1,0:T(8,128)(2,1)S(1)}, s16[32,1152]{1,0:T(8,128)(2,1)S(1)}, u32[]{:S(2)}, u32[]{:S(2)}) collective-permute-start(s16[32,1152]{1,0:T(8,128)(2,1)S(1)} %get-tuple-element.36), channel_id=1, source_target_pairs={{0,8},{4,12},{8,0},{12,4},{1,9},{5,13},{9,1},{13,5},{2,10},{6,14},... | collective-permute-start | bytes 221192 | tf_op jit(solution)/shard_map/ppermute | solution.py:78
  169.7 15.9 %collective-permute-start.17 = (s16[32,1152]{1,0:T(8,128)(2,1)S(1)}, s16[32,1152]{1,0:T(8,128)(2,1)S(1)}, u32[]{:S(2)}, u32[]{:S(2)}) collective-permute-start(s16[32,1152]{1,0:T(8,128)(2,1)S(1)} %get-tuple-element.37), channel_id=1, source_target_pairs={{0,12},{4,0},{8,4},{12,8},{1,13},{5,1},{9,5},{13,9},{2,14},{6,2},{... | collective-permute-start | bytes 221192 | tf_op jit(solution)/shard_map/ppermute | solution.py:78

commit v5 on v4

--- a/solution.py
+++ b/solution.py
@@ -87,8 +87,7 @@
     parts = len(lanes) - 1
     count = parts * (peers - 1)
     list_ref, pieces, refs = refs[0], refs[1 : 1 + count], refs[1 + count :]
-    edges, weights, owners, slots, list_sems, in_sems, out_sems = refs[:7]
-    held = refs[7:]
+    edges, weights, owners, slots, list_sems, sems = refs
     recs = list_ref.shape[1]
     share = pl.ds(pl.multiple_of(me_ref[1] * recs, recs), recs)
     small = [
@@ -99,7 +98,7 @@
     ]
     for copy in small:
         copy.start()
-    taken, put = [], []
+    taken = []
     for j in range(parts):
         for s in range(1, peers):
             target = lax.rem(me_ref[0] + s, peers)
@@ -108,11 +107,10 @@
             taken.append(
                 pltpu.make_async_copy(
                     rows_ref.at[:, pl.ds(pl.multiple_of(start, RIM), lanes[j + 1] - lanes[j])],
-                    held[n],
-                    in_sems.at[n],
+                    pieces[n],
+                    sems.at[n],
                 )
             )
-            put.append(pltpu.make_async_copy(held[n], pieces[n], out_sems.at[n]))
     for copy in taken:
         copy.start()
     for copy in small:
@@ -121,10 +119,7 @@
     list_ref[IW : 2 * IW, :] = weights[...]
     sites = (owners[...] * SDEV + slots[...]).astype(jnp.float32)
     list_ref[2 * IW :, :] = jnp.broadcast_to(sites, (LINES - 2 * IW, recs))
-    for copy, onward in zip(taken, put):
-        copy.wait()
-        onward.start()
-    for copy in put:
+    for copy in taken:
         copy.wait()
 
 
@@ -144,16 +139,14 @@
     out = pl.pallas_call(
         functools.partial(pack_kernel, peers, lanes),
         in_specs=[SMEM] + [HBM] * 5,
-        out_specs=[VMEM] + [HBM] * len(shapes),
+        out_specs=[VMEM] * (1 + len(shapes)),
         out_shape=[jax.ShapeDtypeStruct((LINES, share), jnp.float32)]
         + [jax.ShapeDtypeStruct(shape, rows.dtype) for shape in shapes],
         scratch_shapes=[pltpu.VMEM((x.shape[0], share), x.dtype) for x in small]
         + [
             pltpu.SemaphoreType.DMA((len(small),)),
             pltpu.SemaphoreType.DMA((len(shapes),)),
-            pltpu.SemaphoreType.DMA((len(shapes),)),
-        ]
-        + [pltpu.VMEM(shape, rows.dtype) for shape in shapes],
+        ],
         compiler_params=pltpu.CompilerParams(vmem_limit_bytes=8 << 20),
         cost_estimate=pl.CostEstimate(flops=0, bytes_accessed=8 << 20, transcendentals=0),
         name="packed",
@@ -161,18 +154,9 @@
     return out[0], out[1:]
 
 
-def site_kernel(peers, shares, me_ref, rows_ref, *refs):
-    list_refs, refs = refs[:shares], refs[shares:]
-    own_ref, sent_refs, refs = refs[0], refs[1:peers], refs[peers:]
-    out_ref, rows, turned, picked, pred, ints, scale, row_sems, int_sems = refs[:9]
-    refs = refs[9:]
-    edge_refs = [refs[s * (IW + 1) : (s + 1) * (IW + 1)] for s in range(peers)]
-    tables = refs[peers * (IW + 1) :]
+def turn_kernel(peers, me_ref, rows_ref, turned, rows, row_sems):
     cols = rows_ref.shape[0]
     edge_count = turned.shape[0]
-    share = list_refs[0].shape[1]
-    recs = shares * share
-    per = picked.shape[1]
     parts = row_sems.shape[0]
     width = edge_count // parts
 
@@ -187,6 +171,49 @@
     for part in range(parts):
         for s in range(peers):
             fetch(part, s).start()
+    for part in range(parts):
+        for s in range(peers):
+            fetch(part, s).wait()
+
+        def turn(t, _, part=part):
+            at = pl.multiple_of(part * width + t * LANE, LANE)
+            turned[pl.ds(at, LANE), :] = rows[:, pl.ds(at, LANE)].T.astype(jnp.float32)
+            return 0
+
+        lax.fori_loop(0, width // LANE, turn, 0, unroll=2)
+
+
+def turned_rows(me, rows, peers):
+    cols, all_edges = rows.shape
+    edge_count = all_edges // peers
+    parts = 4
+    return pl.pallas_call(
+        functools.partial(turn_kernel, peers),
+        in_specs=[SMEM, HBM],
+        out_specs=VMEM,
+        out_shape=jax.ShapeDtypeStruct((edge_count, LANE), jnp.float32),
+        scratch_shapes=[
+            pltpu.VMEM((peers * cols, edge_count), rows.dtype),
+            pltpu.SemaphoreType.DMA((parts, peers)),
+        ],
+        compiler_params=pltpu.CompilerParams(vmem_limit_bytes=14 << 20),
+        cost_estimate=pl.CostEstimate(flops=0, bytes_accessed=12 << 20, transcendentals=0),
+        name="turned_rows",
+    )(me, rows)
+
+
+def site_kernel(peers, shares, me_ref, turned, *refs):
+    list_refs, refs = refs[:shares], refs[shares:]
+    own_ref, sent_refs, refs = refs[0], refs[1:peers], refs[peers:]
+    out_ref, picked, pred, ints, scale, int_sems = refs[:6]
+    refs = refs[6:]
+    edge_refs = [refs[s * (IW + 1) : (s + 1) * (IW + 1)] for s in range(peers)]
+    tables = refs[peers * (IW + 1) :]
+    cols = own_ref.shape[0]
+    share = list_refs[0].shape[1]
+    recs = shares * share
+    per = picked.shape[1]
+
     lists = []
     for s in range(peers):
         for j, ref in enumerate(list_refs):
@@ -206,16 +233,6 @@
     for table in tables:
         table[...] = jnp.zeros_like(table)
 
-    for part in range(parts):
-        for s in range(peers):
-            fetch(part, s).wait()
-
-        def turn(t, _, part=part):
-            at = pl.multiple_of(part * width + t * LANE, LANE)
-            turned[pl.ds(at, LANE), :] = rows[:, pl.ds(at, LANE)].T.astype(jnp.float32)
-            return 0
-
-        lax.fori_loop(0, width // LANE, turn, 0, unroll=2)
     lane = lax.broadcasted_iota(jnp.int32, (1, LANE), 1) // cols
     lanes = lax.broadcasted_iota(jnp.int32, (per, LANE), 1) // cols
     for copy in lists:
@@ -278,38 +295,32 @@
         sent_refs[s - 1][:, owned:] = power.astype(jnp.int32).astype(jnp.int16)
 
 
-def site_sums(me, rows, lists, peers):
-    cols, all_edges = rows.shape
-    edge_count = all_edges // peers
+def site_sums(me, turned, cols, lists, peers):
     per = LANE
-    parts = 4
     shares = len(lists)
     recs = lists[0].shape[1] * shares
     sent = jax.ShapeDtypeStruct((cols, SDEV + LANE), jnp.int16)
     out = pl.pallas_call(
         functools.partial(site_kernel, peers, shares),
-        in_specs=[SMEM, HBM] + [VMEM] * shares,
+        in_specs=[SMEM] + [VMEM] * (1 + shares),
         out_specs=[VMEM] * peers,
         out_shape=[jax.ShapeDtypeStruct((cols, SDEV), jnp.float32)] + [sent] * (peers - 1),
         scratch_shapes=[
             pltpu.VMEM((peers, cols, SDEV), jnp.float32),
-            pltpu.VMEM((peers * cols, edge_count), rows.dtype),
-            pltpu.VMEM((edge_count, LANE), jnp.float32),
             pltpu.VMEM((IW, per, LANE), jnp.float32),
             pltpu.VMEM((per, LANE), jnp.float32),
             pltpu.VMEM((peers, IW + 8, recs), jnp.int32),
             pltpu.VMEM((LANE, recs), jnp.float32),
-            pltpu.SemaphoreType.DMA((parts, peers)),
             pltpu.SemaphoreType.DMA((peers, IW + 1)),
         ]
         + [pltpu.SMEM((1, recs), jnp.int32)] * (peers * (IW + 1))
         + [pltpu.VMEM((peers * SDEV, LANE), jnp.float32)] * peers,
-        compiler_params=pltpu.CompilerParams(vmem_limit_bytes=24 << 20),
+        compiler_params=pltpu.CompilerParams(vmem_limit_bytes=16 << 20),
         cost_estimate=pl.CostEstimate(
             flops=2 * recs * peers * IW * 8 * LANE, bytes_accessed=64 << 20, transcendentals=0
         ),
         name="site_sums",
-    )(me, rows, *lists)
+    )(me, turned, *lists)
     return out[0], out[1:]
 
 
@@ -337,23 +348,46 @@
     )(me, after, *got)
 
 
-def band_kernel(first_ref, index_ref, blocks_ref, band_ref, lines):
+def band_kernel(first_ref, index_ref, values_ref, band_ref, pick, lines):
     step = pl.program_id(0)
-    count = NNZB * BS // 2
+    rows = values_ref.shape[0]
+    deep = rows * rows
     half = lax.broadcasted_iota(jnp.int32, (1, 2 * BS), 1) // BS
+
+    @pl.when(step == 0)
+    def _():
+        line = lax.broadcasted_iota(jnp.int32, pick.shape, 0)
+        wanted = (line % (2 * rows)) // 2 * rows + line // (2 * rows)
+        same = wanted == lax.broadcasted_iota(jnp.int32, pick.shape, 1)
+        pick[...] = jnp.where(same, 1.0, 0.0).astype(pick.dtype)
+
+    odd = lax.broadcasted_iota(jnp.int32, (2 * deep, 1), 0) % 2
+    parts = lines.shape[1] // (2 * rows)
+
+    def stacked(part):
+        at = [(part * rows + j) * 2 * BS for j in range(rows)]
+        return jnp.concatenate([values_ref[:, i : i + 2 * BS] for i in at], axis=0)
+
+    for first in range(0, parts, 2):
+        pair = jnp.concatenate([stacked(first), stacked(first + 1)], axis=1)
+        picked = jnp.dot(pick[...], pair, preferred_element_type=jnp.float32)
+        for part in range(first, first + 2):
+            at = (part - first) * 2 * BS
+            both = picked[:, at : at + 2 * BS]
+            crossed = pltpu.roll(both, BS, 1)
+            twice = jnp.where(half == odd, both, crossed).astype(lines.dtype)
+            for row in range(rows):
+                lines[row, part * 2 * rows : (part + 1) * 2 * rows, :] = twice[
+                    row * 2 * rows : (row + 1) * 2 * rows
+                ]
 
     def group(trip, _):
         p = step * GROUPS + trip
         base = GROUP * p - HB + first_ref[0]
         for row in range(GROUP):
-            both = blocks_ref[trip * GROUP + row].astype(jnp.float32)
-            crossed = pltpu.roll(both, BS, 1)
-            lines[row, pl.ds(0, count, stride=2), :] = jnp.where(half == 0, both, crossed)
-            lines[row, pl.ds(1, count, stride=2), :] = jnp.where(half == 0, crossed, both)
-        for row in range(GROUP):
             offs = [index_ref[k, GROUP * p + row] - base for k in range(NNZB)]
             blocks = [
-                lines[row, k * BS : (k + 1) * BS].astype(band_ref.dtype) for k in range(NNZB)
+                lines[trip * GROUP + row, k * BS : (k + 1) * BS, :] for k in range(NNZB)
             ]
             for tile in range(REACH // (2 * BS)):
                 at = slice(tile * 2 * BS, (tile + 1) * 2 * BS)
@@ -374,30 +408,28 @@
 
 
 def banded(kblocks, blk_index, first_block):
-    count = kblocks.shape[0]
+    count, values = kblocks.shape
     groups = count // GROUP
-    lines = NNZB * BS // 2
-    blocks = pl.BlockSpec((GROUPS * GROUP, lines, 2 * BS), lambda i: (i, 0, 0))
+    rows = GROUPS * GROUP
     return pl.pallas_call(
         band_kernel,
-        grid=(groups // GROUPS,),
-        in_specs=[SMEM, SMEM, blocks],
+        grid=(count // rows,),
+        in_specs=[SMEM, SMEM, pl.BlockSpec((rows, values), lambda i: (i, 0))],
         out_specs=VMEM,
-        scratch_shapes=[pltpu.VMEM((GROUP, 2 * lines, 2 * BS), jnp.float32)],
+        scratch_shapes=[
+            pltpu.VMEM((2 * rows * rows, rows * rows), kblocks.dtype),
+            pltpu.VMEM((rows, NNZB * BS, 2 * BS), kblocks.dtype),
+        ],
         out_shape=jax.ShapeDtypeStruct((groups, GROUP * BS, REACH), jnp.bfloat16),
         compiler_params=pltpu.CompilerParams(vmem_limit_bytes=28 << 20),
         cost_estimate=pl.CostEstimate(flops=0, bytes_accessed=40 << 20, transcendentals=0),
         name="banded",
-    )(
-        first_block,
-        blk_index.T,
-        pltpu.with_memory_space_constraint(kblocks.reshape(count, lines, 2 * BS), pltpu.HBM),
-    )
-
-
-def residual_kernel(peers, first, low, keep, me_ref, *refs):
-    pieces = refs[: peers - 1]
-    refs = refs[peers - 1 :]
+    )(first_block, blk_index.T, pltpu.with_memory_space_constraint(kblocks, pltpu.HBM))
+
+
+def residual_kernel(peers, first, low, keep, parts, me_ref, *refs):
+    pieces = [refs[j * (peers - 1) : (j + 1) * (peers - 1)] for j in range(parts)]
+    refs = refs[parts * (peers - 1) :]
     if keep:
         ends, refs = refs[: peers - 1], refs[peers - 1 :]
     rows_ref, band_ref, sigma_ref = refs[:3]
@@ -426,7 +458,11 @@
             at = pl.ds(pl.multiple_of(lax.rem(me + peers - s, peers) * cols, cols), cols)
             if keep:
                 panel[at, RIM : RIM + keep] = ends[s - 1][:, ends[s - 1].shape[1] - keep :]
-            panel[at, RIM + keep : RIM + span] = pieces[s - 1][...]
+            lane = RIM + keep
+            for part in pieces:
+                width_of = part[s - 1].shape[1]
+                panel[at, lane : lane + width_of] = part[s - 1][...]
+                lane += width_of
         copy.wait()
         panel[pl.ds(pl.multiple_of(me * cols, cols), cols), RIM : RIM + span] = own[...]
 
@@ -457,16 +493,20 @@
     width = GROUPS * GROUP * BS
     sigma = sigma.reshape(1, edge_count)
     out, before = None, None
-    for first, steps, low, pieces in parts:
+    calls = [parts[:-1], parts[-1:]]
+    for call in calls:
+        first, low = call[0][0], call[0][2]
+        steps = sum(part[1] for part in call)
         keep = KEEP if low else 0
-        span = keep + pieces[0].shape[1]
-        given = list(pieces) + (list(before) if keep else []) + [rows, band, sigma]
+        span = keep + sum(part[3][0].shape[1] for part in call)
+        given = [x for part in call for x in part[3]]
+        given += (list(before) if keep else []) + [rows, band, sigma]
         specs = [VMEM] * (len(given) - 3) + [HBM, VMEM, VMEM]
         if out is not None:
             given.append(out)
             specs.append(pl.BlockSpec(memory_space=pl.ANY))
         out, token = pl.pallas_call(
-            functools.partial(residual_kernel, peers, first, low, keep),
+            functools.partial(residual_kernel, peers, first, low, keep, len(call)),
             grid_spec=pltpu.PrefetchScalarGridSpec(
                 num_scalar_prefetch=1,
                 grid=(steps,),
@@ -494,7 +534,7 @@
                 transcendentals=0,
             ),
         )(me, *given)
-        before = pieces
+        before = call[-1][3]
     return out, token
 
 
@@ -515,7 +555,7 @@
     length = edge_count + 2 * RIM
     width = GROUPS * GROUP * BS
     steps = edge_count // width
-    marks = [0, 1, steps - 2, steps]
+    marks = [0, 1, steps // 2, steps - 2, steps]
     lanes = [0] + [m * width + KEEP - RIM for m in marks[1:-1]] + [length]
 
     rows = pltpu.with_memory_space_constraint(rows, pltpu.HBM)
@@ -531,7 +571,7 @@
         for k in range(1, shares)
     ]
     band = banded(kblocks, blk_index, me[:1] * (edge_count // BS))
-    own, sent = site_sums(me, rows, lists, peers)
+    own, sent = site_sums(me, turned_rows(me, rows, peers), rows.shape[0], lists, peers)
     got = [own] + [shifted(sent[s - 1], s, peers) for s in shifts]
     residual, token = residual_of(rows, parts, band, sigma, me, peers)
     site_out = placed_rows(me, token, got, peers)

time: 188 us -> 123 us (0.65)
  waiting for transfers between devices: 83.8 us -> 13.1 us
  starting transfers between devices: 20.3 us -> 31.1 us
  local copies, waits for them, and re-layouts: 6.95 us -> 0.02 us
  Pallas kernels: 75.2 us -> 77.6 us
    ppermute x15 -> x18, waiting for transfers between devices: 80.6 us -> 13.1 us  [shifted(): lax.ppermute(x, 'edge', [(i, (i + shift) % peers) for i in range(peers)])]
    ppermute x15 -> x18, starting transfers between devices: 18.8 us -> 29.6 us  [shifted(): lax.ppermute(x, 'edge', [(i, (i + shift) % peers) for i in range(peers)])]
    pallas_call x1 -> x2, Pallas kernels: 14.6 us -> 22.5 us  [the longest x1 16 us: banded(): pl.pallas_call(band_kernel, grid=(count // rows,), in_specs=[SMEM, SMEM,...]
    unnamed x8 -> x7, local copies, waits for them, and re-layouts: 6.94 us -> 0.02 us
    ppermute x3, waiting for transfers between devices: 3.2 us -> 0.01 us  [ordered(): lax.ppermute(lists, ('tx', 'rcv'), [(i, (i + k) % shares) for i in range(...]
    pallas_call x3 -> x2, Pallas kernels: 16.8 us -> 14.7 us  [residual_of(): pl.pallas_call(functools.partial(residual_kernel, peers, first, low, keep...]
    pallas_call x1, Pallas kernels: 38.6 us -> 36.4 us  [site_sums(): pl.pallas_call(functools.partial(site_kernel, peers, shares), in_specs=[S...]
  transfers between devices with their start and end apart: 18 -> 21, of which waited for: 8 -> 2; matrix products, arithmetic and copies ran while one was open for 4% -> 0% of each run, Pallas kernels for 37% -> 60%
where the time goes in v5:
time: 123 us
  Pallas kernels  77.6 us (63%)
  starting transfers between devices  31.1 us (25%)
  waiting for transfers between devices  13.1 us (11%)
    pallas_call x1, Pallas kernels, site_sums(): pl.pallas_call(functools.partial(site_kernel, peers, shares), in_specs=[S...  36.4 us
    ppermute x18, starting transfers between devices, shifted(): lax.ppermute(x, 'edge', [(i, (i + shift) % peers) for i in range(peers)])  29.6 us
    pallas_call x1, Pallas kernels, banded(): pl.pallas_call(band_kernel, grid=(count // rows,), in_specs=[SMEM, SMEM,...  16 us
    pallas_call x2, Pallas kernels, residual_of(): pl.pallas_call(functools.partial(residual_kernel, peers, first, low, keep...  14.7 us
    ppermute x18, waiting for transfers between devices, shifted(): lax.ppermute(x, 'edge', [(i, (i + shift) % peers) for i in range(peers)])  13.1 us
    pallas_call x1, Pallas kernels, turned_rows(): pl.pallas_call(functools.partial(turn_kernel, peers), in_specs=[SMEM, HBM...  6.58 us
    pallas_call x1, Pallas kernels, packed(): pl.pallas_call(functools.partial(pack_kernel, peers, lanes), in_specs=[SM...  2.59 us
  transfers between devices with their start and end apart: 21, of which 2 were waited for; matrix products, arithmetic and copies ran while one was open for 0% of the time, Pallas kernels for 60%

profile of v5, /device:TPU:0, one launch (start us, length us, event | category | flops | bytes accessed | tf_op | source)
XLA Modules:
  0.0 122.7 jit_solution(11485300054508905091)
XLA Ops:
  0.6 0.1 pad_add_fusion.me_ref
  0.7 2.6 %packed.1 = (f32[24,256]{1,0:T(8,128)S(1)}, bf16[32,1408]{1,0:T(8,128)(2,1)S(1)}, bf16[32,1408]{1,0:T(8,128)(2,1)S(1)}, bf16[32,1408]{1,0:T(8,128)(2,1)S(1)}, bf...) custom-call(s32[2]{0:T(128)S(1)} %pad_add_fusion.me_ref, ...), custom_call_target="tpu_custom_call" | custom-call | bytes 8388608 | tf_op jit(solution)/shard_map/packed/pallas_call | solution.py:139
  3.3 3.1 %collective-permute-start.12 = (f32[24,256]{1,0:T(8,128)S(1)}, f32[24,256]{1,0:T(8,128)S(1)}, u32[]{:S(2)}, u32[]{:S(2)}) collective-permute-start(f32[24,256]{1,0:T(8,128)S(1)} %get-tuple-element.37), channel_id=1, source_target_pairs={{0,4},{4,8},{8,12},{12,0},{1,5},{5,9},{9,13},{13,1},{2,6},{6,10},{... | collective-permute-start | bytes 73736 | tf_op jit(solution)/shard_map/ppermute | solution.py:78
  6.4 2.6 %collective-permute-start.13 = (f32[24,256]{1,0:T(8,128)S(1)}, f32[24,256]{1,0:T(8,128)S(1)}, u32[]{:S(2)}, u32[]{:S(2)}) collective-permute-start(f32[24,256]{1,0:T(8,128)S(1)} %get-tuple-element.37), channel_id=1, source_target_pairs={{0,8},{4,12},{8,0},{12,4},{1,9},{5,13},{9,1},{13,5},{2,10},{6,14},... | collective-permute-start | bytes 73736 | tf_op jit(solution)/shard_map/ppermute | solution.py:78
  9.0 1.3 %collective-permute-start.14 = (f32[24,256]{1,0:T(8,128)S(1)}, f32[24,256]{1,0:T(8,128)S(1)}, u32[]{:S(2)}, u32[]{:S(2)}) collective-permute-start(f32[24,256]{1,0:T(8,128)S(1)} %get-tuple-element.37), channel_id=1, source_target_pairs={{0,12},{4,0},{8,4},{12,8},{1,13},{5,1},{9,5},{13,9},{2,14},{6,2},{... | collective-permute-start | bytes 73736 | tf_op jit(solution)/shard_map/ppermute | solution.py:78
  10.4 0.7 collective-permute-start
  11.0 0.1 collective-permute-start.3
  11.1 0.8 collective-permute-start.6
  11.9 0.0 collective-permute-done.13
  11.9 3.5 %collective-permute-start.7 = (bf16[32,1408]{1,0:T(8,128)(2,1)S(1)}, bf16[32,1408]{1,0:T(8,128)(2,1)S(1)}, u32[]{:S(2)}, u32[]{:S(2)}) collective-permute-start(bf16[32,1408]{1,0:T(8,128)(2,1)S(1)} %get-tuple-element.29), channel_id=1, source_target_pairs={{0,8},{4,12},{8,0},{12,4},{1,9},{5,13},{9,1},{13,5},{2,10},{6,14},... | collective-permute-start | bytes 270344 | tf_op jit(solution)/shard_map/ppermute | solution.py:78
  15.4 0.0 collective-permute-done.14
  15.4 2.2 %collective-permute-start.8 = (bf16[32,1408]{1,0:T(8,128)(2,1)S(1)}, bf16[32,1408]{1,0:T(8,128)(2,1)S(1)}, u32[]{:S(2)}, u32[]{:S(2)}) collective-permute-start(bf16[32,1408]{1,0:T(8,128)(2,1)S(1)} %get-tuple-element.30), channel_id=1, source_target_pairs={{0,12},{4,0},{8,4},{12,8},{1,13},{5,1},{9,5},{13,9},{2,14},{6,2},{... | collective-permute-start | bytes 270344 | tf_op jit(solution)/shard_map/ppermute | solution.py:78
  17.7 11.1 %collective-permute-done.6.refs_0_ = bf16[32,1408]{1,0:T(8,128)(2,1)S(1)} collective-permute-done((bf16[32,1408]{1,0:T(8,128)(2,1)S(1)}, bf16[32,1408]{1,0:T(8,128)(2,1)S(1)}, u32[]{:S(2)}, u32[]{:S(2)}) %collective-permute-start.6) | collective-permute-done | bytes 90144 | tf_op jit(solution)/shard_map/ppermute | solution.py:78
  28.8 2.0 %collective-permute-done.7.refs_1_ = bf16[32,1408]{1,0:T(8,128)(2,1)S(1)} collective-permute-done((bf16[32,1408]{1,0:T(8,128)(2,1)S(1)}, bf16[32,1408]{1,0:T(8,128)(2,1)S(1)}, u32[]{:S(2)}, u32[]{:S(2)}) %collective-permute-start.7) | collective-permute-done | bytes 90144 | tf_op jit(solution)/shard_map/ppermute | solution.py:78
  30.7 1.5 %collective-permute-start.16 = (f32[96,256]{1,0:T(8,128)S(1)}, f32[96,256]{1,0:T(8,128)S(1)}, u32[]{:S(2)}, u32[]{:S(2)}) collective-permute-start(f32[96,256]{1,0:T(8,128)S(1)} %constant_dynamic-update-slice_fusion.refs_0_), channel_id=1, source_target_pairs={{0,2},{1,3},{2,0},{3,1},{4,6},{5,7},{6,4},{7,5},{8,10},{9,11},{10,... | collective-permute-start | bytes 294920 | tf_op jit(solution)/shard_map/ppermute | solution.py:570
  32.2 2.0 %collective-permute-start.9 = (bf16[32,7168]{1,0:T(8,128)(2,1)S(1)}, bf16[32,7168]{1,0:T(8,128)(2,1)S(1)}, u32[]{:S(2)}, u32[]{:S(2)}) collective-permute-start(bf16[32,7168]{1,0:T(8,128)(2,1)S(1)} %get-tuple-element.31), channel_id=1, source_target_pairs={{0,4},{4,8},{8,12},{12,0},{1,5},{5,9},{9,13},{13,1},{2,6},{6,10},{... | collective-permute-start | bytes 1376264 | tf_op jit(solution)/shard_map/ppermute | solution.py:78
  34.3 1.4 %collective-permute-start.10 = (bf16[32,7168]{1,0:T(8,128)(2,1)S(1)}, bf16[32,7168]{1,0:T(8,128)(2,1)S(1)}, u32[]{:S(2)}, u32[]{:S(2)}) collective-permute-start(bf16[32,7168]{1,0:T(8,128)(2,1)S(1)} %get-tuple-element.32), channel_id=1, source_target_pairs={{0,8},{4,12},{8,0},{12,4},{1,9},{5,13},{9,1},{13,5},{2,10},{6,14},... | collective-permute-start | bytes 1376264 | tf_op jit(solution)/shard_map/ppermute | solution.py:78
  35.7 2.0 %collective-permute-start.11 = (bf16[32,7168]{1,0:T(8,128)(2,1)S(1)}, bf16[32,7168]{1,0:T(8,128)(2,1)S(1)}, u32[]{:S(2)}, u32[]{:S(2)}) collective-permute-start(bf16[32,7168]{1,0:T(8,128)(2,1)S(1)} %get-tuple-element.33), channel_id=1, source_target_pairs={{0,12},{4,0},{8,4},{12,8},{1,13},{5,1},{9,5},{13,9},{2,14},{6,2},{... | collective-permute-start | bytes 1376264 | tf_op jit(solution)/shard_map/ppermute | solution.py:78
  37.7 0.5 collective-permute-start.4
  38.2 1.9 %collective-permute-start.5 = (bf16[32,6144]{1,0:T(8,128)(2,1)S(1)}, bf16[32,6144]{1,0:T(8,128)(2,1)S(1)}, u32[]{:S(2)}, u32[]{:S(2)}) collective-permute-start(bf16[32,6144]{1,0:T(8,128)(2,1)S(1)} %get-tuple-element.27), channel_id=1, source_target_pairs={{0,12},{4,0},{8,4},{12,8},{1,13},{5,1},{9,5},{13,9},{2,14},{6,2},{... | collective-permute-start | bytes 1179656 | tf_op jit(solution)/shard_map/ppermute | solution.py:78
  40.1 6.6 %turned_rows.1.turned = f32[16384,128]{1,0:T(8,128)S(1)} custom-call(s32[2]{0:T(128)S(1)} %pad_add_fusion.me_ref, bf16[32,65536]{1,0:T(8,128)(2,1)} %bitcast.15), custom_call_target="tpu_custom_call" | custom-call | bytes 12582912 | tf_op jit(solution)/shard_map/turned_rows/pallas_call | solution.py:190
  46.7 16.0 %banded.1.refs_10_.refs_7_ = bf16[64,256,512]{2,1,0:T(8,128)(2,1)S(1)} custom-call(s32[1]{0:T(128)S(6)} %mul.7.first_ref, s32[3,256]{1,0:T(4,128)S(1)} %bitcast.13, bf16[256,12288]{1,0:T(8,128)(2,1)} %values_ref.1), custom_call_target="tpu_custom_call" | custom-call | bytes 41943040 | tf_op jit(solution)/shard_map/banded/pallas_call | solution.py:414
  62.7 0.0 copy-start
  62.7 36.4 %site_sums.1 = (f32[32,1024]{1,0:T(8,128)S(1)}, s16[32,1152]{1,0:T(8,128)(2,1)S(1)}, s16[32,1152]{1,0:T(8,128)(2,1)S(1)}, s16[32,1152]{1,0:T(8,128)(2,1)S(1)}) custom-call(s32[2]{0:T(128)S(1)} %pad_add_fusion.me_ref, f32[16384,128]{1,0:T(8,128)S(1)} %turned_rows.1.turned, f32[96,256]{1,0:T(8,128)S(1)} %constant_dynamic-update-slice_fusion.refs_0_, ...), custom_call_target="tpu_custom_call" | custom-call | flops 67108864 | bytes 67108864 | tf_op jit(solution)/shard_map/site_sums/pallas_call | solution.py:303
  99.1 0.6 collective-permute-start.1
  99.7 1.9 %collective-permute-start.2 = (bf16[32,1920]{1,0:T(8,128)(2,1)S(1)}, bf16[32,1920]{1,0:T(8,128)(2,1)S(1)}, u32[]{:S(2)}, u32[]{:S(2)}) collective-permute-start(bf16[32,1920]{1,0:T(8,128)(2,1)S(1)} %get-tuple-element.24), channel_id=1, source_target_pairs={{0,12},{4,0},{8,4},{12,8},{1,13},{5,1},{9,5},{13,9},{2,14},{6,2},{... | collective-permute-start | bytes 368648 | tf_op jit(solution)/shard_map/ppermute | solution.py:78
  101.6 0.6 collective-permute-start.18
  102.1 2.0 %collective-permute-start.19 = (s16[32,1152]{1,0:T(8,128)(2,1)S(1)}, s16[32,1152]{1,0:T(8,128)(2,1)S(1)}, u32[]{:S(2)}, u32[]{:S(2)}) collective-permute-start(s16[32,1152]{1,0:T(8,128)(2,1)S(1)} %get-tuple-element.40), channel_id=1, source_target_pairs={{0,8},{4,12},{8,0},{12,4},{1,9},{5,13},{9,1},{13,5},{2,10},{6,14},... | collective-permute-start | bytes 221192 | tf_op jit(solution)/shard_map/ppermute | solution.py:78
  104.1 2.4 %collective-permute-start.20 = (s16[32,1152]{1,0:T(8,128)(2,1)S(1)}, s16[32,1152]{1,0:T(8,128)(2,1)S(1)}, u32[]{:S(2)}, u32[]{:S(2)}) collective-permute-start(s16[32,1152]{1,0:T(8,128)(2,1)S(1)} %get-tuple-element.41), channel_id=1, source_target_pairs={{0,12},{4,0},{8,4},{12,8},{1,13},{5,1},{9,5},{13,9},{2,14},{6,2},{... | collective-permute-start | bytes 221192 | tf_op jit(solution)/shard_map/ppermute | solution.py:78
  106.5 11.3 %shard_map.95 = (bf16[128,16384]{1,0:T(8,128)(2,1)}, f32[8,128]{1,0:T(8,128)}) custom-call(s32[2]{0:T(128)S(1)} %pad_add_fusion.me_ref, bf16[32,1408]{1,0:T(8,128)(2,1)S(1)} %collective-permute-done.6.refs_0_, bf16[32,1408]{1,0:T(8,128)(2,1)S(1)} %collective-permute-done.7.refs_1_, bf16[32,1408]{1,0:T(8,128)(2,1)S(1)} %collective-permute-done.8.refs_2_, ...), custom_call_target="tpu_custom_call" | custom-call | flops 1409286144 | bytes 19267584 | tf_op jit(solution)/shard_map/pallas_call | solution.py:508
  117.8 3.4 %shard_map.96 = (bf16[128,16384]{1,0:T(8,128)(2,1)}, f32[8,128]{1,0:T(8,128)S(1)}) custom-call(s32[2]{0:T(128)S(1)} %pad_add_fusion.me_ref, bf16[32,1920]{1,0:T(8,128)(2,1)S(1)} %collective-permute-done.refs_0_, bf16[32,1920]{1,0:T(8,128)(2,1)S(1)} %collective-permute-done.1.refs_1_, ...), custom_call_target="tpu_custom_call", output_to_operand_aliasing={{0}: (10, {})} | custom-call | flops 201326592 | bytes 2752512 | tf_op jit(solution)/shard_map/pallas_call | solution.py:508
  121.3 1.4 %placed_rows.1 = f32[128,1024]{1,0:T(8,128)} custom-call(s32[2]{0:T(128)S(1)} %pad_add_fusion.me_ref, f32[8,128]{1,0:T(8,128)S(1)} %get-tuple-element.36._, f32[32,1024]{1,0:T(8,128)S(1)} %get-tuple-element.38.refs_0_, s16[32,1152]{1,0:T(8,128)(2,1)S(1)} %collective-permute-done.18.refs_1_, s16[32,1152]{1,0:T(8,128)(2,1)S(1)} %collective-permute-done.19.refs_2_, ...), custom_call_target="tpu_custom_call" | custom-call | tf_op jit(solution)/shard_map/placed_rows/pallas_call | solution.py:341
  (26 shorter events, 0.1 us)
Async XLA Ops:
  3.3 7.8 %collective-permute-start.12 = (f32[24,256]{1,0:T(8,128)S(1)}, f32[24,256]{1,0:T(8,128)S(1)}, u32[]{:S(2)}, u32[]{:S(2)}) collective-permute-start(f32[24,256]{1,0:T(8,128)S(1)} %get-tuple-element.37), channel_id=1, source_target_pairs={{0,4},{4,8},{8,12},{12,0},{1,5},{5,9},{9,13},{13,1},{2,6},{6,10},{... | collective-permute-start | bytes 73736 | tf_op jit(solution)/shard_map/ppermute | solution.py:78
  6.4 5.5 %collective-permute-start.13 = (f32[24,256]{1,0:T(8,128)S(1)}, f32[24,256]{1,0:T(8,128)S(1)}, u32[]{:S(2)}, u32[]{:S(2)}) collective-permute-start(f32[24,256]{1,0:T(8,128)S(1)} %get-tuple-element.37), channel_id=1, source_target_pairs={{0,8},{4,12},{8,0},{12,4},{1,9},{5,13},{9,1},{13,5},{2,10},{6,14},... | collective-permute-start | bytes 73736 | tf_op jit(solution)/shard_map/ppermute | solution.py:78
  9.0 6.4 %collective-permute-start.14 = (f32[24,256]{1,0:T(8,128)S(1)}, f32[24,256]{1,0:T(8,128)S(1)}, u32[]{:S(2)}, u32[]{:S(2)}) collective-permute-start(f32[24,256]{1,0:T(8,128)S(1)} %get-tuple-element.37), channel_id=1, source_target_pairs={{0,12},{4,0},{8,4},{12,8},{1,13},{5,1},{9,5},{13,9},{2,14},{6,2},{... | collective-permute-start | bytes 73736 | tf_op jit(solution)/shard_map/ppermute | solution.py:78
  10.4 21.9 %collective-permute-start = (bf16[32,1920]{1,0:T(8,128)(2,1)S(1)}, bf16[32,1920]{1,0:T(8,128)(2,1)S(1)}, u32[]{:S(2)}, u32[]{:S(2)}) collective-permute-start(bf16[32,1920]{1,0:T(8,128)(2,1)S(1)} %get-tuple-element.22), channel_id=1, source_target_pairs={{0,4},{4,8},{8,12},{12,0},{1,5},{5,9},{9,13},{13,1},{2,6},{6,10},{... | collective-permute-start | bytes 368648 | tf_op jit(solution)/shard_map/ppermute | solution.py:78
  11.0 27.1 %collective-permute-start.3 = (bf16[32,6144]{1,0:T(8,128)(2,1)S(1)}, bf16[32,6144]{1,0:T(8,128)(2,1)S(1)}, u32[]{:S(2)}, u32[]{:S(2)}) collective-permute-start(bf16[32,6144]{1,0:T(8,128)(2,1)S(1)} %get-tuple-element.25), channel_id=1, source_target_pairs={{0,4},{4,8},{8,12},{12,0},{1,5},{5,9},{9,13},{13,1},{2,6},{6,10},{... | collective-permute-start | bytes 1179656 | tf_op jit(solution)/shard_map/ppermute | solution.py:78
  11.1 17.6 %collective-permute-start.6 = (bf16[32,1408]{1,0:T(8,128)(2,1)S(1)}, bf16[32,1408]{1,0:T(8,128)(2,1)S(1)}, u32[]{:S(2)}, u32[]{:S(2)}) collective-permute-start(bf16[32,1408]{1,0:T(8,128)(2,1)S(1)} %get-tuple-element.28), channel_id=1, source_target_pairs={{0,4},{4,8},{8,12},{12,0},{1,5},{5,9},{9,13},{13,1},{2,6},{6,10},{... | collective-permute-start | bytes 270344 | tf_op jit(solution)/shard_map/ppermute | solution.py:78
  11.9 18.8 %collective-permute-start.7 = (bf16[32,1408]{1,0:T(8,128)(2,1)S(1)}, bf16[32,1408]{1,0:T(8,128)(2,1)S(1)}, u32[]{:S(2)}, u32[]{:S(2)}) collective-permute-start(bf16[32,1408]{1,0:T(8,128)(2,1)S(1)} %get-tuple-element.29), channel_id=1, source_target_pairs={{0,8},{4,12},{8,0},{12,4},{1,9},{5,13},{9,1},{13,5},{2,10},{6,14},... | collective-permute-start | bytes 270344 | tf_op jit(solution)/shard_map/ppermute | solution.py:78
  15.4 16.8 %collective-permute-start.8 = (bf16[32,1408]{1,0:T(8,128)(2,1)S(1)}, bf16[32,1408]{1,0:T(8,128)(2,1)S(1)}, u32[]{:S(2)}, u32[]{:S(2)}) collective-permute-start(bf16[32,1408]{1,0:T(8,128)(2,1)S(1)} %get-tuple-element.30), channel_id=1, source_target_pairs={{0,12},{4,0},{8,4},{12,8},{1,13},{5,1},{9,5},{13,9},{2,14},{6,2},{... | collective-permute-start | bytes 270344 | tf_op jit(solution)/shard_map/ppermute | solution.py:78
  28.8 5.5 %collective-permute-start.15 = (f32[96,256]{1,0:T(8,128)S(1)}, f32[96,256]{1,0:T(8,128)S(1)}, u32[]{:S(2)}, u32[]{:S(2)}) collective-permute-start(f32[96,256]{1,0:T(8,128)S(1)} %constant_dynamic-update-slice_fusion.refs_0_), channel_id=1, source_target_pairs={{0,1},{1,2},{2,3},{3,0},{4,5},{5,6},{6,7},{7,4},{8,9},{9,10},{10,1... | collective-permute-start | bytes 294920 | tf_op jit(solution)/shard_map/ppermute | solution.py:570
  30.7 5.0 %collective-permute-start.16 = (f32[96,256]{1,0:T(8,128)S(1)}, f32[96,256]{1,0:T(8,128)S(1)}, u32[]{:S(2)}, u32[]{:S(2)}) collective-permute-start(f32[96,256]{1,0:T(8,128)S(1)} %constant_dynamic-update-slice_fusion.refs_0_), channel_id=1, source_target_pairs={{0,2},{1,3},{2,0},{3,1},{4,6},{5,7},{6,4},{7,5},{8,10},{9,11},{10,... | collective-permute-start | bytes 294920 | tf_op jit(solution)/shard_map/ppermute | solution.py:570
  32.2 5.4 %collective-permute-start.17 = (f32[96,256]{1,0:T(8,128)S(1)}, f32[96,256]{1,0:T(8,128)S(1)}, u32[]{:S(2)}, u32[]{:S(2)}) collective-permute-start(f32[96,256]{1,0:T(8,128)S(1)} %constant_dynamic-update-slice_fusion.refs_0_), channel_id=1, source_target_pairs={{0,3},{1,0},{2,1},{3,2},{4,7},{5,4},{6,5},{7,6},{8,11},{9,8},{10,9... | collective-permute-start | bytes 294920 | tf_op jit(solution)/shard_map/ppermute | solution.py:570
  32.2 69.4 %collective-permute-start.9 = (bf16[32,7168]{1,0:T(8,128)(2,1)S(1)}, bf16[32,7168]{1,0:T(8,128)(2,1)S(1)}, u32[]{:S(2)}, u32[]{:S(2)}) collective-permute-start(bf16[32,7168]{1,0:T(8,128)(2,1)S(1)} %get-tuple-element.31), channel_id=1, source_target_pairs={{0,4},{4,8},{8,12},{12,0},{1,5},{5,9},{9,13},{13,1},{2,6},{6,10},{... | collective-permute-start | bytes 1376264 | tf_op jit(solution)/shard_map/ppermute | solution.py:78
  34.3 67.9 %collective-permute-start.10 = (bf16[32,7168]{1,0:T(8,128)(2,1)S(1)}, bf16[32,7168]{1,0:T(8,128)(2,1)S(1)}, u32[]{:S(2)}, u32[]{:S(2)}) collective-permute-start(bf16[32,7168]{1,0:T(8,128)(2,1)S(1)} %get-tuple-element.32), channel_id=1, source_target_pairs={{0,8},{4,12},{8,0},{12,4},{1,9},{5,13},{9,1},{13,5},{2,10},{6,14},... | collective-permute-start | bytes 1376264 | tf_op jit(solution)/shard_map/ppermute | solution.py:78
  35.7 68.4 %collective-permute-start.11 = (bf16[32,7168]{1,0:T(8,128)(2,1)S(1)}, bf16[32,7168]{1,0:T(8,128)(2,1)S(1)}, u32[]{:S(2)}, u32[]{:S(2)}) collective-permute-start(bf16[32,7168]{1,0:T(8,128)(2,1)S(1)} %get-tuple-element.33), channel_id=1, source_target_pairs={{0,12},{4,0},{8,4},{12,8},{1,13},{5,1},{9,5},{13,9},{2,14},{6,2},{... | collective-permute-start | bytes 1376264 | tf_op jit(solution)/shard_map/ppermute | solution.py:78
  37.7 61.4 %collective-permute-start.4 = (bf16[32,6144]{1,0:T(8,128)(2,1)S(1)}, bf16[32,6144]{1,0:T(8,128)(2,1)S(1)}, u32[]{:S(2)}, u32[]{:S(2)}) collective-permute-start(bf16[32,6144]{1,0:T(8,128)(2,1)S(1)} %get-tuple-element.26), channel_id=1, source_target_pairs={{0,8},{4,12},{8,0},{12,4},{1,9},{5,13},{9,1},{13,5},{2,10},{6,14},... | collective-permute-start | bytes 1179656 | tf_op jit(solution)/shard_map/ppermute | solution.py:78
  38.2 8.5 %copy-start.1 = (s32[256,3]{0,1:T(4,128)S(1)}, s32[256,3]{0,1:T(4,128)}, u32[]{:S(2)}) copy-start(s32[256,3]{0,1:T(4,128)} %param.10) | copy-start | bytes 9220
  38.2 61.6 %collective-permute-start.5 = (bf16[32,6144]{1,0:T(8,128)(2,1)S(1)}, bf16[32,6144]{1,0:T(8,128)(2,1)S(1)}, u32[]{:S(2)}, u32[]{:S(2)}) collective-permute-start(bf16[32,6144]{1,0:T(8,128)(2,1)S(1)} %get-tuple-element.27), channel_id=1, source_target_pairs={{0,12},{4,0},{8,4},{12,8},{1,13},{5,1},{9,5},{13,9},{2,14},{6,2},{... | collective-permute-start | bytes 1179656 | tf_op jit(solution)/shard_map/ppermute | solution.py:78
  62.7 43.9 %copy-start = (f32[16384]{0:T(1024)S(1)}, f32[16384]{0:T(1024)}, u32[]{:S(2)}) copy-start(f32[16384]{0:T(1024)} %param.11) | copy-start | bytes 196612
  99.1 18.8 %collective-permute-start.1 = (bf16[32,1920]{1,0:T(8,128)(2,1)S(1)}, bf16[32,1920]{1,0:T(8,128)(2,1)S(1)}, u32[]{:S(2)}, u32[]{:S(2)}) collective-permute-start(bf16[32,1920]{1,0:T(8,128)(2,1)S(1)} %get-tuple-element.23), channel_id=1, source_target_pairs={{0,8},{4,12},{8,0},{12,4},{1,9},{5,13},{9,1},{13,5},{2,10},{6,14},... | collective-permute-start | bytes 368648 | tf_op jit(solution)/shard_map/ppermute | solution.py:78
  99.7 18.1 %collective-permute-start.2 = (bf16[32,1920]{1,0:T(8,128)(2,1)S(1)}, bf16[32,1920]{1,0:T(8,128)(2,1)S(1)}, u32[]{:S(2)}, u32[]{:S(2)}) collective-permute-start(bf16[32,1920]{1,0:T(8,128)(2,1)S(1)} %get-tuple-element.24), channel_id=1, source_target_pairs={{0,12},{4,0},{8,4},{12,8},{1,13},{5,1},{9,5},{13,9},{2,14},{6,2},{... | collective-permute-start | bytes 368648 | tf_op jit(solution)/shard_map/ppermute | solution.py:78
  101.6 19.6 %collective-permute-start.18 = (s16[32,1152]{1,0:T(8,128)(2,1)S(1)}, s16[32,1152]{1,0:T(8,128)(2,1)S(1)}, u32[]{:S(2)}, u32[]{:S(2)}) collective-permute-start(s16[32,1152]{1,0:T(8,128)(2,1)S(1)} %get-tuple-element.39), channel_id=1, source_target_pairs={{0,4},{4,8},{8,12},{12,0},{1,5},{5,9},{9,13},{13,1},{2,6},{6,10},{... | collective-permute-start | bytes 221192 | tf_op jit(solution)/shard_map/ppermute | solution.py:78
  102.1 19.1 %collective-permute-start.19 = (s16[32,1152]{1,0:T(8,128)(2,1)S(1)}, s16[32,1152]{1,0:T(8,128)(2,1)S(1)}, u32[]{:S(2)}, u32[]{:S(2)}) collective-permute-start(s16[32,1152]{1,0:T(8,128)(2,1)S(1)} %get-tuple-element.40), channel_id=1, source_target_pairs={{0,8},{4,12},{8,0},{12,4},{1,9},{5,13},{9,1},{13,5},{2,10},{6,14},... | collective-permute-start | bytes 221192 | tf_op jit(solution)/shard_map/ppermute | solution.py:78
  104.1 17.1 %collective-permute-start.20 = (s16[32,1152]{1,0:T(8,128)(2,1)S(1)}, s16[32,1152]{1,0:T(8,128)(2,1)S(1)}, u32[]{:S(2)}, u32[]{:S(2)}) collective-permute-start(s16[32,1152]{1,0:T(8,128)(2,1)S(1)} %get-tuple-element.41), channel_id=1, source_target_pairs={{0,12},{4,0},{8,4},{12,8},{1,13},{5,1},{9,5},{13,9},{2,14},{6,2},{... | collective-permute-start | bytes 221192 | tf_op jit(solution)/shard_map/ppermute | solution.py:78

commit v6 on v5

--- a/solution.py
+++ b/solution.py
@@ -154,8 +154,17 @@
     return out[0], out[1:]
 
 
-def turn_kernel(peers, me_ref, rows_ref, turned, rows, row_sems):
-    cols = rows_ref.shape[0]
+def site_kernel(peers, shares, me_ref, rows_ref, *refs):
+    list_refs, refs = refs[:shares], refs[shares:]
+    own_ref, sent_refs, refs = refs[0], refs[1:peers], refs[peers:]
+    out_ref, rows, turned, picked, pred, ints, scale, row_sems, int_sems = refs[:9]
+    refs = refs[9:]
+    edge_refs = [refs[s * (IW + 1) : (s + 1) * (IW + 1)] for s in range(peers)]
+    tables = refs[peers * (IW + 1) :]
+    cols = own_ref.shape[0]
+    share = list_refs[0].shape[1]
+    recs = shares * share
+    per = picked.shape[1]
     edge_count = turned.shape[0]
     parts = row_sems.shape[0]
     width = edge_count // parts
@@ -171,49 +180,6 @@
     for part in range(parts):
         for s in range(peers):
             fetch(part, s).start()
-    for part in range(parts):
-        for s in range(peers):
-            fetch(part, s).wait()
-
-        def turn(t, _, part=part):
-            at = pl.multiple_of(part * width + t * LANE, LANE)
-            turned[pl.ds(at, LANE), :] = rows[:, pl.ds(at, LANE)].T.astype(jnp.float32)
-            return 0
-
-        lax.fori_loop(0, width // LANE, turn, 0, unroll=2)
-
-
-def turned_rows(me, rows, peers):
-    cols, all_edges = rows.shape
-    edge_count = all_edges // peers
-    parts = 4
-    return pl.pallas_call(
-        functools.partial(turn_kernel, peers),
-        in_specs=[SMEM, HBM],
-        out_specs=VMEM,
-        out_shape=jax.ShapeDtypeStruct((edge_count, LANE), jnp.float32),
-        scratch_shapes=[
-            pltpu.VMEM((peers * cols, edge_count), rows.dtype),
-            pltpu.SemaphoreType.DMA((parts, peers)),
-        ],
-        compiler_params=pltpu.CompilerParams(vmem_limit_bytes=14 << 20),
-        cost_estimate=pl.CostEstimate(flops=0, bytes_accessed=12 << 20, transcendentals=0),
-        name="turned_rows",
-    )(me, rows)
-
-
-def site_kernel(peers, shares, me_ref, turned, *refs):
-    list_refs, refs = refs[:shares], refs[shares:]
-    own_ref, sent_refs, refs = refs[0], refs[1:peers], refs[peers:]
-    out_ref, picked, pred, ints, scale, int_sems = refs[:6]
-    refs = refs[6:]
-    edge_refs = [refs[s * (IW + 1) : (s + 1) * (IW + 1)] for s in range(peers)]
-    tables = refs[peers * (IW + 1) :]
-    cols = own_ref.shape[0]
-    share = list_refs[0].shape[1]
-    recs = shares * share
-    per = picked.shape[1]
-
     lists = []
     for s in range(peers):
         for j, ref in enumerate(list_refs):
@@ -233,6 +199,16 @@
     for table in tables:
         table[...] = jnp.zeros_like(table)
 
+    for part in range(parts):
+        for s in range(peers):
+            fetch(part, s).wait()
+
+        def turn(t, _, part=part):
+            at = pl.multiple_of(part * width + t * LANE, LANE)
+            turned[pl.ds(at, LANE), :] = rows[:, pl.ds(at, LANE)].T.astype(jnp.float32)
+            return 0
+
+        lax.fori_loop(0, width // LANE, turn, 0, unroll=2)
     lane = lax.broadcasted_iota(jnp.int32, (1, LANE), 1) // cols
     lanes = lax.broadcasted_iota(jnp.int32, (per, LANE), 1) // cols
     for copy in lists:
@@ -295,32 +271,38 @@
         sent_refs[s - 1][:, owned:] = power.astype(jnp.int32).astype(jnp.int16)
 
 
-def site_sums(me, turned, cols, lists, peers):
+def site_sums(me, rows, lists, peers):
+    cols, all_edges = rows.shape
+    edge_count = all_edges // peers
     per = LANE
+    parts = 4
     shares = len(lists)
     recs = lists[0].shape[1] * shares
     sent = jax.ShapeDtypeStruct((cols, SDEV + LANE), jnp.int16)
     out = pl.pallas_call(
         functools.partial(site_kernel, peers, shares),
-        in_specs=[SMEM] + [VMEM] * (1 + shares),
+        in_specs=[SMEM, HBM] + [VMEM] * shares,
         out_specs=[VMEM] * peers,
         out_shape=[jax.ShapeDtypeStruct((cols, SDEV), jnp.float32)] + [sent] * (peers - 1),
         scratch_shapes=[
             pltpu.VMEM((peers, cols, SDEV), jnp.float32),
+            pltpu.VMEM((peers * cols, edge_count), rows.dtype),
+            pltpu.VMEM((edge_count, LANE), jnp.float32),
             pltpu.VMEM((IW, per, LANE), jnp.float32),
             pltpu.VMEM((per, LANE), jnp.float32),
             pltpu.VMEM((peers, IW + 8, recs), jnp.int32),
             pltpu.VMEM((LANE, recs), jnp.float32),
+            pltpu.SemaphoreType.DMA((parts, peers)),
             pltpu.SemaphoreType.DMA((peers, IW + 1)),
         ]
         + [pltpu.SMEM((1, recs), jnp.int32)] * (peers * (IW + 1))
         + [pltpu.VMEM((peers * SDEV, LANE), jnp.float32)] * peers,
-        compiler_params=pltpu.CompilerParams(vmem_limit_bytes=16 << 20),
+        compiler_params=pltpu.CompilerParams(vmem_limit_bytes=24 << 20),
         cost_estimate=pl.CostEstimate(
             flops=2 * recs * peers * IW * 8 * LANE, bytes_accessed=64 << 20, transcendentals=0
         ),
         name="site_sums",
-    )(me, turned, *lists)
+    )(me, rows, *lists)
     return out[0], out[1:]
 
 
@@ -493,7 +475,7 @@
     width = GROUPS * GROUP * BS
     sigma = sigma.reshape(1, edge_count)
     out, before = None, None
-    calls = [parts[:-1], parts[-1:]]
+    calls = [parts[:3], parts[3:]]
     for call in calls:
         first, low = call[0][0], call[0][2]
         steps = sum(part[1] for part in call)
@@ -554,8 +536,7 @@
 
     length = edge_count + 2 * RIM
     width = GROUPS * GROUP * BS
-    steps = edge_count // width
-    marks = [0, 1, steps // 2, steps - 2, steps]
+    marks = [0, 1, 7, 12, 16]
     lanes = [0] + [m * width + KEEP - RIM for m in marks[1:-1]] + [length]
 
     rows = pltpu.with_memory_space_constraint(rows, pltpu.HBM)
@@ -571,7 +552,7 @@
         for k in range(1, shares)
     ]
     band = banded(kblocks, blk_index, me[:1] * (edge_count // BS))
-    own, sent = site_sums(me, turned_rows(me, rows, peers), rows.shape[0], lists, peers)
+    own, sent = site_sums(me, rows, lists, peers)
     got = [own] + [shifted(sent[s - 1], s, peers) for s in shifts]
     residual, token = residual_of(rows, parts, band, sigma, me, peers)
     site_out = placed_rows(me, token, got, peers)

time: 123 us -> 152 us (1.24)
  waiting for transfers between devices: 13.1 us -> 34.8 us
  starting transfers between devices: 31.1 us -> 43.1 us
  Pallas kernels: 77.6 us -> 73.2 us
    ppermute x18, waiting for transfers between devices: 13.1 us -> 34.2 us  [shifted(): lax.ppermute(x, 'edge', [(i, (i + shift) % peers) for i in range(peers)])]
    ppermute x18, starting transfers between devices: 29.6 us -> 41.6 us  [shifted(): lax.ppermute(x, 'edge', [(i, (i + shift) % peers) for i in range(peers)])]
    pallas_call x1 -> x0, Pallas kernels: 6.58 us -> none  [turned_rows(): pl.pallas_call(functools.partial(turn_kernel, peers), in_specs=[SMEM, HBM...]
    pallas_call x1, Pallas kernels: 36.4 us -> 38.6 us  [site_sums(): pl.pallas_call(functools.partial(site_kernel, peers, shares), in_specs=[S...]
  transfers between devices with their start and end apart: 21 -> 21, of which waited for: 2 -> 5; matrix products, arithmetic and copies ran while one was open for 0% -> 0% of each run, Pallas kernels for 60% -> 46%
where the time goes in v6:
time: 152 us
  Pallas kernels  73.2 us (48%)
  starting transfers between devices  43.1 us (28%)
  waiting for transfers between devices  34.8 us (23%)
    ppermute x18, starting transfers between devices, shifted(): lax.ppermute(x, 'edge', [(i, (i + shift) % peers) for i in range(peers)])  41.6 us
    pallas_call x1, Pallas kernels, site_sums(): pl.pallas_call(functools.partial(site_kernel, peers, shares), in_specs=[S...  38.6 us
    ppermute x18, waiting for transfers between devices, shifted(): lax.ppermute(x, 'edge', [(i, (i + shift) % peers) for i in range(peers)])  34.2 us
    pallas_call x1, Pallas kernels, banded(): pl.pallas_call(band_kernel, grid=(count // rows,), in_specs=[SMEM, SMEM,...  15.9 us
    pallas_call x2, Pallas kernels, residual_of(): pl.pallas_call(functools.partial(residual_kernel, peers, first, low, keep...  14.7 us
  transfers between devices with their start and end apart: 21, of which 5 were waited for; matrix products, arithmetic and copies ran while one was open for 0% of the time, Pallas kernels for 46%

profile of v6, /device:TPU:0, one launch (start us, length us, event | category | flops | bytes accessed | tf_op | source)
XLA Modules:
  0.0 152.0 jit_solution(7452371767549899187)
XLA Ops:
  0.6 0.1 pad_add_fusion.me_ref
  0.7 2.6 %packed.1 = (f32[24,256]{1,0:T(8,128)S(1)}, bf16[32,1408]{1,0:T(8,128)(2,1)S(1)}, bf16[32,1408]{1,0:T(8,128)(2,1)S(1)}, bf16[32,1408]{1,0:T(8,128)(2,1)S(1)}, bf...) custom-call(s32[2]{0:T(128)S(1)} %pad_add_fusion.me_ref, ...), custom_call_target="tpu_custom_call" | custom-call | bytes 8388608 | tf_op jit(solution)/shard_map/packed/pallas_call | solution.py:139
  3.3 3.1 %collective-permute-start.12 = (f32[24,256]{1,0:T(8,128)S(1)}, f32[24,256]{1,0:T(8,128)S(1)}, u32[]{:S(2)}, u32[]{:S(2)}) collective-permute-start(f32[24,256]{1,0:T(8,128)S(1)} %get-tuple-element.37), channel_id=1, source_target_pairs={{0,4},{4,8},{8,12},{12,0},{1,5},{5,9},{9,13},{13,1},{2,6},{6,10},{... | collective-permute-start | bytes 73736 | tf_op jit(solution)/shard_map/ppermute | solution.py:78
  6.4 2.6 %collective-permute-start.13 = (f32[24,256]{1,0:T(8,128)S(1)}, f32[24,256]{1,0:T(8,128)S(1)}, u32[]{:S(2)}, u32[]{:S(2)}) collective-permute-start(f32[24,256]{1,0:T(8,128)S(1)} %get-tuple-element.37), channel_id=1, source_target_pairs={{0,8},{4,12},{8,0},{12,4},{1,9},{5,13},{9,1},{13,5},{2,10},{6,14},... | collective-permute-start | bytes 73736 | tf_op jit(solution)/shard_map/ppermute | solution.py:78
  9.0 1.3 collective-permute-start.14
  10.4 0.7 collective-permute-start
  11.1 0.1 collective-permute-start.3
  11.1 0.8 collective-permute-start.6
  12.0 0.0 collective-permute-done.13
  12.0 3.5 %collective-permute-start.7 = (bf16[32,1408]{1,0:T(8,128)(2,1)S(1)}, bf16[32,1408]{1,0:T(8,128)(2,1)S(1)}, u32[]{:S(2)}, u32[]{:S(2)}) collective-permute-start(bf16[32,1408]{1,0:T(8,128)(2,1)S(1)} %get-tuple-element.29), channel_id=1, source_target_pairs={{0,8},{4,12},{8,0},{12,4},{1,9},{5,13},{9,1},{13,5},{2,10},{6,14},... | collective-permute-start | bytes 270344 | tf_op jit(solution)/shard_map/ppermute | solution.py:78
  15.5 0.0 collective-permute-done.14
  15.5 2.2 %collective-permute-start.8 = (bf16[32,1408]{1,0:T(8,128)(2,1)S(1)}, bf16[32,1408]{1,0:T(8,128)(2,1)S(1)}, u32[]{:S(2)}, u32[]{:S(2)}) collective-permute-start(bf16[32,1408]{1,0:T(8,128)(2,1)S(1)} %get-tuple-element.30), channel_id=1, source_target_pairs={{0,12},{4,0},{8,4},{12,8},{1,13},{5,1},{9,5},{13,9},{2,14},{6,2},{... | collective-permute-start | bytes 270344 | tf_op jit(solution)/shard_map/ppermute | solution.py:78
  17.7 12.5 %collective-permute-done.6.refs_0_ = bf16[32,1408]{1,0:T(8,128)(2,1)S(1)} collective-permute-done((bf16[32,1408]{1,0:T(8,128)(2,1)S(1)}, bf16[32,1408]{1,0:T(8,128)(2,1)S(1)}, u32[]{:S(2)}, u32[]{:S(2)}) %collective-permute-start.6) | collective-permute-done | bytes 90144 | tf_op jit(solution)/shard_map/ppermute | solution.py:78
  30.2 2.0 %collective-permute-done.7.refs_1_ = bf16[32,1408]{1,0:T(8,128)(2,1)S(1)} collective-permute-done((bf16[32,1408]{1,0:T(8,128)(2,1)S(1)}, bf16[32,1408]{1,0:T(8,128)(2,1)S(1)}, u32[]{:S(2)}, u32[]{:S(2)}) %collective-permute-start.7) | collective-permute-done | bytes 90144 | tf_op jit(solution)/shard_map/ppermute | solution.py:78
  32.2 1.5 collective-permute-start.16
  33.7 0.6 collective-permute-done.15.refs_1_
  34.2 2.9 %collective-permute-start.4 = (bf16[32,5120]{1,0:T(8,128)(2,1)S(1)}, bf16[32,5120]{1,0:T(8,128)(2,1)S(1)}, u32[]{:S(2)}, u32[]{:S(2)}) collective-permute-start(bf16[32,5120]{1,0:T(8,128)(2,1)S(1)} %get-tuple-element.26), channel_id=1, source_target_pairs={{0,8},{4,12},{8,0},{12,4},{1,9},{5,13},{9,1},{13,5},{2,10},{6,14},... | collective-permute-start | bytes 983048 | tf_op jit(solution)/shard_map/ppermute | solution.py:78
  37.1 2.0 %collective-permute-start.5 = (bf16[32,5120]{1,0:T(8,128)(2,1)S(1)}, bf16[32,5120]{1,0:T(8,128)(2,1)S(1)}, u32[]{:S(2)}, u32[]{:S(2)}) collective-permute-start(bf16[32,5120]{1,0:T(8,128)(2,1)S(1)} %get-tuple-element.27), channel_id=1, source_target_pairs={{0,12},{4,0},{8,4},{12,8},{1,13},{5,1},{9,5},{13,9},{2,14},{6,2},{... | collective-permute-start | bytes 983048 | tf_op jit(solution)/shard_map/ppermute | solution.py:78
  39.1 0.1 collective-permute-start.9
  39.2 1.2 collective-permute-start.10
  40.3 2.7 %collective-permute-start.11 = (bf16[32,6144]{1,0:T(8,128)(2,1)S(1)}, bf16[32,6144]{1,0:T(8,128)(2,1)S(1)}, u32[]{:S(2)}, u32[]{:S(2)}) collective-permute-start(bf16[32,6144]{1,0:T(8,128)(2,1)S(1)} %get-tuple-element.33), channel_id=1, source_target_pairs={{0,12},{4,0},{8,4},{12,8},{1,13},{5,1},{9,5},{13,9},{2,14},{6,2},{... | collective-permute-start | bytes 1179656 | tf_op jit(solution)/shard_map/ppermute | solution.py:78
  43.0 10.7 %collective-permute-done.4.refs_7_.refs_4_ = bf16[32,5120]{1,0:T(8,128)(2,1)S(1)} collective-permute-done((bf16[32,5120]{1,0:T(8,128)(2,1)S(1)}, bf16[32,5120]{1,0:T(8,128)(2,1)S(1)}, u32[]{:S(2)}, u32[]{:S(2)}) %collective-permute-start.4) | collective-permute-done | bytes 327712 | tf_op jit(solution)/shard_map/ppermute | solution.py:78
  53.7 9.0 %collective-permute-done.5.refs_8_.refs_5_ = bf16[32,5120]{1,0:T(8,128)(2,1)S(1)} collective-permute-done((bf16[32,5120]{1,0:T(8,128)(2,1)S(1)}, bf16[32,5120]{1,0:T(8,128)(2,1)S(1)}, u32[]{:S(2)}, u32[]{:S(2)}) %collective-permute-start.5) | collective-permute-done | bytes 327712 | tf_op jit(solution)/shard_map/ppermute | solution.py:78
  62.7 15.9 %banded.1.refs_10_.refs_7_ = bf16[64,256,512]{2,1,0:T(8,128)(2,1)S(1)} custom-call(s32[1]{0:T(128)S(6)} %mul.7.first_ref, s32[3,256]{1,0:T(4,128)S(1)} %bitcast.13, bf16[256,12288]{1,0:T(8,128)(2,1)} %values_ref.1), custom_call_target="tpu_custom_call" | custom-call | bytes 41943040 | tf_op jit(solution)/shard_map/banded/pallas_call | solution.py:396
  78.7 0.0 copy-start
  78.7 38.6 %site_sums.1 = (f32[32,1024]{1,0:T(8,128)S(1)}, s16[32,1152]{1,0:T(8,128)(2,1)S(1)}, s16[32,1152]{1,0:T(8,128)(2,1)S(1)}, s16[32,1152]{1,0:T(8,128)(2,1)S(1)}) custom-call(s32[2]{0:T(128)S(1)} %pad_add_fusion.me_ref, bf16[32,65536]{1,0:T(8,128)(2,1)} %bitcast.15, f32[96,256]{1,0:T(8,128)S(1)} %constant_dynamic-update-slice_fusion.refs_0_, ...), custom_call_target="tpu_custom_call" | custom-call | flops 67108864 | bytes 67108864 | tf_op jit(solution)/shard_map/site_sums/pallas_call | solution.py:282
  117.3 14.1 %collective-permute-start.18 = (s16[32,1152]{1,0:T(8,128)(2,1)S(1)}, s16[32,1152]{1,0:T(8,128)(2,1)S(1)}, u32[]{:S(2)}, u32[]{:S(2)}) collective-permute-start(s16[32,1152]{1,0:T(8,128)(2,1)S(1)} %get-tuple-element.39), channel_id=1, source_target_pairs={{0,4},{4,8},{8,12},{12,0},{1,5},{5,9},{9,13},{13,1},{2,6},{6,10},{... | collective-permute-start | bytes 221192 | tf_op jit(solution)/shard_map/ppermute | solution.py:78
  131.4 1.5 %collective-permute-start.19 = (s16[32,1152]{1,0:T(8,128)(2,1)S(1)}, s16[32,1152]{1,0:T(8,128)(2,1)S(1)}, u32[]{:S(2)}, u32[]{:S(2)}) collective-permute-start(s16[32,1152]{1,0:T(8,128)(2,1)S(1)} %get-tuple-element.40), channel_id=1, source_target_pairs={{0,8},{4,12},{8,0},{12,4},{1,9},{5,13},{9,1},{13,5},{2,10},{6,14},... | collective-permute-start | bytes 221192 | tf_op jit(solution)/shard_map/ppermute | solution.py:78
  132.9 2.8 %collective-permute-start.20 = (s16[32,1152]{1,0:T(8,128)(2,1)S(1)}, s16[32,1152]{1,0:T(8,128)(2,1)S(1)}, u32[]{:S(2)}, u32[]{:S(2)}) collective-permute-start(s16[32,1152]{1,0:T(8,128)(2,1)S(1)} %get-tuple-element.41), channel_id=1, source_target_pairs={{0,12},{4,0},{8,4},{12,8},{1,13},{5,1},{9,5},{13,9},{2,14},{6,2},{... | collective-permute-start | bytes 221192 | tf_op jit(solution)/shard_map/ppermute | solution.py:78
  135.8 10.0 %shard_map.95 = (bf16[128,16384]{1,0:T(8,128)(2,1)}, f32[8,128]{1,0:T(8,128)}) custom-call(s32[2]{0:T(128)S(1)} %pad_add_fusion.me_ref, bf16[32,1408]{1,0:T(8,128)(2,1)S(1)} %collective-permute-done.6.refs_0_, bf16[32,1408]{1,0:T(8,128)(2,1)S(1)} %collective-permute-done.7.refs_1_, bf16[32,1408]{1,0:T(8,128)(2,1)S(1)} %collective-permute-done.8.refs_2_, ...), custom_call_target="tpu_custom_call" | custom-call | flops 1207959552 | bytes 16515072 | tf_op jit(solution)/shard_map/pallas_call | solution.py:490
  145.8 4.7 %shard_map.96 = (bf16[128,16384]{1,0:T(8,128)(2,1)}, f32[8,128]{1,0:T(8,128)S(1)}) custom-call(s32[2]{0:T(128)S(1)} %pad_add_fusion.me_ref, bf16[32,3968]{1,0:T(8,128)(2,1)S(1)} %collective-permute-done.refs_0_, bf16[32,3968]{1,0:T(8,128)(2,1)S(1)} %collective-permute-done.1.refs_1_, ...), custom_call_target="tpu_custom_call", output_to_operand_aliasing={{0}: (10, {})} | custom-call | flops 402653184 | bytes 5505024 | tf_op jit(solution)/shard_map/pallas_call | solution.py:490
  150.5 1.4 placed_rows.1
  (25 shorter events, 0.1 us)
Async XLA Ops:
  0.6 62.1 %copy-start.1 = (s32[256,3]{0,1:T(4,128)S(1)}, s32[256,3]{0,1:T(4,128)}, u32[]{:S(2)}) copy-start(s32[256,3]{0,1:T(4,128)} %param.10) | copy-start | bytes 9220
  3.3 7.8 %collective-permute-start.12 = (f32[24,256]{1,0:T(8,128)S(1)}, f32[24,256]{1,0:T(8,128)S(1)}, u32[]{:S(2)}, u32[]{:S(2)}) collective-permute-start(f32[24,256]{1,0:T(8,128)S(1)} %get-tuple-element.37), channel_id=1, source_target_pairs={{0,4},{4,8},{8,12},{12,0},{1,5},{5,9},{9,13},{13,1},{2,6},{6,10},{... | collective-permute-start | bytes 73736 | tf_op jit(solution)/shard_map/ppermute | solution.py:78
  6.4 5.5 %collective-permute-start.13 = (f32[24,256]{1,0:T(8,128)S(1)}, f32[24,256]{1,0:T(8,128)S(1)}, u32[]{:S(2)}, u32[]{:S(2)}) collective-permute-start(f32[24,256]{1,0:T(8,128)S(1)} %get-tuple-element.37), channel_id=1, source_target_pairs={{0,8},{4,12},{8,0},{12,4},{1,9},{5,13},{9,1},{13,5},{2,10},{6,14},... | collective-permute-start | bytes 73736 | tf_op jit(solution)/shard_map/ppermute | solution.py:78
  9.0 6.4 %collective-permute-start.14 = (f32[24,256]{1,0:T(8,128)S(1)}, f32[24,256]{1,0:T(8,128)S(1)}, u32[]{:S(2)}, u32[]{:S(2)}) collective-permute-start(f32[24,256]{1,0:T(8,128)S(1)} %get-tuple-element.37), channel_id=1, source_target_pairs={{0,12},{4,0},{8,4},{12,8},{1,13},{5,1},{9,5},{13,9},{2,14},{6,2},{... | collective-permute-start | bytes 73736 | tf_op jit(solution)/shard_map/ppermute | solution.py:78
  10.4 28.8 %collective-permute-start = (bf16[32,3968]{1,0:T(8,128)(2,1)S(1)}, bf16[32,3968]{1,0:T(8,128)(2,1)S(1)}, u32[]{:S(2)}, u32[]{:S(2)}) collective-permute-start(bf16[32,3968]{1,0:T(8,128)(2,1)S(1)} %get-tuple-element.22), channel_id=1, source_target_pairs={{0,4},{4,8},{8,12},{12,0},{1,5},{5,9},{9,13},{13,1},{2,6},{6,10},{... | collective-permute-start | bytes 761864 | tf_op jit(solution)/shard_map/ppermute | solution.py:78
  11.1 29.3 %collective-permute-start.3 = (bf16[32,5120]{1,0:T(8,128)(2,1)S(1)}, bf16[32,5120]{1,0:T(8,128)(2,1)S(1)}, u32[]{:S(2)}, u32[]{:S(2)}) collective-permute-start(bf16[32,5120]{1,0:T(8,128)(2,1)S(1)} %get-tuple-element.25), channel_id=1, source_target_pairs={{0,4},{4,8},{8,12},{12,0},{1,5},{5,9},{9,13},{13,1},{2,6},{6,10},{... | collective-permute-start | bytes 983048 | tf_op jit(solution)/shard_map/ppermute | solution.py:78
  11.1 19.0 %collective-permute-start.6 = (bf16[32,1408]{1,0:T(8,128)(2,1)S(1)}, bf16[32,1408]{1,0:T(8,128)(2,1)S(1)}, u32[]{:S(2)}, u32[]{:S(2)}) collective-permute-start(bf16[32,1408]{1,0:T(8,128)(2,1)S(1)} %get-tuple-element.28), channel_id=1, source_target_pairs={{0,4},{4,8},{8,12},{12,0},{1,5},{5,9},{9,13},{13,1},{2,6},{6,10},{... | collective-permute-start | bytes 270344 | tf_op jit(solution)/shard_map/ppermute | solution.py:78
  12.0 20.2 %collective-permute-start.7 = (bf16[32,1408]{1,0:T(8,128)(2,1)S(1)}, bf16[32,1408]{1,0:T(8,128)(2,1)S(1)}, u32[]{:S(2)}, u32[]{:S(2)}) collective-permute-start(bf16[32,1408]{1,0:T(8,128)(2,1)S(1)} %get-tuple-element.29), channel_id=1, source_target_pairs={{0,8},{4,12},{8,0},{12,4},{1,9},{5,13},{9,1},{13,5},{2,10},{6,14},... | collective-permute-start | bytes 270344 | tf_op jit(solution)/shard_map/ppermute | solution.py:78
  15.5 18.2 %collective-permute-start.8 = (bf16[32,1408]{1,0:T(8,128)(2,1)S(1)}, bf16[32,1408]{1,0:T(8,128)(2,1)S(1)}, u32[]{:S(2)}, u32[]{:S(2)}) collective-permute-start(bf16[32,1408]{1,0:T(8,128)(2,1)S(1)} %get-tuple-element.30), channel_id=1, source_target_pairs={{0,12},{4,0},{8,4},{12,8},{1,13},{5,1},{9,5},{13,9},{2,14},{6,2},{... | collective-permute-start | bytes 270344 | tf_op jit(solution)/shard_map/ppermute | solution.py:78
  30.2 4.0 %collective-permute-start.15 = (f32[96,256]{1,0:T(8,128)S(1)}, f32[96,256]{1,0:T(8,128)S(1)}, u32[]{:S(2)}, u32[]{:S(2)}) collective-permute-start(f32[96,256]{1,0:T(8,128)S(1)} %constant_dynamic-update-slice_fusion.refs_0_), channel_id=1, source_target_pairs={{0,1},{1,2},{2,3},{3,0},{4,5},{5,6},{6,7},{7,4},{8,9},{9,10},{10,1... | collective-permute-start | bytes 294920 | tf_op jit(solution)/shard_map/ppermute | solution.py:551
  32.2 5.0 %collective-permute-start.16 = (f32[96,256]{1,0:T(8,128)S(1)}, f32[96,256]{1,0:T(8,128)S(1)}, u32[]{:S(2)}, u32[]{:S(2)}) collective-permute-start(f32[96,256]{1,0:T(8,128)S(1)} %constant_dynamic-update-slice_fusion.refs_0_), channel_id=1, source_target_pairs={{0,2},{1,3},{2,0},{3,1},{4,6},{5,7},{6,4},{7,5},{8,10},{9,11},{10,... | collective-permute-start | bytes 294920 | tf_op jit(solution)/shard_map/ppermute | solution.py:551
  33.7 5.4 %collective-permute-start.17 = (f32[96,256]{1,0:T(8,128)S(1)}, f32[96,256]{1,0:T(8,128)S(1)}, u32[]{:S(2)}, u32[]{:S(2)}) collective-permute-start(f32[96,256]{1,0:T(8,128)S(1)} %constant_dynamic-update-slice_fusion.refs_0_), channel_id=1, source_target_pairs={{0,3},{1,0},{2,1},{3,2},{4,7},{5,4},{6,5},{7,6},{8,11},{9,8},{10,9... | collective-permute-start | bytes 294920 | tf_op jit(solution)/shard_map/ppermute | solution.py:551
  34.2 19.5 %collective-permute-start.4 = (bf16[32,5120]{1,0:T(8,128)(2,1)S(1)}, bf16[32,5120]{1,0:T(8,128)(2,1)S(1)}, u32[]{:S(2)}, u32[]{:S(2)}) collective-permute-start(bf16[32,5120]{1,0:T(8,128)(2,1)S(1)} %get-tuple-element.26), channel_id=1, source_target_pairs={{0,8},{4,12},{8,0},{12,4},{1,9},{5,13},{9,1},{13,5},{2,10},{6,14},... | collective-permute-start | bytes 983048 | tf_op jit(solution)/shard_map/ppermute | solution.py:78
  37.1 25.6 %collective-permute-start.5 = (bf16[32,5120]{1,0:T(8,128)(2,1)S(1)}, bf16[32,5120]{1,0:T(8,128)(2,1)S(1)}, u32[]{:S(2)}, u32[]{:S(2)}) collective-permute-start(bf16[32,5120]{1,0:T(8,128)(2,1)S(1)} %get-tuple-element.27), channel_id=1, source_target_pairs={{0,12},{4,0},{8,4},{12,8},{1,13},{5,1},{9,5},{13,9},{2,14},{6,2},{... | collective-permute-start | bytes 983048 | tf_op jit(solution)/shard_map/ppermute | solution.py:78
  39.1 78.2 %collective-permute-start.9 = (bf16[32,6144]{1,0:T(8,128)(2,1)S(1)}, bf16[32,6144]{1,0:T(8,128)(2,1)S(1)}, u32[]{:S(2)}, u32[]{:S(2)}) collective-permute-start(bf16[32,6144]{1,0:T(8,128)(2,1)S(1)} %get-tuple-element.31), channel_id=1, source_target_pairs={{0,4},{4,8},{8,12},{12,0},{1,5},{5,9},{9,13},{13,1},{2,6},{6,10},{... | collective-permute-start | bytes 1179656 | tf_op jit(solution)/shard_map/ppermute | solution.py:78
  39.2 92.2 %collective-permute-start.10 = (bf16[32,6144]{1,0:T(8,128)(2,1)S(1)}, bf16[32,6144]{1,0:T(8,128)(2,1)S(1)}, u32[]{:S(2)}, u32[]{:S(2)}) collective-permute-start(bf16[32,6144]{1,0:T(8,128)(2,1)S(1)} %get-tuple-element.32), channel_id=1, source_target_pairs={{0,8},{4,12},{8,0},{12,4},{1,9},{5,13},{9,1},{13,5},{2,10},{6,14},... | collective-permute-start | bytes 1179656 | tf_op jit(solution)/shard_map/ppermute | solution.py:78
  40.3 92.6 %collective-permute-start.11 = (bf16[32,6144]{1,0:T(8,128)(2,1)S(1)}, bf16[32,6144]{1,0:T(8,128)(2,1)S(1)}, u32[]{:S(2)}, u32[]{:S(2)}) collective-permute-start(bf16[32,6144]{1,0:T(8,128)(2,1)S(1)} %get-tuple-element.33), channel_id=1, source_target_pairs={{0,12},{4,0},{8,4},{12,8},{1,13},{5,1},{9,5},{13,9},{2,14},{6,2},{... | collective-permute-start | bytes 1179656 | tf_op jit(solution)/shard_map/ppermute | solution.py:78
  53.7 92.0 %collective-permute-start.1 = (bf16[32,3968]{1,0:T(8,128)(2,1)S(1)}, bf16[32,3968]{1,0:T(8,128)(2,1)S(1)}, u32[]{:S(2)}, u32[]{:S(2)}) collective-permute-start(bf16[32,3968]{1,0:T(8,128)(2,1)S(1)} %get-tuple-element.23), channel_id=1, source_target_pairs={{0,8},{4,12},{8,0},{12,4},{1,9},{5,13},{9,1},{13,5},{2,10},{6,14},... | collective-permute-start | bytes 761864 | tf_op jit(solution)/shard_map/ppermute | solution.py:78
  62.7 83.1 %collective-permute-start.2 = (bf16[32,3968]{1,0:T(8,128)(2,1)S(1)}, bf16[32,3968]{1,0:T(8,128)(2,1)S(1)}, u32[]{:S(2)}, u32[]{:S(2)}) collective-permute-start(bf16[32,3968]{1,0:T(8,128)(2,1)S(1)} %get-tuple-element.24), channel_id=1, source_target_pairs={{0,12},{4,0},{8,4},{12,8},{1,13},{5,1},{9,5},{13,9},{2,14},{6,2},{... | collective-permute-start | bytes 761864 | tf_op jit(solution)/shard_map/ppermute | solution.py:78
  78.7 57.1 %copy-start = (f32[16384]{0:T(1024)S(1)}, f32[16384]{0:T(1024)}, u32[]{:S(2)}) copy-start(f32[16384]{0:T(1024)} %param.11) | copy-start | bytes 196612
  117.3 33.2 %collective-permute-start.18 = (s16[32,1152]{1,0:T(8,128)(2,1)S(1)}, s16[32,1152]{1,0:T(8,128)(2,1)S(1)}, u32[]{:S(2)}, u32[]{:S(2)}) collective-permute-start(s16[32,1152]{1,0:T(8,128)(2,1)S(1)} %get-tuple-element.39), channel_id=1, source_target_pairs={{0,4},{4,8},{8,12},{12,0},{1,5},{5,9},{9,13},{13,1},{2,6},{6,10},{... | collective-permute-start | bytes 221192 | tf_op jit(solution)/shard_map/ppermute | solution.py:78
  131.4 19.1 %collective-permute-start.19 = (s16[32,1152]{1,0:T(8,128)(2,1)S(1)}, s16[32,1152]{1,0:T(8,128)(2,1)S(1)}, u32[]{:S(2)}, u32[]{:S(2)}) collective-permute-start(s16[32,1152]{1,0:T(8,128)(2,1)S(1)} %get-tuple-element.40), channel_id=1, source_target_pairs={{0,8},{4,12},{8,0},{12,4},{1,9},{5,13},{9,1},{13,5},{2,10},{6,14},... | collective-permute-start | bytes 221192 | tf_op jit(solution)/shard_map/ppermute | solution.py:78
  132.9 17.6 %collective-permute-start.20 = (s16[32,1152]{1,0:T(8,128)(2,1)S(1)}, s16[32,1152]{1,0:T(8,128)(2,1)S(1)}, u32[]{:S(2)}, u32[]{:S(2)}) collective-permute-start(s16[32,1152]{1,0:T(8,128)(2,1)S(1)} %get-tuple-element.41), channel_id=1, source_target_pairs={{0,12},{4,0},{8,4},{12,8},{1,13},{5,1},{9,5},{13,9},{2,14},{6,2},{... | collective-permute-start | bytes 221192 | tf_op jit(solution)/shard_map/ppermute | solution.py:78
